TPU v7x, 256 devices: a whole 4x4x8 slice. The times are simulated.
256 devices in a mesh: ctx: 32 (over x, z), tp: 8 (over y, core).
Axes of the slice: x: 4, y: 4, z: 8, core: 2. Of those that a mesh axis runs over, the one named last changes fastest.
Arguments:
- tokens: bfloat16 [16384, 4096], P('ctx', 'tp'), may hold values from -16 to 16
- query_weight: bfloat16 [4096, 4096], P(None, 'tp'), may hold values from -0.09375 to 0.09375
- key_weight: bfloat16 [4096, 1024], P(None, 'tp'), may hold values from -0.09375 to 0.09375
- value_weight: bfloat16 [4096, 1024], P(None, 'tp'), may hold values from -0.09375 to 0.09375
- out_weight: bfloat16 [4096, 4096], P('tp'), may hold values from -0.09375 to 0.09375
- links: int32 [128, 16], P('ctx'), may hold values from 0 to 127, as said below
- counts: int32 [128], P('ctx'), may hold values from 1 to 16, as said below
- doc_ids: int32 [128], replicated, may hold values from 0 to 31, never falling along the last dimension, each value on 1 to 8 neighbouring positions
Outputs:
- mixed: bfloat16 [16384, 4096], P(('ctx', 'tp'))
Inputs may be any that keep to these rules, and one draw needn't show every extreme that they name: `links`: the first entry of each row is the query block itself; the entries of a row are distinct; every listed block lies within 4 ctx indices of its query block (block index // 4), and some query block of every ctx index lists a block exactly 4 indices away. `counts`: the first query block of each ctx index has 2 or more live slots, and block 0 has 16.
All inputs are finite; a program needn't handle non-finite values.
Results may differ from a plain program's by a relative error of at most 0.017.
Values may be sent and summed in bfloat16 or wider, within the bound.
No kernel may reach another device: no remote copies, remote signals or barrier semaphores. Data moves between devices by JAX's collectives and lax.ppermute only.
A program may use at most 64 MiB of HBM per device.

v0:
```python
import jax
import jax.numpy as jnp
from jax import lax
from jax.sharding import PartitionSpec as P

HEAD_DIM = 128
BLOCK = 128
LINKS = 16
REACH = 4


def from_behind(block, axis, distance):
    devices = range(lax.axis_size(axis))
    route = [(i - distance, i) for i in devices if i - distance in devices]
    return lax.ppermute(block, axis, route)


def local(tokens, query_weight, key_weight, value_weight, out_weight, links, counts, doc_ids):
    row_count = tokens.shape[0]
    query_width = query_weight.shape[1]
    key_width = key_weight.shape[1]
    piece = lax.all_gather(tokens, "tp", axis=1, tiled=True)
    weights = (query_weight, key_weight, value_weight)
    query, keys, values = tuple(
        (jnp.dot(piece, weight, preferred_element_type=jnp.float32) for weight in weights)
    )
    query = query.astype(jnp.bfloat16)
    block_count = row_count // BLOCK
    stacked = (
        jnp.stack([keys, values]).astype(jnp.bfloat16).reshape(2, block_count, BLOCK, key_width)
    )
    position = lax.axis_index("ctx")
    first_block = position * block_count
    pieces = []
    for offset in range(-REACH, REACH + 1):
        if offset == 0:
            pieces.append(stacked)
        else:
            pieces.append(from_behind(stacked, "ctx", -offset))
    source = jnp.concatenate(pieces, axis=1)
    anchor = (position - REACH) * block_count
    chosen = jnp.take(source, links - anchor, axis=1, mode="clip")
    kv_local = key_width // HEAD_DIM
    group = query_width // key_width
    chosen_keys = chosen[0].reshape(block_count, LINKS, BLOCK, kv_local, HEAD_DIM)
    chosen_values = chosen[1].reshape(block_count, LINKS, BLOCK, kv_local, HEAD_DIM)
    query_blocks = query.reshape(block_count, BLOCK, kv_local, group, HEAD_DIM)
    block_total = doc_ids.shape[0]
    table = jnp.arange(block_total, dtype=jnp.int32)
    query_index = first_block + jnp.arange(block_count, dtype=jnp.int32)[:, None]
    doc_key = jnp.sum(jnp.where(links[:, :, None] == table, doc_ids, 0), axis=-1)
    doc_query = jnp.sum(jnp.where(query_index == table[None, :], doc_ids[None, :], 0), axis=-1)[
        :, None
    ]
    live = jnp.arange(LINKS, dtype=jnp.int32)[None, :] < counts[:, None]
    earlier = (links < query_index) | (doc_key != doc_query)
    same = links == query_index
    causal = jnp.arange(BLOCK)[None, :] <= jnp.arange(BLOCK)[:, None]
    allowed = live[:, None, :, None] & (
        earlier[:, None, :, None] | same[:, None, :, None] & causal[None, :, None, :]
    )
    allowed = allowed[:, None, None]
    scores = jnp.einsum(
        "bqhgd,bskhd->bhgqsk", query_blocks, chosen_keys, preferred_element_type=jnp.float32
    ) * HEAD_DIM ** (-0.5)
    scores = jnp.where(allowed, scores, -1e30)
    top = jnp.max(scores, axis=(4, 5), keepdims=True)
    powers = jnp.where(allowed, jnp.exp(scores - top), 0.0)
    total = jnp.sum(powers, axis=(4, 5), keepdims=True)
    weights = (powers / total).astype(jnp.bfloat16)
    attended = jnp.einsum(
        "bhgqsk,bskhd->bqhgd", weights, chosen_values, preferred_element_type=jnp.float32
    )
    attended = attended.astype(jnp.bfloat16).reshape(row_count, query_width)
    return lax.psum_scatter(
        jnp.dot(attended, out_weight, preferred_element_type=jnp.float32).astype(jnp.bfloat16),
        "tp",
        scatter_dimension=0,
        tiled=True,
    )


def solution(mesh):
    placed = (
        P("ctx", "tp"),
        P(None, "tp"),
        P(None, "tp"),
        P(None, "tp"),
        P("tp", None),
        P("ctx", None),
        P("ctx"),
        P(),
    )
    return jax.shard_map(
        local, mesh=mesh, in_specs=placed, out_specs=P(("ctx", "tp"), None), check_vma=False
    )
```

profile of v0, /device:TPU:6, one launch (start us, length us, event | category | flops | bytes accessed | tf_op | source)
XLA Modules:
  0.0 212.3 jit_solution(15246871406914219502)
XLA Ops:
  6.5 0.7 all-gather.2.cloned.1.call-update
  7.3 0.0 reduce-scatter.2.cloned.1.call-start
  7.3 0.7 broadcast_subtract_fusion
  8.0 0.1 reshape.95
  8.1 0.8 select_reduce_fusion.1
  9.0 0.9 select_reduce_fusion
  9.9 0.7 iota_compare_fusion.3
  10.6 0.8 compare_or_fusion
  11.4 3.7 %or_and_fusion = pred[4,128,16,128]{1,3,2,0:T(8,128)(4,1)} fusion(pred[128,128]{0,1:T(8,128)(4,1)S(1)} %iota_compare_fusion, pred[4,16]{1,0:T(4,128)(4,1)S(1)} %get-tuple-element.6, pred[4,16]{1,0:T(4,128)(4,1)S(1)} %get-tuple-element.5, pred[4,16]{1,0:T(4,128)(4,1)S(1)} %iota_compare_fusion.3), kind=kLoop, calls=%fused_computation.9 | loop fusion | flops 3145728 | bytes 1065152 | tf_op jit(solution)/shard_map/and | solution.py:59
  15.0 31.7 %all-gather.2.cloned.1.call-done = bf16[512,4096]{1,0:T(8,128)(2,1)} async-done(((bf16[512,512]{1,0:T(8,128)(2,1)}), bf16[512,4096]{1,0:T(8,128)(2,1)}) %all-gather.2.cloned.1.call-update) | async-done | bytes 4194320 | tf_op jit(solution)/shard_map/all_gather | solution.py:22
  46.7 3.6 %convolution_convert_fusion.2 = bf16[512,128]{1,0:T(8,128)(2,1)S(1)} fusion(bf16[512,4096]{1,0:T(8,128)(2,1)} %all-gather.2.cloned.1.call-done, bf16[4096,128]{1,0:T(8,128)(2,1)S(1)} %copy-done), kind=kOutput, calls=%fused_computation.17 | convolution fusion | flops 536936448 | bytes 5373952 | tf_op jit(solution)/shard_map/dot_general | solution.py:25
  50.3 0.0 copy-start.6
  50.4 1.3 convolution_convert_fusion.3
  51.6 0.7 pad_maximum_fusion
  52.4 7.9 %collective-permute-start.7 = (bf16[2,4,128,128]{3,2,1,0:T(8,128)(2,1)}, bf16[2,4,128,128]{3,2,1,0:T(8,128)(2,1)}, u32[]{:S(2)}, u32[]{:S(2)}) collective-permute-start(bf16[2,4,128,128]{3,2,1,0:T(8,128)(2,1)} %pad_maximum_fusion), channel_id=1, source_target_pairs={{32,0},{40,8},{48,16},{56,24},{64,32},{72,40},{80,48},{88,56},{96,... | collective-permute-start | bytes 786440 | tf_op jit(solution)/shard_map/ppermute | solution.py:15
  60.3 2.2 %collective-permute-start.6 = (bf16[2,4,128,128]{3,2,1,0:T(8,128)(2,1)}, bf16[2,4,128,128]{3,2,1,0:T(8,128)(2,1)}, u32[]{:S(2)}, u32[]{:S(2)}) collective-permute-start(bf16[2,4,128,128]{3,2,1,0:T(8,128)(2,1)} %pad_maximum_fusion), channel_id=1, source_target_pairs={{24,0},{32,8},{40,16},{48,24},{56,32},{64,40},{72,48},{80,56},{88,... | collective-permute-start | bytes 786440 | tf_op jit(solution)/shard_map/ppermute | solution.py:15
  62.5 4.5 %collective-permute-start.2 = (bf16[2,4,128,128]{3,2,1,0:T(8,128)(2,1)}, bf16[2,4,128,128]{3,2,1,0:T(8,128)(2,1)}, u32[]{:S(2)}, u32[]{:S(2)}) collective-permute-start(bf16[2,4,128,128]{3,2,1,0:T(8,128)(2,1)} %pad_maximum_fusion), channel_id=1, source_target_pairs={{0,16},{8,24},{16,32},{24,40},{32,48},{40,56},{48,64},{56,72},{64,... | collective-permute-start | bytes 786440 | tf_op jit(solution)/shard_map/ppermute | solution.py:15
  67.0 5.5 %collective-permute-start.1 = (bf16[2,4,128,128]{3,2,1,0:T(8,128)(2,1)}, bf16[2,4,128,128]{3,2,1,0:T(8,128)(2,1)}, u32[]{:S(2)}, u32[]{:S(2)}) collective-permute-start(bf16[2,4,128,128]{3,2,1,0:T(8,128)(2,1)} %pad_maximum_fusion), channel_id=1, source_target_pairs={{0,24},{8,32},{16,40},{24,48},{32,56},{40,64},{48,72},{56,80},{64,... | collective-permute-start | bytes 786440 | tf_op jit(solution)/shard_map/ppermute | solution.py:15
  72.5 2.0 collective-permute-start
  74.6 2.3 %convolution_convert_fusion.1 = bf16[512,512]{1,0:T(8,128)(2,1)S(1)} fusion(bf16[512,4096]{1,0:T(8,128)(2,1)S(1)} %copy-done.7, bf16[4096,512]{1,0:T(8,128)(2,1)S(1)} %copy-done.6), kind=kOutput, calls=%fused_computation.14 | convolution fusion | flops 2147745792 | bytes 8912896 | tf_op jit(solution)/shard_map/dot_general | solution.py:25
  76.9 0.9 reshape.90
  77.8 32.8 %collective-permute-done = bf16[2,4,128,128]{3,2,1,0:T(8,128)(2,1)S(1)} collective-permute-done((bf16[2,4,128,128]{3,2,1,0:T(8,128)(2,1)}, bf16[2,4,128,128]{3,2,1,0:T(8,128)(2,1)S(1)}, u32[]{:S(2)}, u32[]{:S(2)}) %collective-permute-start) | collective-permute-done | bytes 262176 | tf_op jit(solution)/shard_map/ppermute | solution.py:15
  110.6 0.7 copy-done.5
  111.4 1.9 collective-permute-start.3
  113.3 1.0 constant_dynamic-update-slice_fusion.8
  114.2 0.0 collective-permute-done.1
  114.2 7.4 %collective-permute-start.5 = (bf16[2,4,128,128]{3,2,1,0:T(8,128)(2,1)}, bf16[2,4,128,128]{3,2,1,0:T(8,128)(2,1)S(1)}, u32[]{:S(2)}, u32[]{:S(2)}) collective-permute-start(bf16[2,4,128,128]{3,2,1,0:T(8,128)(2,1)} %pad_maximum_fusion), channel_id=1, source_target_pairs={{16,0},{24,8},{32,16},{40,24},{48,32},{56,40},{64,48},{72,56},{80,... | collective-permute-start | bytes 786440 | tf_op jit(solution)/shard_map/ppermute | solution.py:15
  121.7 1.0 constant_dynamic-update-slice_fusion.7
  122.7 0.0 collective-permute-done.2
  122.7 4.1 %collective-permute-start.4 = (bf16[2,4,128,128]{3,2,1,0:T(8,128)(2,1)}, bf16[2,4,128,128]{3,2,1,0:T(8,128)(2,1)S(1)}, u32[]{:S(2)}, u32[]{:S(2)}) collective-permute-start(bf16[2,4,128,128]{3,2,1,0:T(8,128)(2,1)} %pad_maximum_fusion), channel_id=1, source_target_pairs={{8,0},{16,8},{24,16},{32,24},{40,32},{48,40},{56,48},{64,56},{72,6... | collective-permute-start | bytes 786440 | tf_op jit(solution)/shard_map/ppermute | solution.py:15
  126.8 1.0 constant_dynamic-update-slice_fusion.6
  127.8 0.0 collective-permute-done.3
  127.9 0.9 constant_dynamic-update-slice_fusion.4
  128.8 9.5 %collective-permute-done.4 = bf16[2,4,128,128]{3,2,1,0:T(8,128)(2,1)S(1)} collective-permute-done((bf16[2,4,128,128]{3,2,1,0:T(8,128)(2,1)}, bf16[2,4,128,128]{3,2,1,0:T(8,128)(2,1)S(1)}, u32[]{:S(2)}, u32[]{:S(2)}) %collective-permute-start.4) | collective-permute-done | bytes 262176 | tf_op jit(solution)/shard_map/ppermute | solution.py:15
  138.4 0.0 collective-permute-done.5
  138.4 0.0 collective-permute-done.6
  138.4 1.0 constant_dynamic-update-slice_fusion.1
  139.4 0.0 collective-permute-done.7
  139.4 1.0 constant_dynamic-update-slice_fusion
  140.4 3.0 %gather_fusion = bf16[64,2,128,128]{3,2,1,0:T(8,128)(2,1)} fusion(bf16[2,36,128,128]{3,2,1,0:T(8,128)(2,1)S(1)} %constant_dynamic-update-slice_fusion, s32[1024]{0:T(1024)S(1)} %pad_clamp_fusion), kind=kCustom, calls=%fused_computation | custom fusion | bytes 8388864 | tf_op jit(solution)/shard_map/jit(_take)/gather | solution.py:42
  143.5 2.9 %copy.18 = bf16[64,2,128,128]{3,2,0,1:T(8,128)(2,1)S(1)} copy(bf16[64,2,128,128]{3,2,1,0:T(8,128)(2,1)} %gather_fusion) | data formatting | bytes 8388608 | tf_op jit(solution)/shard_map/jit(_take)/gather | solution.py:42
  146.4 2.6 %fusion = (f32[4,4,128]{2,1,0:T(4,128)S(1)}, f32[4,16,128,128,4]{3,2,4,1,0:T(8,128)S(1)}) fusion(pred[4,128,16,128]{1,3,2,0:T(8,128)(4,1)S(1)} %copy-done.1, bf16[4,128,4,128,1]{3,2,1,0,4:T(4,128)(2,1)S(1)} %bitcast.87, bf16[2,4,16,128,128]{4,3,2,1,0:T(8,128)(2,1)S(1)} %bitcast.85), kind=kOutput, calls=%fused_computation.4 | convolution fusion | flops 1086322688 | bytes 20455424 | tf_op jit(solution)/shard_map/bqhgd,bskhd->bhgqsk/dot_general | solution.py:63
  149.0 4.3 %fusion.1 = f32[4,4,128]{2,1,0:T(4,128)S(1)} fusion(f32[4,16,128,128,4]{3,2,4,1,0:T(8,128)S(1)} %get-tuple-element.8, f32[4,4,128]{2,1,0:T(4,128)S(1)} %get-tuple-element.7, pred[4,128,16,128]{1,3,2,0:T(8,128)(4,1)S(1)} %copy-done.1), kind=kLoop, calls=%fused_computation.5 | loop fusion | flops 20969472 | bytes 17842176 | tf_op jit(solution)/shard_map/reduce_sum | solution.py:69
  153.2 6.3 %fusion.11 = bf16[4,128,1,4,128]{1,4,3,0,2:T(8,128)(2,1)S(1)} fusion(f32[4,4,128]{2,1,0:T(4,128)S(1)} %fusion.1, f32[4,4,128]{2,1,0:T(4,128)S(1)} %get-tuple-element.7, f32[4,16,128,128,4]{3,2,4,1,0:T(8,128)S(1)} %get-tuple-element.8, pred[4,128,16,128]{1,3,2,0:T(8,128)(4,1)S(1)} %copy-done.1, bf16[2,4,16,128,128]{4,3,2,1,0:T(8,128)(2,1)} %bitcast.86), kind=kOutput, calls=%fused_computation.16 | convolution fusion | flops 1099169792 | bytes 20463616 | tf_op jit(solution)/shard_map/bhgqsk,bskhd->bqhgd/dot_general | solution.py:71
  159.5 0.3 copy.22
  159.8 6.5 %convolution_convert_fusion = bf16[512,4096]{1,0:T(8,128)(2,1)} fusion(bf16[512,4096]{1,0:T(8,128)(2,1)} %param.12, bf16[64,8,4,128]{3,2,1,0:T(4,128)(2,1)S(1)} %bitcast.88), kind=kOutput, calls=%fused_computation.8 | convolution fusion | flops 2149580800 | bytes 8912896 | tf_op jit(solution)/shard_map/dot_general | solution.py:76
  166.3 0.0 reduce-scatter.2.cloned.1.call-update
  166.3 39.1 %reduce-scatter.2.cloned.1.call-done = bf16[64,4096]{1,0:T(8,128)(2,1)} async-done(((bf16[512,4096]{1,0:T(8,128)(2,1)}), bf16[64,4096]{1,0:T(8,128)(2,1)}) %reduce-scatter.2.cloned.1.call-update) | async-done | bytes 524304 | tf_op jit(solution)/shard_map/reduce_scatter | solution.py:75
  (23 shorter events, 0.2 us)
Async XLA Ops:
  6.5 40.2 %copy-start = (bf16[4096,128]{1,0:T(8,128)(2,1)S(1)}, bf16[4096,128]{1,0:T(8,128)(2,1)}, u32[]{:S(2)}) copy-start(bf16[4096,128]{1,0:T(8,128)(2,1)} %param.11) | copy-start | bytes 3145732
  6.5 43.8 %copy-start.8 = (bf16[4096,128]{1,0:T(8,128)(2,1)S(1)}, bf16[4096,128]{1,0:T(8,128)(2,1)}, u32[]{:S(2)}) copy-start(bf16[4096,128]{1,0:T(8,128)(2,1)} %param.10) | copy-start | bytes 3145732
  6.5 40.2 %all-gather.2.cloned.1.call-start = ((), (), s32[]{:S(2)}) async-start(), calls=%async_computation.1 | async-start | bytes 4718592 | tf_op jit(solution)/shard_map/all_gather | solution.py:22
  7.3 198.2 %reduce-scatter.2.cloned.1.call-start = ((), (), s32[]{:S(2)}) async-start(), calls=%async_computation.2 | async-start | bytes 4718592 | tf_op jit(solution)/shard_map/reduce_scatter | solution.py:75
  46.7 3.6 %copy-start.7 = (bf16[512,4096]{1,0:T(8,128)(2,1)S(1)}, bf16[512,4096]{1,0:T(8,128)(2,1)}, u32[]{:S(2)}) copy-start(bf16[512,4096]{1,0:T(8,128)(2,1)} %all-gather.2.cloned.1.call-done) | copy-start | bytes 12582916
  50.3 24.2 %copy-start.6 = (bf16[4096,512]{1,0:T(8,128)(2,1)S(1)}, bf16[4096,512]{1,0:T(8,128)(2,1)}, u32[]{:S(2)}) copy-start(bf16[4096,512]{1,0:T(8,128)(2,1)} %param.9) | copy-start | bytes 12582916
  51.6 20.9 %copy-start.4 = (bf16[512,128]{1,0:T(8,128)(2,1)}, bf16[512,128]{1,0:T(8,128)(2,1)S(1)}, u32[]{:S(2)}) copy-start(bf16[512,128]{1,0:T(8,128)(2,1)S(1)} %convolution_convert_fusion.3) | copy-start | bytes 393220
  52.4 87.0 %collective-permute-start.7 = (bf16[2,4,128,128]{3,2,1,0:T(8,128)(2,1)}, bf16[2,4,128,128]{3,2,1,0:T(8,128)(2,1)}, u32[]{:S(2)}, u32[]{:S(2)}) collective-permute-start(bf16[2,4,128,128]{3,2,1,0:T(8,128)(2,1)} %pad_maximum_fusion), channel_id=1, source_target_pairs={{32,0},{40,8},{48,16},{56,24},{64,32},{72,40},{80,48},{88,56},{96,... | collective-permute-start | bytes 786440 | tf_op jit(solution)/shard_map/ppermute | solution.py:15
  60.3 78.1 %collective-permute-start.6 = (bf16[2,4,128,128]{3,2,1,0:T(8,128)(2,1)}, bf16[2,4,128,128]{3,2,1,0:T(8,128)(2,1)}, u32[]{:S(2)}, u32[]{:S(2)}) collective-permute-start(bf16[2,4,128,128]{3,2,1,0:T(8,128)(2,1)} %pad_maximum_fusion), channel_id=1, source_target_pairs={{24,0},{32,8},{40,16},{48,24},{56,32},{64,40},{72,48},{80,56},{88,... | collective-permute-start | bytes 786440 | tf_op jit(solution)/shard_map/ppermute | solution.py:15
  62.5 60.2 %collective-permute-start.2 = (bf16[2,4,128,128]{3,2,1,0:T(8,128)(2,1)}, bf16[2,4,128,128]{3,2,1,0:T(8,128)(2,1)}, u32[]{:S(2)}, u32[]{:S(2)}) collective-permute-start(bf16[2,4,128,128]{3,2,1,0:T(8,128)(2,1)} %pad_maximum_fusion), channel_id=1, source_target_pairs={{0,16},{8,24},{16,32},{24,40},{32,48},{40,56},{48,64},{56,72},{64,... | collective-permute-start | bytes 786440 | tf_op jit(solution)/shard_map/ppermute | solution.py:15
  67.0 47.3 %collective-permute-start.1 = (bf16[2,4,128,128]{3,2,1,0:T(8,128)(2,1)}, bf16[2,4,128,128]{3,2,1,0:T(8,128)(2,1)}, u32[]{:S(2)}, u32[]{:S(2)}) collective-permute-start(bf16[2,4,128,128]{3,2,1,0:T(8,128)(2,1)} %pad_maximum_fusion), channel_id=1, source_target_pairs={{0,24},{8,32},{16,40},{24,48},{32,56},{40,64},{48,72},{56,80},{64,... | collective-permute-start | bytes 786440 | tf_op jit(solution)/shard_map/ppermute | solution.py:15
  72.5 38.1 %collective-permute-start = (bf16[2,4,128,128]{3,2,1,0:T(8,128)(2,1)}, bf16[2,4,128,128]{3,2,1,0:T(8,128)(2,1)S(1)}, u32[]{:S(2)}, u32[]{:S(2)}) collective-permute-start(bf16[2,4,128,128]{3,2,1,0:T(8,128)(2,1)} %pad_maximum_fusion), channel_id=1, source_target_pairs={{0,32},{8,40},{16,48},{24,56},{32,64},{40,72},{48,80},{56,88},{64,... | collective-permute-start | bytes 786440 | tf_op jit(solution)/shard_map/ppermute | solution.py:15
  110.6 0.7 copy-start.5
  111.4 16.5 %collective-permute-start.3 = (bf16[2,4,128,128]{3,2,1,0:T(8,128)(2,1)}, bf16[2,4,128,128]{3,2,1,0:T(8,128)(2,1)S(1)}, u32[]{:S(2)}, u32[]{:S(2)}) collective-permute-start(bf16[2,4,128,128]{3,2,1,0:T(8,128)(2,1)} %pad_maximum_fusion), channel_id=1, source_target_pairs={{0,8},{8,16},{16,24},{24,32},{32,40},{40,48},{48,56},{56,64},{64,7... | collective-permute-start | bytes 786440 | tf_op jit(solution)/shard_map/ppermute | solution.py:15
  114.2 24.1 %collective-permute-start.5 = (bf16[2,4,128,128]{3,2,1,0:T(8,128)(2,1)}, bf16[2,4,128,128]{3,2,1,0:T(8,128)(2,1)S(1)}, u32[]{:S(2)}, u32[]{:S(2)}) collective-permute-start(bf16[2,4,128,128]{3,2,1,0:T(8,128)(2,1)} %pad_maximum_fusion), channel_id=1, source_target_pairs={{16,0},{24,8},{32,16},{40,24},{48,32},{56,40},{64,48},{72,56},{80,... | collective-permute-start | bytes 786440 | tf_op jit(solution)/shard_map/ppermute | solution.py:15
  122.7 15.6 %collective-permute-start.4 = (bf16[2,4,128,128]{3,2,1,0:T(8,128)(2,1)}, bf16[2,4,128,128]{3,2,1,0:T(8,128)(2,1)S(1)}, u32[]{:S(2)}, u32[]{:S(2)}) collective-permute-start(bf16[2,4,128,128]{3,2,1,0:T(8,128)(2,1)} %pad_maximum_fusion), channel_id=1, source_target_pairs={{8,0},{16,8},{24,16},{32,24},{40,32},{48,40},{56,48},{64,56},{72,6... | collective-permute-start | bytes 786440 | tf_op jit(solution)/shard_map/ppermute | solution.py:15
  143.4 2.9 %copy-start.1 = (pred[4,128,16,128]{1,3,2,0:T(8,128)(4,1)S(1)}, pred[4,128,16,128]{1,3,2,0:T(8,128)(4,1)}, u32[]{:S(2)}) copy-start(pred[4,128,16,128]{1,3,2,0:T(8,128)(4,1)} %or_and_fusion) | copy-start | bytes 3145732
  143.5 2.9 %copy-start.3 = (bf16[4,128,4,128]{3,2,1,0:T(4,128)(2,1)S(1)}, bf16[4,128,4,128]{3,2,1,0:T(4,128)(2,1)}, u32[]{:S(2)}) copy-start(bf16[4,128,4,128]{3,2,1,0:T(4,128)(2,1)} %reshape.90) | copy-start | bytes 1572868
  146.3 2.6 %copy-start.2 = (bf16[64,2,128,128]{3,2,0,1:T(8,128)(2,1)}, bf16[64,2,128,128]{3,2,0,1:T(8,128)(2,1)S(1)}, u32[]{:S(2)}) copy-start(bf16[64,2,128,128]{3,2,0,1:T(8,128)(2,1)S(1)} %copy.18) | copy-start | bytes 12582916
Sparse Core Ops, SparseCore 0:
  9.2 37.5 all-gather.1
  166.5 38.9 reduce-scatter.1
where the time goes:
time: 213 us; the launch traced here: 212 us
  waiting for transfers between devices  114 us (54%)
  starting transfers between devices  35.6 us (17%)
  matrix products  22.5 us (11%)
  between operations  13.7 us (6%)
  other arithmetic  13.6 us (6%)
  local copies, waits for them, and re-layouts  13 us (6%)
    ppermute x8, waiting for transfers between devices, from_behind(): return lax.ppermute(block, axis, route)  42.4 us
    reduce_scatter x1, waiting for transfers between devices, local(): lax.psum_scatter(jnp.dot(attended, out_weight, preferred_element_type=jnp...  39.1 us
    ppermute x8, starting transfers between devices, from_behind(): return lax.ppermute(block, axis, route)  35.6 us
    all_gather x1, waiting for transfers between devices, local(): piece = lax.all_gather(tokens, 'tp', axis=1, tiled=True)  31.7 us
    dot_general x3, matrix products, local(): jnp.dot(piece, weight, preferred_element_type=jnp.float32)  7.17 us
    dot_general x1, matrix products, local(): jnp.dot(attended, out_weight, preferred_element_type=jnp.float32)  6.49 us
    dot_general x1, matrix products, local(): jnp.einsum('bhgqsk,bskhd->bqhgd', weights, chosen_values, preferred_eleme...  6.27 us
    gather x2, local copies, waits for them, and re-layouts, local(): chosen = jnp.take(source, links - anchor, axis=1, mode='clip')  5.91 us
  transfers between devices with their start and end apart: 10, of which 4 were waited for; matrix products, arithmetic and copies ran while one was open for 8% of the time, Pallas kernels for 0%

commit v1 on v0

v1 whole, which is shorter than its diff:
```python
import jax
import jax.numpy as jnp
from jax import lax
from jax.experimental import pallas as pl
from jax.experimental.pallas import tpu as pltpu
from jax.sharding import PartitionSpec as P

HEAD_DIM = 128
BLOCK = 128
LINKS = 16
REACH = 4
GROUP = 4
HALF = BLOCK // 2
ROWS = GROUP * BLOCK
NEG = -1e30
RATE = 1.4426950408889634 * HEAD_DIM ** (-0.5)


SWAP = [(t, t ^ 1) for t in range(8)]


def swap(x):
    return lax.ppermute(x, "tp", SWAP)


def shift(x, chips):
    return lax.ppermute(x, "tp", [(t, (t + 2 * chips) % 8) for t in range(8)])


def ring(x, step):
    n = lax.axis_size("ctx")
    return lax.ppermute(x, "ctx", [(i, i + step) for i in range(n) if 0 <= i + step < n])


def smem():
    return pl.BlockSpec(memory_space=pltpu.SMEM)


def vmem():
    return pl.BlockSpec(memory_space=pltpu.VMEM)


def limit(mib):
    return pltpu.CompilerParams(vmem_limit_bytes=mib << 20)


def chip_and_core():
    t = lax.axis_index("tp")
    return t // 2, t % 2


def destination(which):
    chip, core = chip_and_core()
    return (chip + (2, 1, 3, 0)[which]) % 4, core


def project_kernel(*refs, counts, weights, added, finish, chips):
    refs = list(refs)
    xs = []
    for c in counts:
        xs.append([refs.pop(0) for _ in range(c)])
    ws = [refs.pop(0) for _ in range(weights)]
    before = [refs.pop(0) for _ in range(weights)] if added else [None] * weights
    chip, core = chip_and_core()
    accs = [None if ref is None else ref[...] for ref in before]
    for n, parts in enumerate(xs):
        x = parts[0][...] if len(parts) == 1 else jnp.concatenate([p[...] for p in parts], axis=0)
        width = x.shape[1]
        source = 2 * ((chip + chips[n // 2]) % 4) + (core if n % 2 == 0 else 1 - core)
        first = pl.multiple_of(source * width, width)
        for k, w in enumerate(ws):
            part = jnp.dot(x, w[pl.ds(first, width), :], preferred_element_type=jnp.float32)
            accs[k] = part if accs[k] is None else accs[k] + part
    finish(refs, accs)


def project(chips, chunks, ws, before, out_shape, finish):
    flat = [part for chunk in chunks for part in chunk]
    counts = [len(chunk) for chunk in chunks]
    rows = sum(part.shape[0] for part in chunks[0])
    width = chunks[0][0].shape[1]
    cols = sum(w.shape[1] for w in ws)
    n = len(chunks)
    body = lambda *refs: project_kernel(
        *refs, counts=counts, weights=len(ws), added=bool(before), finish=finish, chips=chips
    )
    return pl.pallas_call(
        body,
        out_shape=out_shape,
        in_specs=[vmem()] * (len(flat) + len(ws) + len(before)),
        out_specs=jax.tree.map(lambda _: vmem(), out_shape),
        cost_estimate=pl.CostEstimate(
            flops=2 * rows * width * n * cols,
            transcendentals=0,
            bytes_accessed=2 * n * width * (rows + cols),
        ),
        compiler_params=limit(20),
    )(*flat, *ws, *before)


def split_kernel(up, down, first, second):
    rows = first.shape[0]
    first[...] = up[pl.ds(0, rows), :]
    second[...] = down[pl.ds(rows, rows), :]


def split(up, down):
    shape = jax.ShapeDtypeStruct((up.shape[0] // 2, up.shape[1]), up.dtype)
    return pl.pallas_call(
        split_kernel,
        out_shape=(shape, shape),
        in_specs=[vmem()] * 2,
        out_specs=(vmem(), vmem()),
        compiler_params=limit(2),
        name="split",
    )(up, down)


def add_kernel(*refs):
    total = refs[0][...].astype(jnp.float32)
    for ref in refs[1:-1]:
        total = total + ref[...].astype(jnp.float32)
    refs[-1][...] = total.astype(jnp.bfloat16)


def add(*parts):
    return pl.pallas_call(
        add_kernel,
        out_shape=jax.ShapeDtypeStruct(parts[0].shape, parts[0].dtype),
        in_specs=[vmem()] * len(parts),
        out_specs=vmem(),
        compiler_params=limit(6),
        name="add",
    )(*parts)


def keep_sums(out, accs):
    for ref, acc in zip(out, accs):
        ref[...] = acc


def store_kv(out, accs):
    kv = out[0]
    for b in range(kv.shape[1]):
        rows = slice(b * BLOCK, (b + 1) * BLOCK)
        kv[0, b] = accs[0][rows].T.astype(jnp.bfloat16)
        kv[1, b] = accs[1][rows].astype(jnp.bfloat16)


def store_q(out, accs):
    q = accs[0].astype(jnp.bfloat16)
    for b in range(q.shape[0] // BLOCK):
        for g in range(GROUP):
            out[0][b, pl.ds(g * BLOCK, BLOCK), :] = q[
                b * BLOCK : (b + 1) * BLOCK, g * HEAD_DIM : (g + 1) * HEAD_DIM
            ]


def absorb(table, line, q, below, above, m, l, acc):
    n = table[line, 0]

    def pick(kind, entry):
        return jnp.where(entry >= 4, above[kind, entry % 4], below[kind, entry % 4])

    def pair(p, carry):
        a = table[line, 1 + 2 * p]
        d = table[line, 2 + 2 * p]
        keys = jnp.concatenate([pick(0, a), pick(0, d)], axis=1)
        s = jnp.dot(q[...], keys, preferred_element_type=jnp.float32)
        s1 = s[:, :BLOCK]
        s2 = jnp.where(2 * p + 1 < n, s[:, BLOCK:], NEG)
        old = m[...]
        new = jnp.maximum(old, jnp.max(jnp.maximum(s1, s2), axis=1, keepdims=True))
        m[...] = new
        fade = jnp.exp2((old - new) * RATE)
        p1 = jnp.exp2((s1 - new) * RATE)
        p2 = jnp.exp2((s2 - new) * RATE)
        l[...] = l[...] * fade + (p1 + p2)
        w = jnp.concatenate([p1.astype(jnp.bfloat16), p2.astype(jnp.bfloat16)], axis=1)
        values = jnp.concatenate([pick(1, a), pick(1, d)], axis=0)
        acc[...] = acc[...] * fade + jnp.dot(w, values, preferred_element_type=jnp.float32)
        return carry

    lax.fori_loop(0, (n + 1) // 2, pair, 0)


def table_kernel(links, counts, docs, table):
    ctx = lax.axis_index("ctx")
    for line in range(5 * 4):
        table[line, 0] = 0
    for b in range(4):
        i = ctx * 4 + b
        mine = docs[i]
        live = counts[b]
        for s in range(1, LINKS):
            j = links[b, s]
            away = j // 4 - ctx
            line = jnp.abs(away) * 4 + b
            at = table[line, 0]
            ok = (s < live) & ((j < i) | (docs[j] != mine))
            table[line, 1 + at] = jnp.where(away > 0, 4, 0) + j % 4
            table[line, 0] = at + ok.astype(jnp.int32)
    for line in range(5 * 4):
        table[line, 1 + table[line, 0]] = 0


def list_slots(links, counts, docs):
    return pl.pallas_call(
        table_kernel,
        out_shape=jax.ShapeDtypeStruct((5 * 4, LINKS + 2), jnp.int32),
        in_specs=[smem()] * 3,
        out_specs=smem(),
        compiler_params=limit(1),
        name="list_slots",
    )(links, counts, docs)


def begin(q, own, b, m, l, acc):
    s = jnp.dot(q[...], own[0, b], preferred_element_type=jnp.float32)
    row = lax.broadcasted_iota(jnp.int32, s.shape, 0) % BLOCK
    col = lax.broadcasted_iota(jnp.int32, s.shape, 1)
    s = jnp.where(col <= row, s, NEG)
    top = jnp.broadcast_to(jnp.max(s, axis=1, keepdims=True), s.shape)
    w = jnp.exp2((s - top) * RATE)
    m[...] = top
    l[...] = w
    acc[...] = jnp.dot(w.astype(jnp.bfloat16), own[1, b], preferred_element_type=jnp.float32)


def close(core, l, acc, wo, keep, give, wide):
    total = jnp.sum(l[...], axis=1, keepdims=True)
    res = (acc[...] / total).astype(jnp.bfloat16)
    for g in range(GROUP):
        wide[:, pl.ds(g * HEAD_DIM, HEAD_DIM)] = res[g * BLOCK : (g + 1) * BLOCK]
    mine = wide[pl.ds(pl.multiple_of(core * HALF, HALF), HALF), :]
    other = wide[pl.ds(pl.multiple_of((1 - core) * HALF, HALF), HALF), :]
    both = jnp.concatenate([mine, other], axis=0)
    term = jnp.dot(both, wo[...], preferred_element_type=jnp.float32).astype(jnp.bfloat16)
    keep[...] = term[:HALF]
    give[...] = term[HALF:]


def attend_kernel(table, q, *refs, which, steps, starts, ends):
    refs = list(refs)
    b, core = destination(which)
    q = q.at[b]
    own = refs.pop(0) if 0 in steps else None
    pieces = {k: (refs.pop(0), refs.pop(0)) for k in steps if k}
    state0 = [] if starts else [refs.pop(0) for _ in range(3)]
    wo = refs.pop(0) if ends else None
    if ends:
        keep, give, m, l, acc, wide = refs
    else:
        m, l, acc = refs
    if starts:
        begin(q, own, b, m, l, acc)
    else:
        for now, past in zip((m, l, acc), state0):
            now[...] = past[...]
    for k in steps:
        below, above = pieces[k] if k else (own, own)
        absorb(table, 4 * k + b, q, below, above, m, l, acc)
    if ends:
        close(core, l, acc, wo, keep, give, wide)


def attend(table, q, which, pieces, state, wo):
    steps = sorted(pieces)
    flat = [piece for k in steps for piece in pieces[k]]
    starts, ends = state is None, wo is not None
    one = jax.ShapeDtypeStruct((ROWS, HEAD_DIM), jnp.float32)
    scratch = [pltpu.VMEM((ROWS, HEAD_DIM), jnp.float32)] * 3
    if ends:
        out_shape = (jax.ShapeDtypeStruct((HALF, wo.shape[1]), jnp.bfloat16),) * 2
        scratch = scratch + [pltpu.VMEM((BLOCK, GROUP * HEAD_DIM), jnp.bfloat16)]
    else:
        out_shape, scratch = (one,) * 3, []
    args = flat + ([] if starts else list(state)) + ([wo] if ends else [])
    return pl.pallas_call(
        lambda *refs: attend_kernel(
            *refs, which=which, steps=steps, starts=starts, ends=ends
        ),
        out_shape=out_shape,
        in_specs=[smem()] + [vmem()] * (1 + len(args)),
        out_specs=(vmem(),) * len(out_shape),
        scratch_shapes=scratch,
        cost_estimate=pl.CostEstimate(
            flops=1 << 29, transcendentals=1 << 20, bytes_accessed=4 << 20
        ),
        compiler_params=limit(16),
    )(table, q, *args)


def layer(tokens, query_weight, key_weight, value_weight, out_weight, links, counts, doc_ids):
    rows = tokens.shape[0]
    table = list_slots(links, counts, doc_ids)

    up, down = shift(tokens, 1), shift(tokens, -1)
    twin = swap(tokens)
    halves = split(up, down)
    far = [shift(halves[0], 1), shift(halves[1], -1)]
    first = [[tokens], [twin], [up], [swap(up)], [down], [swap(down)]]
    second = [far, [swap(far[0]), swap(far[1])]]

    sums = lambda *cols: tuple(jax.ShapeDtypeStruct((rows, n), jnp.float32) for n in cols)
    kv_weights = [key_weight, value_weight]
    *kv_sums, q_sums = project(
        (0, 3, 1), first, kv_weights + [query_weight], [], sums(128, 128, 512), keep_sums
    )
    kv_shape = (jax.ShapeDtypeStruct((2, rows // BLOCK, BLOCK, HEAD_DIM), jnp.bfloat16),)
    kv = project((2,), second, kv_weights, kv_sums, kv_shape, store_kv)[0]
    q_shape = (jax.ShapeDtypeStruct((rows // BLOCK, ROWS, HEAD_DIM), jnp.bfloat16),)
    q = project((2,), second, [query_weight], [q_sums], q_shape, store_q)[0]

    pieces = {0: (kv,)}
    below = above = kv
    for k in range(1, REACH + 1):
        below, above = ring(below, 1), ring(above, -1)
        pieces[k] = below, above
    early = {k: pieces[k] for k in range(REACH)}
    state = attend(table, q, 0, early, None, None)
    whole = lambda which: attend(table, q, which, pieces, None, out_weight)
    merge = lambda pair: add(pair[0], swap(pair[1]))

    pair = attend(table, q, 0, {REACH: pieces[REACH]}, state, out_weight)
    across = shift(merge(pair), 2)
    from_below = shift(merge(whole(1)), 1)
    from_above = shift(merge(whole(2)), -1)
    keep, give = whole(3)
    return add(keep, swap(give), across, from_below, from_above)


def solution(mesh):
    placed = (
        P("ctx", "tp"),
        P(None, "tp"),
        P(None, "tp"),
        P(None, "tp"),
        P("tp", None),
        P("ctx", None),
        P("ctx"),
        P(),
    )
    return jax.shard_map(
        layer, mesh=mesh, in_specs=placed, out_specs=P(("ctx", "tp"), None), check_vma=False
    )
```

time: 213 us -> 138 us (0.65)
  waiting for transfers between devices: 114 us -> 53.4 us
  Pallas kernels: 0 us -> 27.9 us
  matrix products: 22.5 us -> 0 us
  other arithmetic: 13.6 us -> 0 us
  between operations: 13.7 us -> 0.32 us
  starting transfers between devices: 35.6 us -> 48.5 us
  local copies, waits for them, and re-layouts: 13 us -> 5.7 us
    reduce_scatter x1 -> x0, waiting for transfers between devices: 39.1 us -> none  [local(): lax.psum_scatter(jnp.dot(attended, out_weight, preferred_element_type=jnp...]
    all_gather x1 -> x0, waiting for transfers between devices: 31.7 us -> none  [local(): piece = lax.all_gather(tokens, 'tp', axis=1, tiled=True)]
    pallas_call x0 -> x14, Pallas kernels: none -> 27.9 us  [the longest x5 19.1 us: attend(): pl.pallas_call(lambda *refs: attend_kernel(*refs, which=which, steps=step...]
    dot_general x6 -> x0, matrix products: 22.5 us -> none  [the longest x3 7.17 us: local(): jnp.dot(piece, weight, preferred_element_type=jnp.float32)]
    ppermute x8 -> x24, starting transfers between devices: 35.6 us -> 48.5 us  [the longest x8 33.8 us: ring(): lax.ppermute(x, 'ctx', [(i, i + step) for i in range(n) if 0 <= i + step...]
    ppermute x8 -> x24, waiting for transfers between devices: 42.4 us -> 53.4 us  [the longest x7 42.1 us: shift(): return lax.ppermute(x, 'tp', [(t, (t + 2 * chips) % 8) for t in range(8)])]
    reduce_sum x3 -> x0, other arithmetic: 6.01 us -> none  [the longest x1 4.27 us: local(): total = jnp.sum(powers, axis=(4, 5), keepdims=True)]
    gather x2 -> x0, local copies, waits for them, and re-layouts: 5.91 us -> none  [local(): chosen = jnp.take(source, links - anchor, axis=1, mode='clip')]
  transfers between devices with their start and end apart: 10 -> 24, of which waited for: 4 -> 8; matrix products, arithmetic and copies ran while one was open for 8% -> 0% of each run, Pallas kernels for 0% -> 16%
where the time goes in v1:
time: 138 us; the launch traced here: 136 us
  waiting for transfers between devices  53.4 us (39%)
  starting transfers between devices  48.5 us (35%)
  Pallas kernels  27.9 us (20%)
  local copies, waits for them, and re-layouts  5.7 us (4%)
    ppermute x7, waiting for transfers between devices, shift(): return lax.ppermute(x, 'tp', [(t, (t + 2 * chips) % 8) for t in range(8)])  42.1 us
    ppermute x8, starting transfers between devices, ring(): lax.ppermute(x, 'ctx', [(i, i + step) for i in range(n) if 0 <= i + step...  33.8 us
    pallas_call x5, Pallas kernels, attend(): pl.pallas_call(lambda *refs: attend_kernel(*refs, which=which, steps=step...  19.1 us
    ppermute x7, starting transfers between devices, shift(): return lax.ppermute(x, 'tp', [(t, (t + 2 * chips) % 8) for t in range(8)])  12.5 us
    ppermute x8, waiting for transfers between devices, ring(): lax.ppermute(x, 'ctx', [(i, i + step) for i in range(n) if 0 <= i + step...  11.3 us
    unnamed x20, local copies, waits for them, and re-layouts  5.7 us
    pallas_call x3, Pallas kernels, project(): pl.pallas_call(body, out_shape=out_shape, in_specs=[vmem()] * (len(flat)...  4.94 us
  transfers between devices with their start and end apart: 24, of which 8 were waited for; matrix products, arithmetic and copies ran while one was open for 0% of the time, Pallas kernels for 16%

profile of v1, /device:TPU:6, one launch (start us, length us, event | category | flops | bytes accessed | tf_op | source)
XLA Modules:
  0.0 135.8 jit_solution(3169304997692427861)
XLA Ops:
  0.0 1.6 %collective-permute-start = (bf16[512,512]{1,0:T(8,128)(2,1)}, bf16[512,512]{1,0:T(8,128)(2,1)S(1)}, u32[]{:S(2)}, u32[]{:S(2)}) collective-permute-start(bf16[512,512]{1,0:T(8,128)(2,1)} %refs_0_.1), channel_id=1, source_target_pairs={{0,2},{1,3},{2,4},{3,5},{4,6},{5,7},{6,0},{7,1},{8,10},{9,11},{10,... | collective-permute-start | bytes 1572872 | tf_op jit(solution)/shard_map/ppermute | solution.py:27
  1.6 1.7 %collective-permute-start.1 = (bf16[512,512]{1,0:T(8,128)(2,1)}, bf16[512,512]{1,0:T(8,128)(2,1)S(1)}, u32[]{:S(2)}, u32[]{:S(2)}) collective-permute-start(bf16[512,512]{1,0:T(8,128)(2,1)} %refs_0_.1), channel_id=1, source_target_pairs={{0,6},{1,7},{2,0},{3,1},{4,2},{5,3},{6,4},{7,5},{8,14},{9,15},{10,... | collective-permute-start | bytes 1572872 | tf_op jit(solution)/shard_map/ppermute | solution.py:27
  3.2 11.9 %collective-permute-done.up.refs_2_ = bf16[512,512]{1,0:T(8,128)(2,1)S(1)} collective-permute-done((bf16[512,512]{1,0:T(8,128)(2,1)}, bf16[512,512]{1,0:T(8,128)(2,1)S(1)}, u32[]{:S(2)}, u32[]{:S(2)}) %collective-permute-start) | collective-permute-done | bytes 524320 | tf_op jit(solution)/shard_map/ppermute | solution.py:27
  15.1 0.0 collective-permute-done.1.down.refs_4_
  15.2 0.5 collective-permute-start.8
  15.7 0.0 copy-start.7
  15.7 1.2 collective-permute-start.2
  16.9 2.1 %collective-permute-start.3 = (bf16[256,512]{1,0:T(8,128)(2,1)S(1)}, bf16[256,512]{1,0:T(8,128)(2,1)S(1)}, u32[]{:S(2)}, u32[]{:S(2)}) collective-permute-start(bf16[256,512]{1,0:T(8,128)(2,1)S(1)} %get-tuple-element.22), channel_id=1, source_target_pairs={{0,6},{1,7},{2,0},{3,1},{4,2},{5,3},{6,4},{7,5},{8,14},{9,15},{10,... | collective-permute-start | bytes 786440 | tf_op jit(solution)/shard_map/ppermute | solution.py:27
  19.0 6.2 %collective-permute-done.2.refs_0_ = bf16[256,512]{1,0:T(8,128)(2,1)S(1)} collective-permute-done((bf16[256,512]{1,0:T(8,128)(2,1)S(1)}, bf16[256,512]{1,0:T(8,128)(2,1)S(1)}, u32[]{:S(2)}, u32[]{:S(2)}) %collective-permute-start.2) | collective-permute-done | bytes 262176 | tf_op jit(solution)/shard_map/ppermute | solution.py:27
  25.2 0.1 collective-permute-done.3.refs_1_
  25.3 0.4 collective-permute-start.5
  25.8 2.2 %copy-done.1 = bf16[4096,512]{1,0:T(8,128)(2,1)S(1)} copy-done((bf16[4096,512]{1,0:T(8,128)(2,1)S(1)}, bf16[4096,512]{1,0:T(8,128)(2,1)}, u32[]{:S(2)}) %copy-start.1) | copy-done | bytes 4194328
  28.0 1.2 copy-done.3
  29.2 1.2 copy-done.5
  30.4 1.0 copy-done.6
  31.4 3.4 %shard_map.82 = (f32[512,128]{1,0:T(8,128)S(1)}, f32[512,128]{1,0:T(8,128)S(1)}, f32[512,512]{1,0:T(8,128)S(1)}) custom-call(bf16[512,512]{1,0:T(8,128)(2,1)S(1)} %copy-done.6, bf16[512,512]{1,0:T(8,128)(2,1)S(1)} %collective-permute-done.6.refs_1_, bf16[512,512]{1,0:T(8,128)(2,1)S(1)} %collective-permute-done.up.refs_2_, ...), custom_call_target="tpu_custom_call" | custom-call | flops 2415919104 | bytes 7864320 | tf_op jit(solution)/shard_map/pallas_call | solution.py:87
  34.9 0.8 shard_map.84.refs_2_
  35.7 3.8 %collective-permute-start.9 = (bf16[2,4,128,128]{3,2,1,0:T(8,128)(2,1)S(1)}, bf16[2,4,128,128]{3,2,1,0:T(8,128)(2,1)S(1)}, u32[]{:S(2)}, u32[]{:S(2)}) collective-permute-start(bf16[2,4,128,128]{3,2,1,0:T(8,128)(2,1)S(1)} %shard_map.84.refs_2_), channel_id=1, source_target_pairs={{0,8},{8,16},{16,24},{24,32},{32,40},{40,48},{48,56},{56,64},{64,7... | collective-permute-start | bytes 786440 | tf_op jit(solution)/shard_map/ppermute | solution.py:32
  39.5 6.1 %collective-permute-start.10 = (bf16[2,4,128,128]{3,2,1,0:T(8,128)(2,1)S(1)}, bf16[2,4,128,128]{3,2,1,0:T(8,128)(2,1)S(1)}, u32[]{:S(2)}, u32[]{:S(2)}) collective-permute-start(bf16[2,4,128,128]{3,2,1,0:T(8,128)(2,1)S(1)} %shard_map.84.refs_2_), channel_id=1, source_target_pairs={{8,0},{16,8},{24,16},{32,24},{40,32},{48,40},{56,48},{64,56},{72,6... | collective-permute-start | bytes 786440 | tf_op jit(solution)/shard_map/ppermute | solution.py:32
  45.7 4.6 %collective-permute-done.9.refs_3_ = bf16[2,4,128,128]{3,2,1,0:T(8,128)(2,1)S(1)} collective-permute-done((bf16[2,4,128,128]{3,2,1,0:T(8,128)(2,1)S(1)}, bf16[2,4,128,128]{3,2,1,0:T(8,128)(2,1)S(1)}, u32[]{:S(2)}, u32[]{:S(2)}) %collective-permute-start.9) | collective-permute-done | bytes 262176 | tf_op jit(solution)/shard_map/ppermute | solution.py:32
  50.3 1.9 %collective-permute-start.11 = (bf16[2,4,128,128]{3,2,1,0:T(8,128)(2,1)S(1)}, bf16[2,4,128,128]{3,2,1,0:T(8,128)(2,1)S(1)}, u32[]{:S(2)}, u32[]{:S(2)}) collective-permute-start(bf16[2,4,128,128]{3,2,1,0:T(8,128)(2,1)S(1)} %collective-permute-done.9.refs_3_), channel_id=1, source_target_pairs={{0,8},{8,16},{16,24},{24,32},{32,40},{40,48},{48,56},{56,64},{64,7... | collective-permute-start | bytes 786440 | tf_op jit(solution)/shard_map/ppermute | solution.py:32
  52.2 6.0 %collective-permute-start.12 = (bf16[2,4,128,128]{3,2,1,0:T(8,128)(2,1)S(1)}, bf16[2,4,128,128]{3,2,1,0:T(8,128)(2,1)S(1)}, u32[]{:S(2)}, u32[]{:S(2)}) collective-permute-start(bf16[2,4,128,128]{3,2,1,0:T(8,128)(2,1)S(1)} %collective-permute-done.10.refs_4_), channel_id=1, source_target_pairs={{8,0},{16,8},{24,16},{32,24},{40,32},{48,40},{56,48},{64,56},{72,6... | collective-permute-start | bytes 786440 | tf_op jit(solution)/shard_map/ppermute | solution.py:32
  58.2 3.7 %collective-permute-done.11.refs_5_ = bf16[2,4,128,128]{3,2,1,0:T(8,128)(2,1)S(1)} collective-permute-done((bf16[2,4,128,128]{3,2,1,0:T(8,128)(2,1)S(1)}, bf16[2,4,128,128]{3,2,1,0:T(8,128)(2,1)S(1)}, u32[]{:S(2)}, u32[]{:S(2)}) %collective-permute-start.11) | collective-permute-done | bytes 262176 | tf_op jit(solution)/shard_map/ppermute | solution.py:32
  62.0 1.9 %collective-permute-start.13 = (bf16[2,4,128,128]{3,2,1,0:T(8,128)(2,1)S(1)}, bf16[2,4,128,128]{3,2,1,0:T(8,128)(2,1)S(1)}, u32[]{:S(2)}, u32[]{:S(2)}) collective-permute-start(bf16[2,4,128,128]{3,2,1,0:T(8,128)(2,1)S(1)} %collective-permute-done.11.refs_5_), channel_id=1, source_target_pairs={{0,8},{8,16},{16,24},{24,32},{32,40},{40,48},{48,56},{56,64},{64,7... | collective-permute-start | bytes 786440 | tf_op jit(solution)/shard_map/ppermute | solution.py:32
  63.9 6.0 %collective-permute-start.14 = (bf16[2,4,128,128]{3,2,1,0:T(8,128)(2,1)S(1)}, bf16[2,4,128,128]{3,2,1,0:T(8,128)(2,1)S(1)}, u32[]{:S(2)}, u32[]{:S(2)}) collective-permute-start(bf16[2,4,128,128]{3,2,1,0:T(8,128)(2,1)S(1)} %collective-permute-done.12.refs_6_), channel_id=1, source_target_pairs={{8,0},{16,8},{24,16},{32,24},{40,32},{48,40},{56,48},{64,56},{72,6... | collective-permute-start | bytes 786440 | tf_op jit(solution)/shard_map/ppermute | solution.py:32
  70.0 2.9 %collective-permute-done.13.refs_7_ = bf16[2,4,128,128]{3,2,1,0:T(8,128)(2,1)S(1)} collective-permute-done((bf16[2,4,128,128]{3,2,1,0:T(8,128)(2,1)S(1)}, bf16[2,4,128,128]{3,2,1,0:T(8,128)(2,1)S(1)}, u32[]{:S(2)}, u32[]{:S(2)}) %collective-permute-start.13) | collective-permute-done | bytes 262176 | tf_op jit(solution)/shard_map/ppermute | solution.py:32
  72.8 1.9 %collective-permute-start.15 = (bf16[2,4,128,128]{3,2,1,0:T(8,128)(2,1)S(1)}, bf16[2,4,128,128]{3,2,1,0:T(8,128)(2,1)S(1)}, u32[]{:S(2)}, u32[]{:S(2)}) collective-permute-start(bf16[2,4,128,128]{3,2,1,0:T(8,128)(2,1)S(1)} %collective-permute-done.13.refs_7_), channel_id=1, source_target_pairs={{0,8},{8,16},{16,24},{24,32},{32,40},{40,48},{48,56},{56,64},{64,7... | collective-permute-start | bytes 786440 | tf_op jit(solution)/shard_map/ppermute | solution.py:32
  74.8 6.0 %collective-permute-start.16 = (bf16[2,4,128,128]{3,2,1,0:T(8,128)(2,1)S(1)}, bf16[2,4,128,128]{3,2,1,0:T(8,128)(2,1)S(1)}, u32[]{:S(2)}, u32[]{:S(2)}) collective-permute-start(bf16[2,4,128,128]{3,2,1,0:T(8,128)(2,1)S(1)} %collective-permute-done.14.refs_8_), channel_id=1, source_target_pairs={{8,0},{16,8},{24,16},{32,24},{40,32},{48,40},{56,48},{64,56},{72,6... | collective-permute-start | bytes 786440 | tf_op jit(solution)/shard_map/ppermute | solution.py:32
  80.8 2.3 %list_slots.1.refs_0_ = s32[20,18]{1,0:T(8,128)S(1)} custom-call(s32[4,16]{1,0:T(4,128)S(1)} %copy-done.7, s32[4]{0:T(128)S(1)} %copy-done.8, s32[128]{0:T(128)S(1)} %copy-done.9), custom_call_target="tpu_custom_call" | custom-call | tf_op jit(solution)/shard_map/list_slots/pallas_call | solution.py:208
  83.2 0.7 shard_map.83.refs_1_
  84.0 3.4 %shard_map.86 = (f32[512,128]{1,0:T(8,128)S(1)}, f32[512,128]{1,0:T(8,128)S(1)}, f32[512,128]{1,0:T(8,128)S(1)}) custom-call(s32[20,18]{1,0:T(8,128)S(1)} %list_slots.1.refs_0_, bf16[4,512,128]{2,1,0:T(8,128)(2,1)S(1)} %shard_map.83.refs_1_, bf16[2,4,128,128]{3,2,1,0:T(8,128)(2,1)S(1)} %shard_map.84.refs_2_, ...), custom_call_target="tpu_custom_call" | custom-call | flops 536870912 | bytes 4194304 | tf_op jit(solution)/shard_map/pallas_call | solution.py:279
  87.4 4.0 %shard_map.89 = (bf16[64,4096]{1,0:T(8,128)(2,1)S(1)}, bf16[64,4096]{1,0:T(8,128)(2,1)S(1)}) custom-call(s32[20,18]{1,0:T(8,128)S(1)} %list_slots.1.refs_0_, bf16[4,512,128]{2,1,0:T(8,128)(2,1)S(1)} %shard_map.83.refs_1_, bf16[2,4,128,128]{3,2,1,0:T(8,128)(2,1)S(1)} %shard_map.84.refs_2_, bf16[2,4,128,128]{3,2,1,0:T(8,128)(2,1)S(1)} %collective-permute-done.9.refs_3_, ...), custom_call_target="tpu_custom_call" | custom-call | flops 536870912 | bytes 4194304 | tf_op jit(solution)/shard_map/pallas_call | solution.py:279
  91.3 0.1 collective-permute-start.22
  91.4 5.0 %shard_map.88 = (bf16[64,4096]{1,0:T(8,128)(2,1)S(1)}, bf16[64,4096]{1,0:T(8,128)(2,1)S(1)}) custom-call(s32[20,18]{1,0:T(8,128)S(1)} %list_slots.1.refs_0_, bf16[4,512,128]{2,1,0:T(8,128)(2,1)S(1)} %shard_map.83.refs_1_, bf16[2,4,128,128]{3,2,1,0:T(8,128)(2,1)S(1)} %shard_map.84.refs_2_, bf16[2,4,128,128]{3,2,1,0:T(8,128)(2,1)S(1)} %collective-permute-done.9.refs_3_, ...), custom_call_target="tpu_custom_call" | custom-call | flops 536870912 | bytes 4194304 | tf_op jit(solution)/shard_map/pallas_call | solution.py:279
  96.4 0.6 collective-permute-start.20
  97.0 1.6 %shard_map.87 = (bf16[64,4096]{1,0:T(8,128)(2,1)S(1)}, bf16[64,4096]{1,0:T(8,128)(2,1)S(1)}) custom-call(s32[20,18]{1,0:T(8,128)S(1)} %list_slots.1.refs_0_, bf16[4,512,128]{2,1,0:T(8,128)(2,1)S(1)} %shard_map.83.refs_1_, bf16[2,4,128,128]{3,2,1,0:T(8,128)(2,1)S(1)} %collective-permute-done.15.refs_9_.refs_2_, ...), custom_call_target="tpu_custom_call" | custom-call | flops 536870912 | bytes 4194304 | tf_op jit(solution)/shard_map/pallas_call | solution.py:279
  98.6 0.1 collective-permute-start.18
  98.7 5.2 %shard_map.85 = (bf16[64,4096]{1,0:T(8,128)(2,1)S(1)}, bf16[64,4096]{1,0:T(8,128)(2,1)S(1)}) custom-call(s32[20,18]{1,0:T(8,128)S(1)} %list_slots.1.refs_0_, bf16[4,512,128]{2,1,0:T(8,128)(2,1)S(1)} %shard_map.83.refs_1_, bf16[2,4,128,128]{3,2,1,0:T(8,128)(2,1)S(1)} %shard_map.84.refs_2_, bf16[2,4,128,128]{3,2,1,0:T(8,128)(2,1)S(1)} %collective-permute-done.9.refs_3_, ...), custom_call_target="tpu_custom_call" | custom-call | flops 536870912 | bytes 4194304 | tf_op jit(solution)/shard_map/pallas_call | solution.py:279
  103.9 0.6 collective-permute-start.17
  104.4 0.1 add.6
  104.6 3.9 %collective-permute-start.23 = (bf16[64,4096]{1,0:T(8,128)(2,1)S(1)}, bf16[64,4096]{1,0:T(8,128)(2,1)S(1)}, u32[]{:S(2)}, u32[]{:S(2)}) collective-permute-start(bf16[64,4096]{1,0:T(8,128)(2,1)S(1)} %add.6), channel_id=1, source_target_pairs={{0,6},{1,7},{2,0},{3,1},{4,2},{5,3},{6,4},{7,5},{8,14},{9,15},{10,... | collective-permute-start | bytes 1572872 | tf_op jit(solution)/shard_map/ppermute | solution.py:27
  108.4 0.1 add.5
  108.6 0.1 collective-permute-start.21
  108.7 0.1 add.4
  108.8 2.0 %collective-permute-start.19 = (bf16[64,4096]{1,0:T(8,128)(2,1)S(1)}, bf16[64,4096]{1,0:T(8,128)(2,1)S(1)}, u32[]{:S(2)}, u32[]{:S(2)}) collective-permute-start(bf16[64,4096]{1,0:T(8,128)(2,1)S(1)} %add.4), channel_id=1, source_target_pairs={{0,4},{1,5},{2,6},{3,7},{4,0},{5,1},{6,2},{7,3},{8,12},{9,13},{10,... | collective-permute-start | bytes 1572872 | tf_op jit(solution)/shard_map/ppermute | solution.py:27
  110.7 20.3 %collective-permute-done.23.refs_4_ = bf16[64,4096]{1,0:T(8,128)(2,1)S(1)} collective-permute-done((bf16[64,4096]{1,0:T(8,128)(2,1)S(1)}, bf16[64,4096]{1,0:T(8,128)(2,1)S(1)}, u32[]{:S(2)}, u32[]{:S(2)}) %collective-permute-start.23) | collective-permute-done | bytes 524320 | tf_op jit(solution)/shard_map/ppermute | solution.py:27
  131.0 3.6 %collective-permute-done.21.refs_3_ = bf16[64,4096]{1,0:T(8,128)(2,1)S(1)} collective-permute-done((bf16[64,4096]{1,0:T(8,128)(2,1)S(1)}, bf16[64,4096]{1,0:T(8,128)(2,1)S(1)}, u32[]{:S(2)}, u32[]{:S(2)}) %collective-permute-start.21) | collective-permute-done | bytes 524320 | tf_op jit(solution)/shard_map/ppermute | solution.py:27
  134.7 1.1 add.7
  (34 shorter events, 0.1 us)
Async XLA Ops:
  0.0 15.1 %collective-permute-start = (bf16[512,512]{1,0:T(8,128)(2,1)}, bf16[512,512]{1,0:T(8,128)(2,1)S(1)}, u32[]{:S(2)}, u32[]{:S(2)}) collective-permute-start(bf16[512,512]{1,0:T(8,128)(2,1)} %refs_0_.1), channel_id=1, source_target_pairs={{0,2},{1,3},{2,4},{3,5},{4,6},{5,7},{6,0},{7,1},{8,10},{9,11},{10,... | collective-permute-start | bytes 1572872 | tf_op jit(solution)/shard_map/ppermute | solution.py:27
  1.6 13.6 %collective-permute-start.1 = (bf16[512,512]{1,0:T(8,128)(2,1)}, bf16[512,512]{1,0:T(8,128)(2,1)S(1)}, u32[]{:S(2)}, u32[]{:S(2)}) collective-permute-start(bf16[512,512]{1,0:T(8,128)(2,1)} %refs_0_.1), channel_id=1, source_target_pairs={{0,6},{1,7},{2,0},{3,1},{4,2},{5,3},{6,4},{7,5},{8,14},{9,15},{10,... | collective-permute-start | bytes 1572872 | tf_op jit(solution)/shard_map/ppermute | solution.py:27
  3.2 22.5 %collective-permute-start.6 = (bf16[512,512]{1,0:T(8,128)(2,1)}, bf16[512,512]{1,0:T(8,128)(2,1)S(1)}, u32[]{:S(2)}, u32[]{:S(2)}) collective-permute-start(bf16[512,512]{1,0:T(8,128)(2,1)} %refs_0_.1), channel_id=1, source_target_pairs={{0,1},{1,0},{2,3},{3,2},{4,5},{5,4},{6,7},{7,6},{8,9},{9,8},{10,11... | collective-permute-start | bytes 1572872 | tf_op jit(solution)/shard_map/ppermute | solution.py:23
  15.1 10.6 %collective-permute-start.7 = (bf16[512,512]{1,0:T(8,128)(2,1)S(1)}, bf16[512,512]{1,0:T(8,128)(2,1)S(1)}, u32[]{:S(2)}, u32[]{:S(2)}) collective-permute-start(bf16[512,512]{1,0:T(8,128)(2,1)S(1)} %collective-permute-done.up.refs_2_), channel_id=1, source_target_pairs={{0,1},{1,0},{2,3},{3,2},{4,5},{5,4},{6,7},{7,6},{8,9},{9,8},{10,11... | collective-permute-start | bytes 1572872 | tf_op jit(solution)/shard_map/ppermute | solution.py:23
  15.2 10.6 %collective-permute-start.8 = (bf16[512,512]{1,0:T(8,128)(2,1)S(1)}, bf16[512,512]{1,0:T(8,128)(2,1)S(1)}, u32[]{:S(2)}, u32[]{:S(2)}) collective-permute-start(bf16[512,512]{1,0:T(8,128)(2,1)S(1)} %collective-permute-done.1.down.refs_4_), channel_id=1, source_target_pairs={{0,1},{1,0},{2,3},{3,2},{4,5},{5,4},{6,7},{7,6},{8,9},{9,8},{10,11... | collective-permute-start | bytes 1572872 | tf_op jit(solution)/shard_map/ppermute | solution.py:23
  15.7 19.2 %copy-start.4 = (bf16[4096,128]{1,0:T(8,128)(2,1)S(1)}, bf16[4096,128]{1,0:T(8,128)(2,1)}, u32[]{:S(2)}) copy-start(bf16[4096,128]{1,0:T(8,128)(2,1)} %refs_4_.3) | copy-start | bytes 3145732
  15.7 65.1 %copy-start.7 = (s32[4,16]{1,0:T(4,128)S(1)}, s32[4,16]{1,0:T(4,128)}, u32[]{:S(2)}) copy-start(s32[4,16]{1,0:T(4,128)} %links.1) | copy-start | bytes 772
  15.7 9.5 %collective-permute-start.2 = (bf16[256,512]{1,0:T(8,128)(2,1)S(1)}, bf16[256,512]{1,0:T(8,128)(2,1)S(1)}, u32[]{:S(2)}, u32[]{:S(2)}) collective-permute-start(bf16[256,512]{1,0:T(8,128)(2,1)S(1)} %get-tuple-element.21), channel_id=1, source_target_pairs={{0,2},{1,3},{2,4},{3,5},{4,6},{5,7},{6,0},{7,1},{8,10},{9,11},{10,... | collective-permute-start | bytes 786440 | tf_op jit(solution)/shard_map/ppermute | solution.py:27
  16.9 63.9 %copy-start.8 = (s32[4]{0:T(128)S(1)}, s32[4]{0:T(128)}, u32[]{:S(2)}) copy-start(s32[4]{0:T(128)} %counts.1) | copy-start | bytes 52
  16.9 64.0 %copy-start.9 = (s32[128]{0:T(128)S(1)}, s32[128]{0:T(128)}, u32[]{:S(2)}) copy-start(s32[128]{0:T(128)} %docs.1) | copy-start | bytes 1540
  16.9 8.4 %collective-permute-start.3 = (bf16[256,512]{1,0:T(8,128)(2,1)S(1)}, bf16[256,512]{1,0:T(8,128)(2,1)S(1)}, u32[]{:S(2)}, u32[]{:S(2)}) collective-permute-start(bf16[256,512]{1,0:T(8,128)(2,1)S(1)} %get-tuple-element.22), channel_id=1, source_target_pairs={{0,6},{1,7},{2,0},{3,1},{4,2},{5,3},{6,4},{7,5},{8,14},{9,15},{10,... | collective-permute-start | bytes 786440 | tf_op jit(solution)/shard_map/ppermute | solution.py:27
  25.2 9.6 %collective-permute-start.4 = (bf16[256,512]{1,0:T(8,128)(2,1)S(1)}, bf16[256,512]{1,0:T(8,128)(2,1)S(1)}, u32[]{:S(2)}, u32[]{:S(2)}) collective-permute-start(bf16[256,512]{1,0:T(8,128)(2,1)S(1)} %collective-permute-done.2.refs_0_), channel_id=1, source_target_pairs={{0,1},{1,0},{2,3},{3,2},{4,5},{5,4},{6,7},{7,6},{8,9},{9,8},{10,11... | collective-permute-start | bytes 786440 | tf_op jit(solution)/shard_map/ppermute | solution.py:23
  25.3 9.6 %collective-permute-start.5 = (bf16[256,512]{1,0:T(8,128)(2,1)S(1)}, bf16[256,512]{1,0:T(8,128)(2,1)S(1)}, u32[]{:S(2)}, u32[]{:S(2)}) collective-permute-start(bf16[256,512]{1,0:T(8,128)(2,1)S(1)} %collective-permute-done.3.refs_1_), channel_id=1, source_target_pairs={{0,1},{1,0},{2,3},{3,2},{4,5},{5,4},{6,7},{7,6},{8,9},{9,8},{10,11... | collective-permute-start | bytes 786440 | tf_op jit(solution)/shard_map/ppermute | solution.py:23
  25.8 2.2 %copy-start.1 = (bf16[4096,512]{1,0:T(8,128)(2,1)S(1)}, bf16[4096,512]{1,0:T(8,128)(2,1)}, u32[]{:S(2)}) copy-start(bf16[4096,512]{1,0:T(8,128)(2,1)} %refs_4_.2) | copy-start | bytes 12582916
  28.0 1.2 copy-start.3
  29.2 1.2 copy-start.5
  30.4 1.0 copy-start.6
  31.4 51.7 %copy-start.2 = (bf16[4096,512]{1,0:T(8,128)(2,1)S(1)}, bf16[4096,512]{1,0:T(8,128)(2,1)}, u32[]{:S(2)}) copy-start(bf16[4096,512]{1,0:T(8,128)(2,1)} %refs_4_.2) | copy-start | bytes 12582916
  35.7 14.6 %collective-permute-start.9 = (bf16[2,4,128,128]{3,2,1,0:T(8,128)(2,1)S(1)}, bf16[2,4,128,128]{3,2,1,0:T(8,128)(2,1)S(1)}, u32[]{:S(2)}, u32[]{:S(2)}) collective-permute-start(bf16[2,4,128,128]{3,2,1,0:T(8,128)(2,1)S(1)} %shard_map.84.refs_2_), channel_id=1, source_target_pairs={{0,8},{8,16},{16,24},{24,32},{32,40},{40,48},{48,56},{56,64},{64,7... | collective-permute-start | bytes 786440 | tf_op jit(solution)/shard_map/ppermute | solution.py:32
  39.5 12.7 %collective-permute-start.10 = (bf16[2,4,128,128]{3,2,1,0:T(8,128)(2,1)S(1)}, bf16[2,4,128,128]{3,2,1,0:T(8,128)(2,1)S(1)}, u32[]{:S(2)}, u32[]{:S(2)}) collective-permute-start(bf16[2,4,128,128]{3,2,1,0:T(8,128)(2,1)S(1)} %shard_map.84.refs_2_), channel_id=1, source_target_pairs={{8,0},{16,8},{24,16},{32,24},{40,32},{48,40},{56,48},{64,56},{72,6... | collective-permute-start | bytes 786440 | tf_op jit(solution)/shard_map/ppermute | solution.py:32
  50.3 11.7 %collective-permute-start.11 = (bf16[2,4,128,128]{3,2,1,0:T(8,128)(2,1)S(1)}, bf16[2,4,128,128]{3,2,1,0:T(8,128)(2,1)S(1)}, u32[]{:S(2)}, u32[]{:S(2)}) collective-permute-start(bf16[2,4,128,128]{3,2,1,0:T(8,128)(2,1)S(1)} %collective-permute-done.9.refs_3_), channel_id=1, source_target_pairs={{0,8},{8,16},{16,24},{24,32},{32,40},{40,48},{48,56},{56,64},{64,7... | collective-permute-start | bytes 786440 | tf_op jit(solution)/shard_map/ppermute | solution.py:32
  52.2 11.7 %collective-permute-start.12 = (bf16[2,4,128,128]{3,2,1,0:T(8,128)(2,1)S(1)}, bf16[2,4,128,128]{3,2,1,0:T(8,128)(2,1)S(1)}, u32[]{:S(2)}, u32[]{:S(2)}) collective-permute-start(bf16[2,4,128,128]{3,2,1,0:T(8,128)(2,1)S(1)} %collective-permute-done.10.refs_4_), channel_id=1, source_target_pairs={{8,0},{16,8},{24,16},{32,24},{40,32},{48,40},{56,48},{64,56},{72,6... | collective-permute-start | bytes 786440 | tf_op jit(solution)/shard_map/ppermute | solution.py:32
  62.0 10.9 %collective-permute-start.13 = (bf16[2,4,128,128]{3,2,1,0:T(8,128)(2,1)S(1)}, bf16[2,4,128,128]{3,2,1,0:T(8,128)(2,1)S(1)}, u32[]{:S(2)}, u32[]{:S(2)}) collective-permute-start(bf16[2,4,128,128]{3,2,1,0:T(8,128)(2,1)S(1)} %collective-permute-done.11.refs_5_), channel_id=1, source_target_pairs={{0,8},{8,16},{16,24},{24,32},{32,40},{40,48},{48,56},{56,64},{64,7... | collective-permute-start | bytes 786440 | tf_op jit(solution)/shard_map/ppermute | solution.py:32
  63.9 10.9 %collective-permute-start.14 = (bf16[2,4,128,128]{3,2,1,0:T(8,128)(2,1)S(1)}, bf16[2,4,128,128]{3,2,1,0:T(8,128)(2,1)S(1)}, u32[]{:S(2)}, u32[]{:S(2)}) collective-permute-start(bf16[2,4,128,128]{3,2,1,0:T(8,128)(2,1)S(1)} %collective-permute-done.12.refs_6_), channel_id=1, source_target_pairs={{8,0},{16,8},{24,16},{32,24},{40,32},{48,40},{56,48},{64,56},{72,6... | collective-permute-start | bytes 786440 | tf_op jit(solution)/shard_map/ppermute | solution.py:32
  72.8 14.5 %collective-permute-start.15 = (bf16[2,4,128,128]{3,2,1,0:T(8,128)(2,1)S(1)}, bf16[2,4,128,128]{3,2,1,0:T(8,128)(2,1)S(1)}, u32[]{:S(2)}, u32[]{:S(2)}) collective-permute-start(bf16[2,4,128,128]{3,2,1,0:T(8,128)(2,1)S(1)} %collective-permute-done.13.refs_7_), channel_id=1, source_target_pairs={{0,8},{8,16},{16,24},{24,32},{32,40},{40,48},{48,56},{56,64},{64,7... | collective-permute-start | bytes 786440 | tf_op jit(solution)/shard_map/ppermute | solution.py:32
  74.8 12.6 %collective-permute-start.16 = (bf16[2,4,128,128]{3,2,1,0:T(8,128)(2,1)S(1)}, bf16[2,4,128,128]{3,2,1,0:T(8,128)(2,1)S(1)}, u32[]{:S(2)}, u32[]{:S(2)}) collective-permute-start(bf16[2,4,128,128]{3,2,1,0:T(8,128)(2,1)S(1)} %collective-permute-done.14.refs_8_), channel_id=1, source_target_pairs={{8,0},{16,8},{24,16},{32,24},{40,32},{48,40},{56,48},{64,56},{72,6... | collective-permute-start | bytes 786440 | tf_op jit(solution)/shard_map/ppermute | solution.py:32
  83.2 4.1 %copy-start = (bf16[512,4096]{1,0:T(8,128)(2,1)S(1)}, bf16[512,4096]{1,0:T(8,128)(2,1)}, u32[]{:S(2)}) copy-start(bf16[512,4096]{1,0:T(8,128)(2,1)} %refs_11_.5) | copy-start | bytes 12582916
  91.3 13.1 %collective-permute-start.22 = (bf16[64,4096]{1,0:T(8,128)(2,1)S(1)}, bf16[64,4096]{1,0:T(8,128)(2,1)S(1)}, u32[]{:S(2)}, u32[]{:S(2)}) collective-permute-start(bf16[64,4096]{1,0:T(8,128)(2,1)S(1)} %get-tuple-element.36), channel_id=1, source_target_pairs={{0,1},{1,0},{2,3},{3,2},{4,5},{5,4},{6,7},{7,6},{8,9},{9,8},{10,11... | collective-permute-start | bytes 1572872 | tf_op jit(solution)/shard_map/ppermute | solution.py:23
  96.4 12.0 %collective-permute-start.20 = (bf16[64,4096]{1,0:T(8,128)(2,1)S(1)}, bf16[64,4096]{1,0:T(8,128)(2,1)S(1)}, u32[]{:S(2)}, u32[]{:S(2)}) collective-permute-start(bf16[64,4096]{1,0:T(8,128)(2,1)S(1)} %get-tuple-element.34), channel_id=1, source_target_pairs={{0,1},{1,0},{2,3},{3,2},{4,5},{5,4},{6,7},{7,6},{8,9},{9,8},{10,11... | collective-permute-start | bytes 1572872 | tf_op jit(solution)/shard_map/ppermute | solution.py:23
  98.6 10.1 %collective-permute-start.18 = (bf16[64,4096]{1,0:T(8,128)(2,1)S(1)}, bf16[64,4096]{1,0:T(8,128)(2,1)S(1)}, u32[]{:S(2)}, u32[]{:S(2)}) collective-permute-start(bf16[64,4096]{1,0:T(8,128)(2,1)S(1)} %get-tuple-element.32), channel_id=1, source_target_pairs={{0,1},{1,0},{2,3},{3,2},{4,5},{5,4},{6,7},{7,6},{8,9},{9,8},{10,11... | collective-permute-start | bytes 1572872 | tf_op jit(solution)/shard_map/ppermute | solution.py:23
  103.9 6.9 %collective-permute-start.17 = (bf16[64,4096]{1,0:T(8,128)(2,1)S(1)}, bf16[64,4096]{1,0:T(8,128)(2,1)S(1)}, u32[]{:S(2)}, u32[]{:S(2)}) collective-permute-start(bf16[64,4096]{1,0:T(8,128)(2,1)S(1)} %get-tuple-element.27), channel_id=1, source_target_pairs={{0,1},{1,0},{2,3},{3,2},{4,5},{5,4},{6,7},{7,6},{8,9},{9,8},{10,11... | collective-permute-start | bytes 1572872 | tf_op jit(solution)/shard_map/ppermute | solution.py:23
  104.6 26.5 %collective-permute-start.23 = (bf16[64,4096]{1,0:T(8,128)(2,1)S(1)}, bf16[64,4096]{1,0:T(8,128)(2,1)S(1)}, u32[]{:S(2)}, u32[]{:S(2)}) collective-permute-start(bf16[64,4096]{1,0:T(8,128)(2,1)S(1)} %add.6), channel_id=1, source_target_pairs={{0,6},{1,7},{2,0},{3,1},{4,2},{5,3},{6,4},{7,5},{8,14},{9,15},{10,... | collective-permute-start | bytes 1572872 | tf_op jit(solution)/shard_map/ppermute | solution.py:27
  108.6 26.1 %collective-permute-start.21 = (bf16[64,4096]{1,0:T(8,128)(2,1)S(1)}, bf16[64,4096]{1,0:T(8,128)(2,1)S(1)}, u32[]{:S(2)}, u32[]{:S(2)}) collective-permute-start(bf16[64,4096]{1,0:T(8,128)(2,1)S(1)} %add.5), channel_id=1, source_target_pairs={{0,2},{1,3},{2,4},{3,5},{4,6},{5,7},{6,0},{7,1},{8,10},{9,11},{10,... | collective-permute-start | bytes 1572872 | tf_op jit(solution)/shard_map/ppermute | solution.py:27
  108.8 25.9 %collective-permute-start.19 = (bf16[64,4096]{1,0:T(8,128)(2,1)S(1)}, bf16[64,4096]{1,0:T(8,128)(2,1)S(1)}, u32[]{:S(2)}, u32[]{:S(2)}) collective-permute-start(bf16[64,4096]{1,0:T(8,128)(2,1)S(1)} %add.4), channel_id=1, source_target_pairs={{0,4},{1,5},{2,6},{3,7},{4,0},{5,1},{6,2},{7,3},{8,12},{9,13},{10,... | collective-permute-start | bytes 1572872 | tf_op jit(solution)/shard_map/ppermute | solution.py:27

commit v2 on v1

--- a/solution.py
+++ b/solution.py
@@ -98,22 +98,41 @@
     )(*flat, *ws, *before)
 
 
-def split_kernel(up, down, first, second):
-    rows = first.shape[0]
-    first[...] = up[pl.ds(0, rows), :]
-    second[...] = down[pl.ds(rows, rows), :]
-
-
-def split(up, down):
-    shape = jax.ShapeDtypeStruct((up.shape[0] // 2, up.shape[1]), up.dtype)
-    return pl.pallas_call(
-        split_kernel,
-        out_shape=(shape, shape),
-        in_specs=[vmem()] * 2,
-        out_specs=(vmem(), vmem()),
+def half_of(x, second):
+    rows = x.shape[0] // 2
+
+    def body(x, out):
+        out[...] = x[pl.ds(rows if second else 0, rows), :]
+
+    return pl.pallas_call(
+        body,
+        out_shape=jax.ShapeDtypeStruct((rows, x.shape[1]), x.dtype),
+        in_specs=[vmem()],
+        out_specs=vmem(),
         compiler_params=limit(2),
-        name="split",
-    )(up, down)
+    )(x)
+
+
+def load_kernel(*refs):
+    n = len(refs) // 2
+    sems = refs[-1]
+    copies = [pltpu.make_async_copy(refs[k], refs[n + k], sems.at[k]) for k in range(n)]
+    for copy in copies:
+        copy.start()
+    for copy in copies:
+        copy.wait()
+
+
+def load(*arrays):
+    return pl.pallas_call(
+        load_kernel,
+        out_shape=tuple(jax.ShapeDtypeStruct(x.shape, x.dtype) for x in arrays),
+        in_specs=[pl.BlockSpec(memory_space=pltpu.HBM)] * len(arrays),
+        out_specs=(vmem(),) * len(arrays),
+        scratch_shapes=[pltpu.SemaphoreType.DMA((len(arrays),))],
+        compiler_params=limit(12),
+        name="load",
+    )(*arrays)
 
 
 def add_kernel(*refs):
@@ -297,9 +316,10 @@
 
     up, down = shift(tokens, 1), shift(tokens, -1)
     twin = swap(tokens)
-    halves = split(up, down)
-    far = [shift(halves[0], 1), shift(halves[1], -1)]
-    first = [[tokens], [twin], [up], [swap(up)], [down], [swap(down)]]
+    key_weight, value_weight, query_weight, mine = load(key_weight, value_weight, query_weight, tokens)
+    far_down = shift(half_of(down, True), -1)
+    far = [shift(half_of(up, False), 1), far_down]
+    first = [[mine], [twin], [up], [swap(up)], [down], [swap(down)]]
     second = [far, [swap(far[0]), swap(far[1])]]
 
     sums = lambda *cols: tuple(jax.ShapeDtypeStruct((rows, n), jnp.float32) for n in cols)
@@ -317,16 +337,17 @@
     for k in range(1, REACH + 1):
         below, above = ring(below, 1), ring(above, -1)
         pieces[k] = below, above
-    early = {k: pieces[k] for k in range(REACH)}
-    state = attend(table, q, 0, early, None, None)
-    whole = lambda which: attend(table, q, which, pieces, None, out_weight)
     merge = lambda pair: add(pair[0], swap(pair[1]))
 
-    pair = attend(table, q, 0, {REACH: pieces[REACH]}, state, out_weight)
-    across = shift(merge(pair), 2)
-    from_below = shift(merge(whole(1)), 1)
-    from_above = shift(merge(whole(2)), -1)
-    keep, give = whole(3)
+    def two_parts(which, cut):
+        parts = {k: pieces[k] for k in range(cut)}, {k: pieces[k] for k in range(cut, REACH + 1)}
+        state = attend(table, q, which, parts[0], None, None)
+        return attend(table, q, which, parts[1], state, out_weight)
+
+    across = shift(merge(two_parts(0, 4)), 2)
+    from_below = shift(merge(two_parts(1, 2)), 1)
+    from_above = shift(merge(two_parts(2, 3)), -1)
+    keep, give = attend(table, q, 3, pieces, None, out_weight)
     return add(keep, swap(give), across, from_below, from_above)
 
 

time: 138 us -> 141 us (1.022)
  Pallas kernels: 27.9 us -> 30.1 us
    pallas_call x5 -> x7, Pallas kernels: 19.1 us -> 20.8 us  [attend(): pl.pallas_call(lambda *refs: attend_kernel(*refs, which=which, steps=step...]
    unnamed x20 -> x16, local copies, waits for them, and re-layouts: 5.7 us -> 5.7 us
  transfers between devices with their start and end apart: 24 -> 24, of which waited for: 8 -> 8; matrix products, arithmetic and copies ran while one was open for 0% -> 0% of each run, Pallas kernels for 16% -> 19%
where the time goes in v2:
time: 141 us; the launch traced here: 138 us
  waiting for transfers between devices  53.6 us (38%)
  starting transfers between devices  48.3 us (34%)
  Pallas kernels  30.1 us (21%)
  local copies, waits for them, and re-layouts  5.7 us (4%)
    ppermute x7, waiting for transfers between devices, shift(): return lax.ppermute(x, 'tp', [(t, (t + 2 * chips) % 8) for t in range(8)])  42 us
    ppermute x8, starting transfers between devices, ring(): lax.ppermute(x, 'ctx', [(i, i + step) for i in range(n) if 0 <= i + step...  33.8 us
    pallas_call x7, Pallas kernels, attend(): pl.pallas_call(lambda *refs: attend_kernel(*refs, which=which, steps=step...  20.8 us
    ppermute x7, starting transfers between devices, shift(): return lax.ppermute(x, 'tp', [(t, (t + 2 * chips) % 8) for t in range(8)])  12.3 us
    ppermute x8, waiting for transfers between devices, ring(): lax.ppermute(x, 'ctx', [(i, i + step) for i in range(n) if 0 <= i + step...  11.5 us
    unnamed x16, local copies, waits for them, and re-layouts  5.7 us
    pallas_call x3, Pallas kernels, project(): pl.pallas_call(body, out_shape=out_shape, in_specs=[vmem()] * (len(flat)...  4.96 us
  transfers between devices with their start and end apart: 24, of which 8 were waited for; matrix products, arithmetic and copies ran while one was open for 0% of the time, Pallas kernels for 19%

profile of v2, /device:TPU:6, one launch (start us, length us, event | category | flops | bytes accessed | tf_op | source)
XLA Modules:
  0.0 138.1 jit_solution(6265168965937609787)
XLA Ops:
  0.0 1.6 %collective-permute-start = (bf16[512,512]{1,0:T(8,128)(2,1)}, bf16[512,512]{1,0:T(8,128)(2,1)S(1)}, u32[]{:S(2)}, u32[]{:S(2)}) collective-permute-start(bf16[512,512]{1,0:T(8,128)(2,1)} %refs_3_.1), channel_id=1, source_target_pairs={{0,2},{1,3},{2,4},{3,5},{4,6},{5,7},{6,0},{7,1},{8,10},{9,11},{10,... | collective-permute-start | bytes 1572872 | tf_op jit(solution)/shard_map/ppermute | solution.py:27
  1.6 1.7 %collective-permute-start.2 = (bf16[512,512]{1,0:T(8,128)(2,1)}, bf16[512,512]{1,0:T(8,128)(2,1)S(1)}, u32[]{:S(2)}, u32[]{:S(2)}) collective-permute-start(bf16[512,512]{1,0:T(8,128)(2,1)} %refs_3_.1), channel_id=1, source_target_pairs={{0,6},{1,7},{2,0},{3,1},{4,2},{5,3},{6,4},{7,5},{8,14},{9,15},{10,... | collective-permute-start | bytes 1572872 | tf_op jit(solution)/shard_map/ppermute | solution.py:27
  3.2 11.9 %collective-permute-done.x.refs_2_ = bf16[512,512]{1,0:T(8,128)(2,1)S(1)} collective-permute-done((bf16[512,512]{1,0:T(8,128)(2,1)}, bf16[512,512]{1,0:T(8,128)(2,1)S(1)}, u32[]{:S(2)}, u32[]{:S(2)}) %collective-permute-start) | collective-permute-done | bytes 524320 | tf_op jit(solution)/shard_map/ppermute | solution.py:27
  15.2 0.5 collective-permute-start.8
  15.7 1.2 collective-permute-start.1
  16.9 2.2 %collective-permute-start.3 = (bf16[256,512]{1,0:T(8,128)(2,1)S(1)}, bf16[256,512]{1,0:T(8,128)(2,1)S(1)}, u32[]{:S(2)}, u32[]{:S(2)}) collective-permute-start(bf16[256,512]{1,0:T(8,128)(2,1)S(1)} %shard_map.83), channel_id=1, source_target_pairs={{0,6},{1,7},{2,0},{3,1},{4,2},{5,3},{6,4},{7,5},{8,14},{9,15},{10,... | collective-permute-start | bytes 786440 | tf_op jit(solution)/shard_map/ppermute | solution.py:27
  19.1 6.1 %collective-permute-done.1.refs_0_ = bf16[256,512]{1,0:T(8,128)(2,1)S(1)} collective-permute-done((bf16[256,512]{1,0:T(8,128)(2,1)S(1)}, bf16[256,512]{1,0:T(8,128)(2,1)S(1)}, u32[]{:S(2)}, u32[]{:S(2)}) %collective-permute-start.1) | collective-permute-done | bytes 262176 | tf_op jit(solution)/shard_map/ppermute | solution.py:27
  25.2 0.2 collective-permute-done.3.refs_1_
  25.4 0.3 collective-permute-start.5
  25.7 2.2 %copy-done.1 = bf16[4096,512]{1,0:T(8,128)(2,1)S(1)} copy-done((bf16[4096,512]{1,0:T(8,128)(2,1)S(1)}, bf16[4096,512]{1,0:T(8,128)(2,1)}, u32[]{:S(2)}) %copy-start.1) | copy-done | bytes 4194328
  27.9 1.2 copy-done.2
  29.1 1.2 copy-done.3
  30.4 1.0 copy-done.4
  31.4 0.5 load.1
  32.0 3.4 %shard_map.84 = (f32[512,128]{1,0:T(8,128)S(1)}, f32[512,128]{1,0:T(8,128)S(1)}, f32[512,512]{1,0:T(8,128)S(1)}) custom-call(bf16[512,512]{1,0:T(8,128)(2,1)S(1)} %get-tuple-element.30.refs_0_, bf16[512,512]{1,0:T(8,128)(2,1)S(1)} %collective-permute-done.6.refs_1_, bf16[512,512]{1,0:T(8,128)(2,1)S(1)} %collective-permute-done.x.refs_2_, ...), custom_call_target="tpu_custom_call" | custom-call | flops 2415919104 | bytes 7864320 | tf_op jit(solution)/shard_map/pallas_call | solution.py:87
  35.4 0.8 shard_map.86.refs_2_
  36.2 3.8 %collective-permute-start.9 = (bf16[2,4,128,128]{3,2,1,0:T(8,128)(2,1)S(1)}, bf16[2,4,128,128]{3,2,1,0:T(8,128)(2,1)S(1)}, u32[]{:S(2)}, u32[]{:S(2)}) collective-permute-start(bf16[2,4,128,128]{3,2,1,0:T(8,128)(2,1)S(1)} %shard_map.86.refs_2_), channel_id=1, source_target_pairs={{0,8},{8,16},{16,24},{24,32},{32,40},{40,48},{48,56},{56,64},{64,7... | collective-permute-start | bytes 786440 | tf_op jit(solution)/shard_map/ppermute | solution.py:32
  40.1 6.1 %collective-permute-start.10 = (bf16[2,4,128,128]{3,2,1,0:T(8,128)(2,1)S(1)}, bf16[2,4,128,128]{3,2,1,0:T(8,128)(2,1)S(1)}, u32[]{:S(2)}, u32[]{:S(2)}) collective-permute-start(bf16[2,4,128,128]{3,2,1,0:T(8,128)(2,1)S(1)} %shard_map.86.refs_2_), channel_id=1, source_target_pairs={{8,0},{16,8},{24,16},{32,24},{40,32},{48,40},{56,48},{64,56},{72,6... | collective-permute-start | bytes 786440 | tf_op jit(solution)/shard_map/ppermute | solution.py:32
  46.2 4.7 %collective-permute-done.9.refs_3_ = bf16[2,4,128,128]{3,2,1,0:T(8,128)(2,1)S(1)} collective-permute-done((bf16[2,4,128,128]{3,2,1,0:T(8,128)(2,1)S(1)}, bf16[2,4,128,128]{3,2,1,0:T(8,128)(2,1)S(1)}, u32[]{:S(2)}, u32[]{:S(2)}) %collective-permute-start.9) | collective-permute-done | bytes 262176 | tf_op jit(solution)/shard_map/ppermute | solution.py:32
  50.9 1.9 %collective-permute-start.11 = (bf16[2,4,128,128]{3,2,1,0:T(8,128)(2,1)S(1)}, bf16[2,4,128,128]{3,2,1,0:T(8,128)(2,1)S(1)}, u32[]{:S(2)}, u32[]{:S(2)}) collective-permute-start(bf16[2,4,128,128]{3,2,1,0:T(8,128)(2,1)S(1)} %collective-permute-done.9.refs_3_), channel_id=1, source_target_pairs={{0,8},{8,16},{16,24},{24,32},{32,40},{40,48},{48,56},{56,64},{64,7... | collective-permute-start | bytes 786440 | tf_op jit(solution)/shard_map/ppermute | solution.py:32
  52.8 6.0 %collective-permute-start.12 = (bf16[2,4,128,128]{3,2,1,0:T(8,128)(2,1)S(1)}, bf16[2,4,128,128]{3,2,1,0:T(8,128)(2,1)S(1)}, u32[]{:S(2)}, u32[]{:S(2)}) collective-permute-start(bf16[2,4,128,128]{3,2,1,0:T(8,128)(2,1)S(1)} %collective-permute-done.10.refs_4_), channel_id=1, source_target_pairs={{8,0},{16,8},{24,16},{32,24},{40,32},{48,40},{56,48},{64,56},{72,6... | collective-permute-start | bytes 786440 | tf_op jit(solution)/shard_map/ppermute | solution.py:32
  58.9 3.8 %collective-permute-done.11.refs_5_.refs_2_ = bf16[2,4,128,128]{3,2,1,0:T(8,128)(2,1)S(1)} collective-permute-done((bf16[2,4,128,128]{3,2,1,0:T(8,128)(2,1)S(1)}, bf16[2,4,128,128]{3,2,1,0:T(8,128)(2,1)S(1)}, u32[]{:S(2)}, u32[]{:S(2)}) %collective-permute-start.11) | collective-permute-done | bytes 262176 | tf_op jit(solution)/shard_map/ppermute | solution.py:32
  62.7 1.9 %collective-permute-start.13 = (bf16[2,4,128,128]{3,2,1,0:T(8,128)(2,1)S(1)}, bf16[2,4,128,128]{3,2,1,0:T(8,128)(2,1)S(1)}, u32[]{:S(2)}, u32[]{:S(2)}) collective-permute-start(bf16[2,4,128,128]{3,2,1,0:T(8,128)(2,1)S(1)} %collective-permute-done.11.refs_5_.refs_2_), channel_id=1, source_target_pairs={{0,8},{8,16},{16,24},{24,32},{32,40},{40,48},{48,56},{56,64},{64,7... | collective-permute-start | bytes 786440 | tf_op jit(solution)/shard_map/ppermute | solution.py:32
  64.6 6.0 %collective-permute-start.14 = (bf16[2,4,128,128]{3,2,1,0:T(8,128)(2,1)S(1)}, bf16[2,4,128,128]{3,2,1,0:T(8,128)(2,1)S(1)}, u32[]{:S(2)}, u32[]{:S(2)}) collective-permute-start(bf16[2,4,128,128]{3,2,1,0:T(8,128)(2,1)S(1)} %collective-permute-done.12.refs_6_.refs_3_), channel_id=1, source_target_pairs={{8,0},{16,8},{24,16},{32,24},{40,32},{48,40},{56,48},{64,56},{72,6... | collective-permute-start | bytes 786440 | tf_op jit(solution)/shard_map/ppermute | solution.py:32
  70.7 3.0 %collective-permute-done.13.refs_7_.refs_4_.refs_2_ = bf16[2,4,128,128]{3,2,1,0:T(8,128)(2,1)S(1)} collective-permute-done((bf16[2,4,128,128]{3,2,1,0:T(8,128)(2,1)S(1)}, bf16[2,4,128,128]{3,2,1,0:T(8,128)(2,1)S(1)}, u32[]{:S(2)}, u32[]{:S(2)}) %collective-permute-start.13) | collective-permute-done | bytes 262176 | tf_op jit(solution)/shard_map/ppermute | solution.py:32
  73.7 1.9 %collective-permute-start.15 = (bf16[2,4,128,128]{3,2,1,0:T(8,128)(2,1)S(1)}, bf16[2,4,128,128]{3,2,1,0:T(8,128)(2,1)S(1)}, u32[]{:S(2)}, u32[]{:S(2)}) collective-permute-start(bf16[2,4,128,128]{3,2,1,0:T(8,128)(2,1)S(1)} %collective-permute-done.13.refs_7_.refs_4_.refs_2_), channel_id=1, source_target_pairs={{0,8},{8,16},{16,24},{24,32},{32,40},{40,48},{48,56},{56,64},{64,7... | collective-permute-start | bytes 786440 | tf_op jit(solution)/shard_map/ppermute | solution.py:32
  75.6 6.0 %collective-permute-start.16 = (bf16[2,4,128,128]{3,2,1,0:T(8,128)(2,1)S(1)}, bf16[2,4,128,128]{3,2,1,0:T(8,128)(2,1)S(1)}, u32[]{:S(2)}, u32[]{:S(2)}) collective-permute-start(bf16[2,4,128,128]{3,2,1,0:T(8,128)(2,1)S(1)} %collective-permute-done.14.refs_8_.refs_5_.refs_3_), channel_id=1, source_target_pairs={{8,0},{16,8},{24,16},{32,24},{40,32},{48,40},{56,48},{64,56},{72,6... | collective-permute-start | bytes 786440 | tf_op jit(solution)/shard_map/ppermute | solution.py:32
  81.7 2.3 %list_slots.1.refs_0_ = s32[20,18]{1,0:T(8,128)S(1)} custom-call(s32[4,16]{1,0:T(4,128)S(1)} %copy-done.5, s32[4]{0:T(128)S(1)} %copy-done.6, s32[128]{0:T(128)S(1)} %copy-done.7), custom_call_target="tpu_custom_call" | custom-call | tf_op jit(solution)/shard_map/list_slots/pallas_call | solution.py:227
  84.0 0.7 shard_map.85.refs_1_
  84.8 2.8 %shard_map.90 = (f32[512,128]{1,0:T(8,128)S(1)}, f32[512,128]{1,0:T(8,128)S(1)}, f32[512,128]{1,0:T(8,128)S(1)}) custom-call(s32[20,18]{1,0:T(8,128)S(1)} %list_slots.1.refs_0_, bf16[4,512,128]{2,1,0:T(8,128)(2,1)S(1)} %shard_map.85.refs_1_, bf16[2,4,128,128]{3,2,1,0:T(8,128)(2,1)S(1)} %shard_map.86.refs_2_, ...), custom_call_target="tpu_custom_call" | custom-call | flops 536870912 | bytes 4194304 | tf_op jit(solution)/shard_map/pallas_call | solution.py:298
  87.6 2.7 %shard_map.92 = (f32[512,128]{1,0:T(8,128)S(1)}, f32[512,128]{1,0:T(8,128)S(1)}, f32[512,128]{1,0:T(8,128)S(1)}) custom-call(s32[20,18]{1,0:T(8,128)S(1)} %list_slots.1.refs_0_, bf16[4,512,128]{2,1,0:T(8,128)(2,1)S(1)} %shard_map.85.refs_1_, bf16[2,4,128,128]{3,2,1,0:T(8,128)(2,1)S(1)} %shard_map.86.refs_2_, ...), custom_call_target="tpu_custom_call" | custom-call | flops 536870912 | bytes 4194304 | tf_op jit(solution)/shard_map/pallas_call | solution.py:298
  90.3 3.2 %shard_map.88 = (f32[512,128]{1,0:T(8,128)S(1)}, f32[512,128]{1,0:T(8,128)S(1)}, f32[512,128]{1,0:T(8,128)S(1)}) custom-call(s32[20,18]{1,0:T(8,128)S(1)} %list_slots.1.refs_0_, bf16[4,512,128]{2,1,0:T(8,128)(2,1)S(1)} %shard_map.85.refs_1_, bf16[2,4,128,128]{3,2,1,0:T(8,128)(2,1)S(1)} %shard_map.86.refs_2_, ...), custom_call_target="tpu_custom_call" | custom-call | flops 536870912 | bytes 4194304 | tf_op jit(solution)/shard_map/pallas_call | solution.py:298
  93.5 2.1 %shard_map.93 = (bf16[64,4096]{1,0:T(8,128)(2,1)S(1)}, bf16[64,4096]{1,0:T(8,128)(2,1)S(1)}) custom-call(s32[20,18]{1,0:T(8,128)S(1)} %list_slots.1.refs_0_, bf16[4,512,128]{2,1,0:T(8,128)(2,1)S(1)} %shard_map.85.refs_1_, bf16[2,4,128,128]{3,2,1,0:T(8,128)(2,1)S(1)} %collective-permute-done.13.refs_7_.refs_4_.refs_2_, ...), custom_call_target="tpu_custom_call" | custom-call | flops 536870912 | bytes 4194304 | tf_op jit(solution)/shard_map/pallas_call | solution.py:298
  95.7 0.1 collective-permute-start.22
  95.8 3.2 %shard_map.91 = (bf16[64,4096]{1,0:T(8,128)(2,1)S(1)}, bf16[64,4096]{1,0:T(8,128)(2,1)S(1)}) custom-call(s32[20,18]{1,0:T(8,128)S(1)} %list_slots.1.refs_0_, bf16[4,512,128]{2,1,0:T(8,128)(2,1)S(1)} %shard_map.85.refs_1_, bf16[2,4,128,128]{3,2,1,0:T(8,128)(2,1)S(1)} %collective-permute-done.11.refs_5_.refs_2_, ...), custom_call_target="tpu_custom_call" | custom-call | flops 536870912 | bytes 4194304 | tf_op jit(solution)/shard_map/pallas_call | solution.py:298
  98.9 0.6 collective-permute-start.20
  99.5 1.6 %shard_map.89 = (bf16[64,4096]{1,0:T(8,128)(2,1)S(1)}, bf16[64,4096]{1,0:T(8,128)(2,1)S(1)}) custom-call(s32[20,18]{1,0:T(8,128)S(1)} %list_slots.1.refs_0_, bf16[4,512,128]{2,1,0:T(8,128)(2,1)S(1)} %shard_map.85.refs_1_, bf16[2,4,128,128]{3,2,1,0:T(8,128)(2,1)S(1)} %collective-permute-done.15.refs_9_.refs_2_.refs_6_.refs_4_, ...), custom_call_target="tpu_custom_call" | custom-call | flops 536870912 | bytes 4194304 | tf_op jit(solution)/shard_map/pallas_call | solution.py:298
  101.1 0.1 collective-permute-start.18
  101.2 5.2 %shard_map.87 = (bf16[64,4096]{1,0:T(8,128)(2,1)S(1)}, bf16[64,4096]{1,0:T(8,128)(2,1)S(1)}) custom-call(s32[20,18]{1,0:T(8,128)S(1)} %list_slots.1.refs_0_, bf16[4,512,128]{2,1,0:T(8,128)(2,1)S(1)} %shard_map.85.refs_1_, bf16[2,4,128,128]{3,2,1,0:T(8,128)(2,1)S(1)} %shard_map.86.refs_2_, bf16[2,4,128,128]{3,2,1,0:T(8,128)(2,1)S(1)} %collective-permute-done.9.refs_3_, ...), custom_call_target="tpu_custom_call" | custom-call | flops 536870912 | bytes 4194304 | tf_op jit(solution)/shard_map/pallas_call | solution.py:298
  106.5 0.6 collective-permute-start.17
  107.1 0.1 add.6
  107.2 3.6 %collective-permute-start.23 = (bf16[64,4096]{1,0:T(8,128)(2,1)S(1)}, bf16[64,4096]{1,0:T(8,128)(2,1)S(1)}, u32[]{:S(2)}, u32[]{:S(2)}) collective-permute-start(bf16[64,4096]{1,0:T(8,128)(2,1)S(1)} %add.6), channel_id=1, source_target_pairs={{0,6},{1,7},{2,0},{3,1},{4,2},{5,3},{6,4},{7,5},{8,14},{9,15},{10,... | collective-permute-start | bytes 1572872 | tf_op jit(solution)/shard_map/ppermute | solution.py:27
  110.8 0.1 add.5
  111.0 0.1 add.4
  111.1 2.0 %collective-permute-start.19 = (bf16[64,4096]{1,0:T(8,128)(2,1)S(1)}, bf16[64,4096]{1,0:T(8,128)(2,1)S(1)}, u32[]{:S(2)}, u32[]{:S(2)}) collective-permute-start(bf16[64,4096]{1,0:T(8,128)(2,1)S(1)} %add.4), channel_id=1, source_target_pairs={{0,4},{1,5},{2,6},{3,7},{4,0},{5,1},{6,2},{7,3},{8,12},{9,13},{10,... | collective-permute-start | bytes 1572872 | tf_op jit(solution)/shard_map/ppermute | solution.py:27
  113.2 20.2 %collective-permute-done.23.refs_4_ = bf16[64,4096]{1,0:T(8,128)(2,1)S(1)} collective-permute-done((bf16[64,4096]{1,0:T(8,128)(2,1)S(1)}, bf16[64,4096]{1,0:T(8,128)(2,1)S(1)}, u32[]{:S(2)}, u32[]{:S(2)}) %collective-permute-start.23) | collective-permute-done | bytes 524320 | tf_op jit(solution)/shard_map/ppermute | solution.py:27
  133.4 3.6 %collective-permute-done.21.refs_3_ = bf16[64,4096]{1,0:T(8,128)(2,1)S(1)} collective-permute-done((bf16[64,4096]{1,0:T(8,128)(2,1)S(1)}, bf16[64,4096]{1,0:T(8,128)(2,1)S(1)}, u32[]{:S(2)}, u32[]{:S(2)}) %collective-permute-start.21) | collective-permute-done | bytes 524320 | tf_op jit(solution)/shard_map/ppermute | solution.py:27
  137.0 1.1 add.7
  (34 shorter events, 0.2 us)
Async XLA Ops:
  0.0 15.1 %collective-permute-start = (bf16[512,512]{1,0:T(8,128)(2,1)}, bf16[512,512]{1,0:T(8,128)(2,1)S(1)}, u32[]{:S(2)}, u32[]{:S(2)}) collective-permute-start(bf16[512,512]{1,0:T(8,128)(2,1)} %refs_3_.1), channel_id=1, source_target_pairs={{0,2},{1,3},{2,4},{3,5},{4,6},{5,7},{6,0},{7,1},{8,10},{9,11},{10,... | collective-permute-start | bytes 1572872 | tf_op jit(solution)/shard_map/ppermute | solution.py:27
  1.6 13.6 %collective-permute-start.2 = (bf16[512,512]{1,0:T(8,128)(2,1)}, bf16[512,512]{1,0:T(8,128)(2,1)S(1)}, u32[]{:S(2)}, u32[]{:S(2)}) collective-permute-start(bf16[512,512]{1,0:T(8,128)(2,1)} %refs_3_.1), channel_id=1, source_target_pairs={{0,6},{1,7},{2,0},{3,1},{4,2},{5,3},{6,4},{7,5},{8,14},{9,15},{10,... | collective-permute-start | bytes 1572872 | tf_op jit(solution)/shard_map/ppermute | solution.py:27
  3.2 28.7 %collective-permute-start.6 = (bf16[512,512]{1,0:T(8,128)(2,1)}, bf16[512,512]{1,0:T(8,128)(2,1)S(1)}, u32[]{:S(2)}, u32[]{:S(2)}) collective-permute-start(bf16[512,512]{1,0:T(8,128)(2,1)} %refs_3_.1), channel_id=1, source_target_pairs={{0,1},{1,0},{2,3},{3,2},{4,5},{5,4},{6,7},{7,6},{8,9},{9,8},{10,11... | collective-permute-start | bytes 1572872 | tf_op jit(solution)/shard_map/ppermute | solution.py:23
  15.1 16.8 %collective-permute-start.7 = (bf16[512,512]{1,0:T(8,128)(2,1)S(1)}, bf16[512,512]{1,0:T(8,128)(2,1)S(1)}, u32[]{:S(2)}, u32[]{:S(2)}) collective-permute-start(bf16[512,512]{1,0:T(8,128)(2,1)S(1)} %collective-permute-done.x.refs_2_), channel_id=1, source_target_pairs={{0,1},{1,0},{2,3},{3,2},{4,5},{5,4},{6,7},{7,6},{8,9},{9,8},{10,11... | collective-permute-start | bytes 1572872 | tf_op jit(solution)/shard_map/ppermute | solution.py:23
  15.2 16.8 %collective-permute-start.8 = (bf16[512,512]{1,0:T(8,128)(2,1)S(1)}, bf16[512,512]{1,0:T(8,128)(2,1)S(1)}, u32[]{:S(2)}, u32[]{:S(2)}) collective-permute-start(bf16[512,512]{1,0:T(8,128)(2,1)S(1)} %collective-permute-done.2.x.refs_4_), channel_id=1, source_target_pairs={{0,1},{1,0},{2,3},{3,2},{4,5},{5,4},{6,7},{7,6},{8,9},{9,8},{10,11... | collective-permute-start | bytes 1572872 | tf_op jit(solution)/shard_map/ppermute | solution.py:23
  15.7 9.5 %collective-permute-start.1 = (bf16[256,512]{1,0:T(8,128)(2,1)S(1)}, bf16[256,512]{1,0:T(8,128)(2,1)S(1)}, u32[]{:S(2)}, u32[]{:S(2)}) collective-permute-start(bf16[256,512]{1,0:T(8,128)(2,1)S(1)} %shard_map.82), channel_id=1, source_target_pairs={{0,2},{1,3},{2,4},{3,5},{4,6},{5,7},{6,0},{7,1},{8,10},{9,11},{10,... | collective-permute-start | bytes 786440 | tf_op jit(solution)/shard_map/ppermute | solution.py:27
  16.9 8.5 %collective-permute-start.3 = (bf16[256,512]{1,0:T(8,128)(2,1)S(1)}, bf16[256,512]{1,0:T(8,128)(2,1)S(1)}, u32[]{:S(2)}, u32[]{:S(2)}) collective-permute-start(bf16[256,512]{1,0:T(8,128)(2,1)S(1)} %shard_map.83), channel_id=1, source_target_pairs={{0,6},{1,7},{2,0},{3,1},{4,2},{5,3},{6,4},{7,5},{8,14},{9,15},{10,... | collective-permute-start | bytes 786440 | tf_op jit(solution)/shard_map/ppermute | solution.py:27
  25.2 10.2 %collective-permute-start.4 = (bf16[256,512]{1,0:T(8,128)(2,1)S(1)}, bf16[256,512]{1,0:T(8,128)(2,1)S(1)}, u32[]{:S(2)}, u32[]{:S(2)}) collective-permute-start(bf16[256,512]{1,0:T(8,128)(2,1)S(1)} %collective-permute-done.1.refs_0_), channel_id=1, source_target_pairs={{0,1},{1,0},{2,3},{3,2},{4,5},{5,4},{6,7},{7,6},{8,9},{9,8},{10,11... | collective-permute-start | bytes 786440 | tf_op jit(solution)/shard_map/ppermute | solution.py:23
  25.4 10.0 %collective-permute-start.5 = (bf16[256,512]{1,0:T(8,128)(2,1)S(1)}, bf16[256,512]{1,0:T(8,128)(2,1)S(1)}, u32[]{:S(2)}, u32[]{:S(2)}) collective-permute-start(bf16[256,512]{1,0:T(8,128)(2,1)S(1)} %collective-permute-done.3.refs_1_), channel_id=1, source_target_pairs={{0,1},{1,0},{2,3},{3,2},{4,5},{5,4},{6,7},{7,6},{8,9},{9,8},{10,11... | collective-permute-start | bytes 786440 | tf_op jit(solution)/shard_map/ppermute | solution.py:23
  25.7 2.2 %copy-start.1 = (bf16[4096,512]{1,0:T(8,128)(2,1)S(1)}, bf16[4096,512]{1,0:T(8,128)(2,1)}, u32[]{:S(2)}) copy-start(bf16[4096,512]{1,0:T(8,128)(2,1)} %refs_2_.1) | copy-start | bytes 12582916
  27.9 1.2 copy-start.2
  29.1 1.2 copy-start.3
  30.4 1.0 copy-start.4
  31.9 49.7 %copy-start.5 = (s32[4,16]{1,0:T(4,128)S(1)}, s32[4,16]{1,0:T(4,128)}, u32[]{:S(2)}) copy-start(s32[4,16]{1,0:T(4,128)} %links.1) | copy-start | bytes 772
  31.9 49.7 %copy-start.6 = (s32[4]{0:T(128)S(1)}, s32[4]{0:T(128)}, u32[]{:S(2)}) copy-start(s32[4]{0:T(128)} %counts.1) | copy-start | bytes 52
  32.0 49.7 %copy-start.7 = (s32[128]{0:T(128)S(1)}, s32[128]{0:T(128)}, u32[]{:S(2)}) copy-start(s32[128]{0:T(128)} %docs.1) | copy-start | bytes 1540
  36.2 14.7 %collective-permute-start.9 = (bf16[2,4,128,128]{3,2,1,0:T(8,128)(2,1)S(1)}, bf16[2,4,128,128]{3,2,1,0:T(8,128)(2,1)S(1)}, u32[]{:S(2)}, u32[]{:S(2)}) collective-permute-start(bf16[2,4,128,128]{3,2,1,0:T(8,128)(2,1)S(1)} %shard_map.86.refs_2_), channel_id=1, source_target_pairs={{0,8},{8,16},{16,24},{24,32},{32,40},{40,48},{48,56},{56,64},{64,7... | collective-permute-start | bytes 786440 | tf_op jit(solution)/shard_map/ppermute | solution.py:32
  40.1 12.8 %collective-permute-start.10 = (bf16[2,4,128,128]{3,2,1,0:T(8,128)(2,1)S(1)}, bf16[2,4,128,128]{3,2,1,0:T(8,128)(2,1)S(1)}, u32[]{:S(2)}, u32[]{:S(2)}) collective-permute-start(bf16[2,4,128,128]{3,2,1,0:T(8,128)(2,1)S(1)} %shard_map.86.refs_2_), channel_id=1, source_target_pairs={{8,0},{16,8},{24,16},{32,24},{40,32},{48,40},{56,48},{64,56},{72,6... | collective-permute-start | bytes 786440 | tf_op jit(solution)/shard_map/ppermute | solution.py:32
  50.9 11.8 %collective-permute-start.11 = (bf16[2,4,128,128]{3,2,1,0:T(8,128)(2,1)S(1)}, bf16[2,4,128,128]{3,2,1,0:T(8,128)(2,1)S(1)}, u32[]{:S(2)}, u32[]{:S(2)}) collective-permute-start(bf16[2,4,128,128]{3,2,1,0:T(8,128)(2,1)S(1)} %collective-permute-done.9.refs_3_), channel_id=1, source_target_pairs={{0,8},{8,16},{16,24},{24,32},{32,40},{40,48},{48,56},{56,64},{64,7... | collective-permute-start | bytes 786440 | tf_op jit(solution)/shard_map/ppermute | solution.py:32
  52.8 11.8 %collective-permute-start.12 = (bf16[2,4,128,128]{3,2,1,0:T(8,128)(2,1)S(1)}, bf16[2,4,128,128]{3,2,1,0:T(8,128)(2,1)S(1)}, u32[]{:S(2)}, u32[]{:S(2)}) collective-permute-start(bf16[2,4,128,128]{3,2,1,0:T(8,128)(2,1)S(1)} %collective-permute-done.10.refs_4_), channel_id=1, source_target_pairs={{8,0},{16,8},{24,16},{32,24},{40,32},{48,40},{56,48},{64,56},{72,6... | collective-permute-start | bytes 786440 | tf_op jit(solution)/shard_map/ppermute | solution.py:32
  62.7 11.0 %collective-permute-start.13 = (bf16[2,4,128,128]{3,2,1,0:T(8,128)(2,1)S(1)}, bf16[2,4,128,128]{3,2,1,0:T(8,128)(2,1)S(1)}, u32[]{:S(2)}, u32[]{:S(2)}) collective-permute-start(bf16[2,4,128,128]{3,2,1,0:T(8,128)(2,1)S(1)} %collective-permute-done.11.refs_5_.refs_2_), channel_id=1, source_target_pairs={{0,8},{8,16},{16,24},{24,32},{32,40},{40,48},{48,56},{56,64},{64,7... | collective-permute-start | bytes 786440 | tf_op jit(solution)/shard_map/ppermute | solution.py:32
  64.6 10.9 %collective-permute-start.14 = (bf16[2,4,128,128]{3,2,1,0:T(8,128)(2,1)S(1)}, bf16[2,4,128,128]{3,2,1,0:T(8,128)(2,1)S(1)}, u32[]{:S(2)}, u32[]{:S(2)}) collective-permute-start(bf16[2,4,128,128]{3,2,1,0:T(8,128)(2,1)S(1)} %collective-permute-done.12.refs_6_.refs_3_), channel_id=1, source_target_pairs={{8,0},{16,8},{24,16},{32,24},{40,32},{48,40},{56,48},{64,56},{72,6... | collective-permute-start | bytes 786440 | tf_op jit(solution)/shard_map/ppermute | solution.py:32
  73.7 19.8 %collective-permute-start.15 = (bf16[2,4,128,128]{3,2,1,0:T(8,128)(2,1)S(1)}, bf16[2,4,128,128]{3,2,1,0:T(8,128)(2,1)S(1)}, u32[]{:S(2)}, u32[]{:S(2)}) collective-permute-start(bf16[2,4,128,128]{3,2,1,0:T(8,128)(2,1)S(1)} %collective-permute-done.13.refs_7_.refs_4_.refs_2_), channel_id=1, source_target_pairs={{0,8},{8,16},{16,24},{24,32},{32,40},{40,48},{48,56},{56,64},{64,7... | collective-permute-start | bytes 786440 | tf_op jit(solution)/shard_map/ppermute | solution.py:32
  75.6 17.9 %collective-permute-start.16 = (bf16[2,4,128,128]{3,2,1,0:T(8,128)(2,1)S(1)}, bf16[2,4,128,128]{3,2,1,0:T(8,128)(2,1)S(1)}, u32[]{:S(2)}, u32[]{:S(2)}) collective-permute-start(bf16[2,4,128,128]{3,2,1,0:T(8,128)(2,1)S(1)} %collective-permute-done.14.refs_8_.refs_5_.refs_3_), channel_id=1, source_target_pairs={{8,0},{16,8},{24,16},{32,24},{40,32},{48,40},{56,48},{64,56},{72,6... | collective-permute-start | bytes 786440 | tf_op jit(solution)/shard_map/ppermute | solution.py:32
  84.7 8.8 %copy-start = (bf16[512,4096]{1,0:T(8,128)(2,1)S(1)}, bf16[512,4096]{1,0:T(8,128)(2,1)}, u32[]{:S(2)}) copy-start(bf16[512,4096]{1,0:T(8,128)(2,1)} %refs_9_.1) | copy-start | bytes 12582916
  95.7 11.4 %collective-permute-start.22 = (bf16[64,4096]{1,0:T(8,128)(2,1)S(1)}, bf16[64,4096]{1,0:T(8,128)(2,1)S(1)}, u32[]{:S(2)}, u32[]{:S(2)}) collective-permute-start(bf16[64,4096]{1,0:T(8,128)(2,1)S(1)} %get-tuple-element.52), channel_id=1, source_target_pairs={{0,1},{1,0},{2,3},{3,2},{4,5},{5,4},{6,7},{7,6},{8,9},{9,8},{10,11... | collective-permute-start | bytes 1572872 | tf_op jit(solution)/shard_map/ppermute | solution.py:23
  98.9 11.9 %collective-permute-start.20 = (bf16[64,4096]{1,0:T(8,128)(2,1)S(1)}, bf16[64,4096]{1,0:T(8,128)(2,1)S(1)}, u32[]{:S(2)}, u32[]{:S(2)}) collective-permute-start(bf16[64,4096]{1,0:T(8,128)(2,1)S(1)} %get-tuple-element.47), channel_id=1, source_target_pairs={{0,1},{1,0},{2,3},{3,2},{4,5},{5,4},{6,7},{7,6},{8,9},{9,8},{10,11... | collective-permute-start | bytes 1572872 | tf_op jit(solution)/shard_map/ppermute | solution.py:23
  101.1 9.9 %collective-permute-start.18 = (bf16[64,4096]{1,0:T(8,128)(2,1)S(1)}, bf16[64,4096]{1,0:T(8,128)(2,1)S(1)}, u32[]{:S(2)}, u32[]{:S(2)}) collective-permute-start(bf16[64,4096]{1,0:T(8,128)(2,1)S(1)} %get-tuple-element.42), channel_id=1, source_target_pairs={{0,1},{1,0},{2,3},{3,2},{4,5},{5,4},{6,7},{7,6},{8,9},{9,8},{10,11... | collective-permute-start | bytes 1572872 | tf_op jit(solution)/shard_map/ppermute | solution.py:23
  106.5 6.7 %collective-permute-start.17 = (bf16[64,4096]{1,0:T(8,128)(2,1)S(1)}, bf16[64,4096]{1,0:T(8,128)(2,1)S(1)}, u32[]{:S(2)}, u32[]{:S(2)}) collective-permute-start(bf16[64,4096]{1,0:T(8,128)(2,1)S(1)} %get-tuple-element.37), channel_id=1, source_target_pairs={{0,1},{1,0},{2,3},{3,2},{4,5},{5,4},{6,7},{7,6},{8,9},{9,8},{10,11... | collective-permute-start | bytes 1572872 | tf_op jit(solution)/shard_map/ppermute | solution.py:23
  107.2 26.2 %collective-permute-start.23 = (bf16[64,4096]{1,0:T(8,128)(2,1)S(1)}, bf16[64,4096]{1,0:T(8,128)(2,1)S(1)}, u32[]{:S(2)}, u32[]{:S(2)}) collective-permute-start(bf16[64,4096]{1,0:T(8,128)(2,1)S(1)} %add.6), channel_id=1, source_target_pairs={{0,6},{1,7},{2,0},{3,1},{4,2},{5,3},{6,4},{7,5},{8,14},{9,15},{10,... | collective-permute-start | bytes 1572872 | tf_op jit(solution)/shard_map/ppermute | solution.py:27
  110.9 26.1 %collective-permute-start.21 = (bf16[64,4096]{1,0:T(8,128)(2,1)S(1)}, bf16[64,4096]{1,0:T(8,128)(2,1)S(1)}, u32[]{:S(2)}, u32[]{:S(2)}) collective-permute-start(bf16[64,4096]{1,0:T(8,128)(2,1)S(1)} %add.5), channel_id=1, source_target_pairs={{0,2},{1,3},{2,4},{3,5},{4,6},{5,7},{6,0},{7,1},{8,10},{9,11},{10,... | collective-permute-start | bytes 1572872 | tf_op jit(solution)/shard_map/ppermute | solution.py:27
  111.1 25.9 %collective-permute-start.19 = (bf16[64,4096]{1,0:T(8,128)(2,1)S(1)}, bf16[64,4096]{1,0:T(8,128)(2,1)S(1)}, u32[]{:S(2)}, u32[]{:S(2)}) collective-permute-start(bf16[64,4096]{1,0:T(8,128)(2,1)S(1)} %add.4), channel_id=1, source_target_pairs={{0,4},{1,5},{2,6},{3,7},{4,0},{5,1},{6,2},{7,3},{8,12},{9,13},{10,... | collective-permute-start | bytes 1572872 | tf_op jit(solution)/shard_map/ppermute | solution.py:27

commit v3 on v2

--- a/solution.py
+++ b/solution.py
@@ -23,13 +23,15 @@
     return lax.ppermute(x, "tp", SWAP)
 
 
-def shift(x, chips):
-    return lax.ppermute(x, "tp", [(t, (t + 2 * chips) % 8) for t in range(8)])
-
-
-def ring(x, step):
-    n = lax.axis_size("ctx")
-    return lax.ppermute(x, "ctx", [(i, i + step) for i in range(n) if 0 <= i + step < n])
+def across_y(x, mask):
+    return lax.ppermute(x, "tp", [(t, t ^ (2 * mask)) for t in range(8)])
+
+
+def exchange(x, first):
+    route = []
+    for c in range(first, lax.axis_size("ctx") - 1, 2):
+        route += [(c, c + 1), (c + 1, c)]
+    return lax.ppermute(x, "ctx", route)
 
 
 def smem():
@@ -51,7 +53,7 @@
 
 def destination(which):
     chip, core = chip_and_core()
-    return (chip + (2, 1, 3, 0)[which]) % 4, core
+    return chip ^ (2, 1, 3, 0)[which], core
 
 
 def project_kernel(*refs, counts, weights, added, finish, chips):
@@ -66,7 +68,7 @@
     for n, parts in enumerate(xs):
         x = parts[0][...] if len(parts) == 1 else jnp.concatenate([p[...] for p in parts], axis=0)
         width = x.shape[1]
-        source = 2 * ((chip + chips[n // 2]) % 4) + (core if n % 2 == 0 else 1 - core)
+        source = 2 * (chip ^ chips[n // 2]) + (core if n % 2 == 0 else 1 - core)
         first = pl.multiple_of(source * width, width)
         for k, w in enumerate(ws):
             part = jnp.dot(x, w[pl.ds(first, width), :], preferred_element_type=jnp.float32)
@@ -217,7 +219,7 @@
             line = jnp.abs(away) * 4 + b
             at = table[line, 0]
             ok = (s < live) & ((j < i) | (docs[j] != mine))
-            table[line, 1 + at] = jnp.where(away > 0, 4, 0) + j % 4
+            table[line, 1 + at] = jnp.where((away > 0) == (ctx % 2 == 1), 4, 0) + j % 4
             table[line, 0] = at + ok.astype(jnp.int32)
     for line in range(5 * 4):
         table[line, 1 + table[line, 0]] = 0
@@ -314,18 +316,19 @@
     rows = tokens.shape[0]
     table = list_slots(links, counts, doc_ids)
 
-    up, down = shift(tokens, 1), shift(tokens, -1)
+    up, down = across_y(tokens, 1), across_y(tokens, 3)
     twin = swap(tokens)
     key_weight, value_weight, query_weight, mine = load(key_weight, value_weight, query_weight, tokens)
-    far_down = shift(half_of(down, True), -1)
-    far = [shift(half_of(up, False), 1), far_down]
+    far_up = across_y(half_of(down, True), 1)
+    far_down = across_y(half_of(up, False), 3)
+    far = [far_down, far_up]
     first = [[mine], [twin], [up], [swap(up)], [down], [swap(down)]]
-    second = [far, [swap(far[0]), swap(far[1])]]
+    second = [far, [swap(far_down), swap(far_up)]]
 
     sums = lambda *cols: tuple(jax.ShapeDtypeStruct((rows, n), jnp.float32) for n in cols)
     kv_weights = [key_weight, value_weight]
     *kv_sums, q_sums = project(
-        (0, 3, 1), first, kv_weights + [query_weight], [], sums(128, 128, 512), keep_sums
+        (0, 1, 3), first, kv_weights + [query_weight], [], sums(128, 128, 512), keep_sums
     )
     kv_shape = (jax.ShapeDtypeStruct((2, rows // BLOCK, BLOCK, HEAD_DIM), jnp.bfloat16),)
     kv = project((2,), second, kv_weights, kv_sums, kv_shape, store_kv)[0]
@@ -333,10 +336,10 @@
     q = project((2,), second, [query_weight], [q_sums], q_shape, store_q)[0]
 
     pieces = {0: (kv,)}
-    below = above = kv
+    even = odd = kv
     for k in range(1, REACH + 1):
-        below, above = ring(below, 1), ring(above, -1)
-        pieces[k] = below, above
+        even, odd = exchange(odd, 0), exchange(even, 1)
+        pieces[k] = even, odd
     merge = lambda pair: add(pair[0], swap(pair[1]))
 
     def two_parts(which, cut):
@@ -344,9 +347,9 @@
         state = attend(table, q, which, parts[0], None, None)
         return attend(table, q, which, parts[1], state, out_weight)
 
-    across = shift(merge(two_parts(0, 4)), 2)
-    from_below = shift(merge(two_parts(1, 2)), 1)
-    from_above = shift(merge(two_parts(2, 3)), -1)
+    across = across_y(merge(two_parts(0, 4)), 2)
+    from_below = across_y(merge(two_parts(1, 2)), 1)
+    from_above = across_y(merge(two_parts(2, 3)), 3)
     keep, give = attend(table, q, 3, pieces, None, out_weight)
     return add(keep, swap(give), across, from_below, from_above)
 

time: 141 us -> 134 us (0.950)
  starting transfers between devices: 48.3 us -> 34.7 us
  waiting for transfers between devices: 53.6 us -> 61.4 us
    ppermute x15, starting transfers between devices: 46.1 us -> 33.1 us  [the longest x8 22 us: exchange(): return lax.ppermute(x, 'ctx', route)]
    ppermute x15, waiting for transfers between devices: 53.6 us -> 61.3 us  [the longest x7 43.6 us: across_y(): return lax.ppermute(x, 'tp', [(t, t ^ 2 * mask) for t in range(8)])]
  transfers between devices with their start and end apart: 24 -> 24, of which waited for: 8 -> 12; matrix products, arithmetic and copies ran while one was open for 0% -> 0% of each run, Pallas kernels for 19% -> 20%
where the time goes in v3:
time: 134 us; the launch traced here: 132 us
  waiting for transfers between devices  61.4 us (46%)
  starting transfers between devices  34.7 us (26%)
  Pallas kernels  29.8 us (22%)
  local copies, waits for them, and re-layouts  5.7 us (4%)
    ppermute x7, waiting for transfers between devices, across_y(): return lax.ppermute(x, 'tp', [(t, t ^ 2 * mask) for t in range(8)])  43.6 us
    ppermute x8, starting transfers between devices, exchange(): return lax.ppermute(x, 'ctx', route)  22 us
    pallas_call x7, Pallas kernels, attend(): pl.pallas_call(lambda *refs: attend_kernel(*refs, which=which, steps=step...  20.4 us
    ppermute x8, waiting for transfers between devices, exchange(): return lax.ppermute(x, 'ctx', route)  17.7 us
    ppermute x7, starting transfers between devices, across_y(): return lax.ppermute(x, 'tp', [(t, t ^ 2 * mask) for t in range(8)])  11.1 us
    unnamed x16, local copies, waits for them, and re-layouts  5.7 us
    pallas_call x3, Pallas kernels, project(): pl.pallas_call(body, out_shape=out_shape, in_specs=[vmem()] * (len(flat)...  4.95 us
  transfers between devices with their start and end apart: 24, of which 12 were waited for; matrix products, arithmetic and copies ran while one was open for 0% of the time, Pallas kernels for 20%

profile of v3, /device:TPU:6, one launch (start us, length us, event | category | flops | bytes accessed | tf_op | source)
XLA Modules:
  0.0 131.9 jit_solution(4208166843191966295)
XLA Ops:
  0.0 1.6 %collective-permute-start = (bf16[512,512]{1,0:T(8,128)(2,1)}, bf16[512,512]{1,0:T(8,128)(2,1)S(1)}, u32[]{:S(2)}, u32[]{:S(2)}) collective-permute-start(bf16[512,512]{1,0:T(8,128)(2,1)} %refs_3_.1), channel_id=1, source_target_pairs={{0,2},{1,3},{2,0},{3,1},{4,6},{5,7},{6,4},{7,5},{8,10},{9,11},{10,... | collective-permute-start | bytes 1572872 | tf_op jit(solution)/shard_map/ppermute | solution.py:27
  1.6 2.2 %collective-permute-start.2 = (bf16[512,512]{1,0:T(8,128)(2,1)}, bf16[512,512]{1,0:T(8,128)(2,1)S(1)}, u32[]{:S(2)}, u32[]{:S(2)}) collective-permute-start(bf16[512,512]{1,0:T(8,128)(2,1)} %refs_3_.1), channel_id=1, source_target_pairs={{0,6},{1,7},{2,4},{3,5},{4,2},{5,3},{6,0},{7,1},{8,14},{9,15},{10,... | collective-permute-start | bytes 1572872 | tf_op jit(solution)/shard_map/ppermute | solution.py:27
  3.8 10.1 %collective-permute-done.x.refs_2_ = bf16[512,512]{1,0:T(8,128)(2,1)S(1)} collective-permute-done((bf16[512,512]{1,0:T(8,128)(2,1)}, bf16[512,512]{1,0:T(8,128)(2,1)S(1)}, u32[]{:S(2)}, u32[]{:S(2)}) %collective-permute-start) | collective-permute-done | bytes 524320 | tf_op jit(solution)/shard_map/ppermute | solution.py:27
  13.9 2.5 %collective-permute-done.2.x.refs_4_ = bf16[512,512]{1,0:T(8,128)(2,1)S(1)} collective-permute-done((bf16[512,512]{1,0:T(8,128)(2,1)}, bf16[512,512]{1,0:T(8,128)(2,1)S(1)}, u32[]{:S(2)}, u32[]{:S(2)}) %collective-permute-start.2) | collective-permute-done | bytes 524320 | tf_op jit(solution)/shard_map/ppermute | solution.py:27
  16.4 2.3 %collective-permute-start.1 = (bf16[256,512]{1,0:T(8,128)(2,1)S(1)}, bf16[256,512]{1,0:T(8,128)(2,1)S(1)}, u32[]{:S(2)}, u32[]{:S(2)}) collective-permute-start(bf16[256,512]{1,0:T(8,128)(2,1)S(1)} %shard_map.82), channel_id=1, source_target_pairs={{0,6},{1,7},{2,4},{3,5},{4,2},{5,3},{6,0},{7,1},{8,14},{9,15},{10,... | collective-permute-start | bytes 786440 | tf_op jit(solution)/shard_map/ppermute | solution.py:27
  18.7 0.1 collective-permute-start.3
  18.8 7.6 %collective-permute-done.1.refs_0_ = bf16[256,512]{1,0:T(8,128)(2,1)S(1)} collective-permute-done((bf16[256,512]{1,0:T(8,128)(2,1)S(1)}, bf16[256,512]{1,0:T(8,128)(2,1)S(1)}, u32[]{:S(2)}, u32[]{:S(2)}) %collective-permute-start.1) | collective-permute-done | bytes 262176 | tf_op jit(solution)/shard_map/ppermute | solution.py:27
  26.4 0.8 collective-permute-done.3.refs_1_
  27.2 2.2 %copy-done.1 = bf16[4096,512]{1,0:T(8,128)(2,1)S(1)} copy-done((bf16[4096,512]{1,0:T(8,128)(2,1)S(1)}, bf16[4096,512]{1,0:T(8,128)(2,1)}, u32[]{:S(2)}) %copy-start.1) | copy-done | bytes 4194328
  29.4 1.2 copy-done.2
  30.6 1.2 copy-done.3
  31.9 1.0 copy-done.4
  32.9 0.5 load.1
  33.5 3.4 %shard_map.84 = (f32[512,128]{1,0:T(8,128)S(1)}, f32[512,128]{1,0:T(8,128)S(1)}, f32[512,512]{1,0:T(8,128)S(1)}) custom-call(bf16[512,512]{1,0:T(8,128)(2,1)S(1)} %get-tuple-element.30.refs_0_, bf16[512,512]{1,0:T(8,128)(2,1)S(1)} %collective-permute-done.6.refs_1_, bf16[512,512]{1,0:T(8,128)(2,1)S(1)} %collective-permute-done.x.refs_2_, ...), custom_call_target="tpu_custom_call" | custom-call | flops 2415919104 | bytes 7864320 | tf_op jit(solution)/shard_map/pallas_call | solution.py:89
  36.9 0.8 shard_map.86.refs_2_
  37.7 8.0 %collective-permute-start.10 = (bf16[2,4,128,128]{3,2,1,0:T(8,128)(2,1)S(1)}, bf16[2,4,128,128]{3,2,1,0:T(8,128)(2,1)S(1)}, u32[]{:S(2)}, u32[]{:S(2)}) collective-permute-start(bf16[2,4,128,128]{3,2,1,0:T(8,128)(2,1)S(1)} %shard_map.86.refs_2_), channel_id=1, source_target_pairs={{8,16},{16,8},{24,32},{32,24},{40,48},{48,40},{56,64},{64,56},{72,... | collective-permute-start | bytes 786440 | tf_op jit(solution)/shard_map/ppermute | solution.py:34
  45.8 0.1 collective-permute-start.9
  45.9 6.9 %collective-permute-done.10.refs_4_ = bf16[2,4,128,128]{3,2,1,0:T(8,128)(2,1)S(1)} collective-permute-done((bf16[2,4,128,128]{3,2,1,0:T(8,128)(2,1)S(1)}, bf16[2,4,128,128]{3,2,1,0:T(8,128)(2,1)S(1)}, u32[]{:S(2)}, u32[]{:S(2)}) %collective-permute-start.10) | collective-permute-done | bytes 262176 | tf_op jit(solution)/shard_map/ppermute | solution.py:34
  52.7 1.6 %collective-permute-done.9.refs_3_ = bf16[2,4,128,128]{3,2,1,0:T(8,128)(2,1)S(1)} collective-permute-done((bf16[2,4,128,128]{3,2,1,0:T(8,128)(2,1)S(1)}, bf16[2,4,128,128]{3,2,1,0:T(8,128)(2,1)S(1)}, u32[]{:S(2)}, u32[]{:S(2)}) %collective-permute-start.9) | collective-permute-done | bytes 262176 | tf_op jit(solution)/shard_map/ppermute | solution.py:34
  54.3 4.2 %collective-permute-start.12 = (bf16[2,4,128,128]{3,2,1,0:T(8,128)(2,1)S(1)}, bf16[2,4,128,128]{3,2,1,0:T(8,128)(2,1)S(1)}, u32[]{:S(2)}, u32[]{:S(2)}) collective-permute-start(bf16[2,4,128,128]{3,2,1,0:T(8,128)(2,1)S(1)} %collective-permute-done.9.refs_3_), channel_id=1, source_target_pairs={{8,16},{16,8},{24,32},{32,24},{40,48},{48,40},{56,64},{64,56},{72,... | collective-permute-start | bytes 786440 | tf_op jit(solution)/shard_map/ppermute | solution.py:34
  58.5 2.4 %collective-permute-done.11.refs_5_.refs_2_ = bf16[2,4,128,128]{3,2,1,0:T(8,128)(2,1)S(1)} collective-permute-done((bf16[2,4,128,128]{3,2,1,0:T(8,128)(2,1)S(1)}, bf16[2,4,128,128]{3,2,1,0:T(8,128)(2,1)S(1)}, u32[]{:S(2)}, u32[]{:S(2)}) %collective-permute-start.11) | collective-permute-done | bytes 262176 | tf_op jit(solution)/shard_map/ppermute | solution.py:34
  60.9 5.5 %collective-permute-start.14 = (bf16[2,4,128,128]{3,2,1,0:T(8,128)(2,1)S(1)}, bf16[2,4,128,128]{3,2,1,0:T(8,128)(2,1)S(1)}, u32[]{:S(2)}, u32[]{:S(2)}) collective-permute-start(bf16[2,4,128,128]{3,2,1,0:T(8,128)(2,1)S(1)} %collective-permute-done.11.refs_5_.refs_2_), channel_id=1, source_target_pairs={{8,16},{16,8},{24,32},{32,24},{40,48},{48,40},{56,64},{64,56},{72,... | collective-permute-start | bytes 786440 | tf_op jit(solution)/shard_map/ppermute | solution.py:34
  66.4 0.1 collective-permute-start.13
  66.5 5.7 %collective-permute-done.14.refs_8_.refs_5_.refs_3_ = bf16[2,4,128,128]{3,2,1,0:T(8,128)(2,1)S(1)} collective-permute-done((bf16[2,4,128,128]{3,2,1,0:T(8,128)(2,1)S(1)}, bf16[2,4,128,128]{3,2,1,0:T(8,128)(2,1)S(1)}, u32[]{:S(2)}, u32[]{:S(2)}) %collective-permute-start.14) | collective-permute-done | bytes 262176 | tf_op jit(solution)/shard_map/ppermute | solution.py:34
  72.2 1.2 collective-permute-done.13.refs_7_.refs_4_.refs_2_
  73.4 4.2 %collective-permute-start.16 = (bf16[2,4,128,128]{3,2,1,0:T(8,128)(2,1)S(1)}, bf16[2,4,128,128]{3,2,1,0:T(8,128)(2,1)S(1)}, u32[]{:S(2)}, u32[]{:S(2)}) collective-permute-start(bf16[2,4,128,128]{3,2,1,0:T(8,128)(2,1)S(1)} %collective-permute-done.13.refs_7_.refs_4_.refs_2_), channel_id=1, source_target_pairs={{8,16},{16,8},{24,32},{32,24},{40,48},{48,40},{56,64},{64,56},{72,... | collective-permute-start | bytes 786440 | tf_op jit(solution)/shard_map/ppermute | solution.py:34
  77.6 2.4 %list_slots.1.refs_0_ = s32[20,18]{1,0:T(8,128)S(1)} custom-call(s32[4,16]{1,0:T(4,128)S(1)} %copy-done.5, s32[4]{0:T(128)S(1)} %copy-done.6, s32[128]{0:T(128)S(1)} %copy-done.7), custom_call_target="tpu_custom_call" | custom-call | tf_op jit(solution)/shard_map/list_slots/pallas_call | solution.py:229
  80.0 0.7 shard_map.85.refs_1_
  80.8 2.7 %shard_map.90 = (f32[512,128]{1,0:T(8,128)S(1)}, f32[512,128]{1,0:T(8,128)S(1)}, f32[512,128]{1,0:T(8,128)S(1)}) custom-call(s32[20,18]{1,0:T(8,128)S(1)} %list_slots.1.refs_0_, bf16[4,512,128]{2,1,0:T(8,128)(2,1)S(1)} %shard_map.85.refs_1_, bf16[2,4,128,128]{3,2,1,0:T(8,128)(2,1)S(1)} %shard_map.86.refs_2_, ...), custom_call_target="tpu_custom_call" | custom-call | flops 536870912 | bytes 4194304 | tf_op jit(solution)/shard_map/pallas_call | solution.py:300
  83.4 2.7 %shard_map.92 = (f32[512,128]{1,0:T(8,128)S(1)}, f32[512,128]{1,0:T(8,128)S(1)}, f32[512,128]{1,0:T(8,128)S(1)}) custom-call(s32[20,18]{1,0:T(8,128)S(1)} %list_slots.1.refs_0_, bf16[4,512,128]{2,1,0:T(8,128)(2,1)S(1)} %shard_map.85.refs_1_, bf16[2,4,128,128]{3,2,1,0:T(8,128)(2,1)S(1)} %shard_map.86.refs_2_, ...), custom_call_target="tpu_custom_call" | custom-call | flops 536870912 | bytes 4194304 | tf_op jit(solution)/shard_map/pallas_call | solution.py:300
  86.1 3.2 %shard_map.88 = (f32[512,128]{1,0:T(8,128)S(1)}, f32[512,128]{1,0:T(8,128)S(1)}, f32[512,128]{1,0:T(8,128)S(1)}) custom-call(s32[20,18]{1,0:T(8,128)S(1)} %list_slots.1.refs_0_, bf16[4,512,128]{2,1,0:T(8,128)(2,1)S(1)} %shard_map.85.refs_1_, bf16[2,4,128,128]{3,2,1,0:T(8,128)(2,1)S(1)} %shard_map.86.refs_2_, ...), custom_call_target="tpu_custom_call" | custom-call | flops 536870912 | bytes 4194304 | tf_op jit(solution)/shard_map/pallas_call | solution.py:300
  89.3 2.1 %shard_map.93 = (bf16[64,4096]{1,0:T(8,128)(2,1)S(1)}, bf16[64,4096]{1,0:T(8,128)(2,1)S(1)}) custom-call(s32[20,18]{1,0:T(8,128)S(1)} %list_slots.1.refs_0_, bf16[4,512,128]{2,1,0:T(8,128)(2,1)S(1)} %shard_map.85.refs_1_, bf16[2,4,128,128]{3,2,1,0:T(8,128)(2,1)S(1)} %collective-permute-done.13.refs_7_.refs_4_.refs_2_, ...), custom_call_target="tpu_custom_call" | custom-call | flops 536870912 | bytes 4194304 | tf_op jit(solution)/shard_map/pallas_call | solution.py:300
  91.6 3.2 %shard_map.91 = (bf16[64,4096]{1,0:T(8,128)(2,1)S(1)}, bf16[64,4096]{1,0:T(8,128)(2,1)S(1)}) custom-call(s32[20,18]{1,0:T(8,128)S(1)} %list_slots.1.refs_0_, bf16[4,512,128]{2,1,0:T(8,128)(2,1)S(1)} %shard_map.85.refs_1_, bf16[2,4,128,128]{3,2,1,0:T(8,128)(2,1)S(1)} %collective-permute-done.11.refs_5_.refs_2_, ...), custom_call_target="tpu_custom_call" | custom-call | flops 536870912 | bytes 4194304 | tf_op jit(solution)/shard_map/pallas_call | solution.py:300
  94.7 0.6 collective-permute-start.20
  95.3 1.6 %shard_map.89 = (bf16[64,4096]{1,0:T(8,128)(2,1)S(1)}, bf16[64,4096]{1,0:T(8,128)(2,1)S(1)}) custom-call(s32[20,18]{1,0:T(8,128)S(1)} %list_slots.1.refs_0_, bf16[4,512,128]{2,1,0:T(8,128)(2,1)S(1)} %shard_map.85.refs_1_, bf16[2,4,128,128]{3,2,1,0:T(8,128)(2,1)S(1)} %collective-permute-done.15.refs_9_.refs_2_.refs_6_.refs_4_, ...), custom_call_target="tpu_custom_call" | custom-call | flops 536870912 | bytes 4194304 | tf_op jit(solution)/shard_map/pallas_call | solution.py:300
  97.0 0.3 collective-permute-start.18
  97.3 5.0 %shard_map.87 = (bf16[64,4096]{1,0:T(8,128)(2,1)S(1)}, bf16[64,4096]{1,0:T(8,128)(2,1)S(1)}) custom-call(s32[20,18]{1,0:T(8,128)S(1)} %list_slots.1.refs_0_, bf16[4,512,128]{2,1,0:T(8,128)(2,1)S(1)} %shard_map.85.refs_1_, bf16[2,4,128,128]{3,2,1,0:T(8,128)(2,1)S(1)} %shard_map.86.refs_2_, bf16[2,4,128,128]{3,2,1,0:T(8,128)(2,1)S(1)} %collective-permute-done.9.refs_3_, ...), custom_call_target="tpu_custom_call" | custom-call | flops 536870912 | bytes 4194304 | tf_op jit(solution)/shard_map/pallas_call | solution.py:300
  102.3 0.6 collective-permute-start.17
  102.9 0.1 add.6
  103.0 0.5 collective-permute-start.23
  103.5 0.1 add.5
  103.6 0.4 collective-permute-start.21
  104.0 0.1 add.4
  104.1 4.1 %collective-permute-start.19 = (bf16[64,4096]{1,0:T(8,128)(2,1)S(1)}, bf16[64,4096]{1,0:T(8,128)(2,1)S(1)}, u32[]{:S(2)}, u32[]{:S(2)}) collective-permute-start(bf16[64,4096]{1,0:T(8,128)(2,1)S(1)} %add.4), channel_id=1, source_target_pairs={{0,4},{1,5},{2,6},{3,7},{4,0},{5,1},{6,2},{7,3},{8,12},{9,13},{10,... | collective-permute-start | bytes 1572872 | tf_op jit(solution)/shard_map/ppermute | solution.py:27
  108.2 9.9 %collective-permute-done.23.refs_4_ = bf16[64,4096]{1,0:T(8,128)(2,1)S(1)} collective-permute-done((bf16[64,4096]{1,0:T(8,128)(2,1)S(1)}, bf16[64,4096]{1,0:T(8,128)(2,1)S(1)}, u32[]{:S(2)}, u32[]{:S(2)}) %collective-permute-start.23) | collective-permute-done | bytes 524320 | tf_op jit(solution)/shard_map/ppermute | solution.py:27
  118.2 0.3 collective-permute-done.21.refs_3_
  118.5 12.3 %collective-permute-done.19.refs_2_ = bf16[64,4096]{1,0:T(8,128)(2,1)S(1)} collective-permute-done((bf16[64,4096]{1,0:T(8,128)(2,1)S(1)}, bf16[64,4096]{1,0:T(8,128)(2,1)S(1)}, u32[]{:S(2)}, u32[]{:S(2)}) %collective-permute-start.19) | collective-permute-done | bytes 524320 | tf_op jit(solution)/shard_map/ppermute | solution.py:27
  130.8 1.1 add.7
  (34 shorter events, 0.2 us)
Async XLA Ops:
  0.0 13.9 %collective-permute-start = (bf16[512,512]{1,0:T(8,128)(2,1)}, bf16[512,512]{1,0:T(8,128)(2,1)S(1)}, u32[]{:S(2)}, u32[]{:S(2)}) collective-permute-start(bf16[512,512]{1,0:T(8,128)(2,1)} %refs_3_.1), channel_id=1, source_target_pairs={{0,2},{1,3},{2,0},{3,1},{4,6},{5,7},{6,4},{7,5},{8,10},{9,11},{10,... | collective-permute-start | bytes 1572872 | tf_op jit(solution)/shard_map/ppermute | solution.py:27
  1.6 14.8 %collective-permute-start.2 = (bf16[512,512]{1,0:T(8,128)(2,1)}, bf16[512,512]{1,0:T(8,128)(2,1)S(1)}, u32[]{:S(2)}, u32[]{:S(2)}) collective-permute-start(bf16[512,512]{1,0:T(8,128)(2,1)} %refs_3_.1), channel_id=1, source_target_pairs={{0,6},{1,7},{2,4},{3,5},{4,2},{5,3},{6,0},{7,1},{8,14},{9,15},{10,... | collective-permute-start | bytes 1572872 | tf_op jit(solution)/shard_map/ppermute | solution.py:27
  3.8 29.7 %collective-permute-start.6 = (bf16[512,512]{1,0:T(8,128)(2,1)}, bf16[512,512]{1,0:T(8,128)(2,1)S(1)}, u32[]{:S(2)}, u32[]{:S(2)}) collective-permute-start(bf16[512,512]{1,0:T(8,128)(2,1)} %refs_3_.1), channel_id=1, source_target_pairs={{0,1},{1,0},{2,3},{3,2},{4,5},{5,4},{6,7},{7,6},{8,9},{9,8},{10,11... | collective-permute-start | bytes 1572872 | tf_op jit(solution)/shard_map/ppermute | solution.py:23
  13.9 19.5 %collective-permute-start.7 = (bf16[512,512]{1,0:T(8,128)(2,1)S(1)}, bf16[512,512]{1,0:T(8,128)(2,1)S(1)}, u32[]{:S(2)}, u32[]{:S(2)}) collective-permute-start(bf16[512,512]{1,0:T(8,128)(2,1)S(1)} %collective-permute-done.x.refs_2_), channel_id=1, source_target_pairs={{0,1},{1,0},{2,3},{3,2},{4,5},{5,4},{6,7},{7,6},{8,9},{9,8},{10,11... | collective-permute-start | bytes 1572872 | tf_op jit(solution)/shard_map/ppermute | solution.py:23
  16.4 17.1 %collective-permute-start.8 = (bf16[512,512]{1,0:T(8,128)(2,1)S(1)}, bf16[512,512]{1,0:T(8,128)(2,1)S(1)}, u32[]{:S(2)}, u32[]{:S(2)}) collective-permute-start(bf16[512,512]{1,0:T(8,128)(2,1)S(1)} %collective-permute-done.2.x.refs_4_), channel_id=1, source_target_pairs={{0,1},{1,0},{2,3},{3,2},{4,5},{5,4},{6,7},{7,6},{8,9},{9,8},{10,11... | collective-permute-start | bytes 1572872 | tf_op jit(solution)/shard_map/ppermute | solution.py:23
  16.4 10.0 %collective-permute-start.1 = (bf16[256,512]{1,0:T(8,128)(2,1)S(1)}, bf16[256,512]{1,0:T(8,128)(2,1)S(1)}, u32[]{:S(2)}, u32[]{:S(2)}) collective-permute-start(bf16[256,512]{1,0:T(8,128)(2,1)S(1)} %shard_map.82), channel_id=1, source_target_pairs={{0,6},{1,7},{2,4},{3,5},{4,2},{5,3},{6,0},{7,1},{8,14},{9,15},{10,... | collective-permute-start | bytes 786440 | tf_op jit(solution)/shard_map/ppermute | solution.py:27
  18.7 8.5 %collective-permute-start.3 = (bf16[256,512]{1,0:T(8,128)(2,1)S(1)}, bf16[256,512]{1,0:T(8,128)(2,1)S(1)}, u32[]{:S(2)}, u32[]{:S(2)}) collective-permute-start(bf16[256,512]{1,0:T(8,128)(2,1)S(1)} %shard_map.83), channel_id=1, source_target_pairs={{0,2},{1,3},{2,0},{3,1},{4,6},{5,7},{6,4},{7,5},{8,10},{9,11},{10,... | collective-permute-start | bytes 786440 | tf_op jit(solution)/shard_map/ppermute | solution.py:27
  26.4 10.5 %collective-permute-start.4 = (bf16[256,512]{1,0:T(8,128)(2,1)S(1)}, bf16[256,512]{1,0:T(8,128)(2,1)S(1)}, u32[]{:S(2)}, u32[]{:S(2)}) collective-permute-start(bf16[256,512]{1,0:T(8,128)(2,1)S(1)} %collective-permute-done.1.refs_0_), channel_id=1, source_target_pairs={{0,1},{1,0},{2,3},{3,2},{4,5},{5,4},{6,7},{7,6},{8,9},{9,8},{10,11... | collective-permute-start | bytes 786440 | tf_op jit(solution)/shard_map/ppermute | solution.py:23
  27.2 9.7 %collective-permute-start.5 = (bf16[256,512]{1,0:T(8,128)(2,1)S(1)}, bf16[256,512]{1,0:T(8,128)(2,1)S(1)}, u32[]{:S(2)}, u32[]{:S(2)}) collective-permute-start(bf16[256,512]{1,0:T(8,128)(2,1)S(1)} %collective-permute-done.3.refs_1_), channel_id=1, source_target_pairs={{0,1},{1,0},{2,3},{3,2},{4,5},{5,4},{6,7},{7,6},{8,9},{9,8},{10,11... | collective-permute-start | bytes 786440 | tf_op jit(solution)/shard_map/ppermute | solution.py:23
  27.2 2.2 %copy-start.1 = (bf16[4096,512]{1,0:T(8,128)(2,1)S(1)}, bf16[4096,512]{1,0:T(8,128)(2,1)}, u32[]{:S(2)}) copy-start(bf16[4096,512]{1,0:T(8,128)(2,1)} %refs_2_.1) | copy-start | bytes 12582916
  29.4 1.2 copy-start.2
  30.6 1.2 copy-start.3
  31.9 1.0 copy-start.4
  33.4 44.1 %copy-start.5 = (s32[4,16]{1,0:T(4,128)S(1)}, s32[4,16]{1,0:T(4,128)}, u32[]{:S(2)}) copy-start(s32[4,16]{1,0:T(4,128)} %links.1) | copy-start | bytes 772
  33.5 44.1 %copy-start.6 = (s32[4]{0:T(128)S(1)}, s32[4]{0:T(128)}, u32[]{:S(2)}) copy-start(s32[4]{0:T(128)} %counts.1) | copy-start | bytes 52
  33.5 44.1 %copy-start.7 = (s32[128]{0:T(128)S(1)}, s32[128]{0:T(128)}, u32[]{:S(2)}) copy-start(s32[128]{0:T(128)} %docs.1) | copy-start | bytes 1540
  37.7 15.0 %collective-permute-start.10 = (bf16[2,4,128,128]{3,2,1,0:T(8,128)(2,1)S(1)}, bf16[2,4,128,128]{3,2,1,0:T(8,128)(2,1)S(1)}, u32[]{:S(2)}, u32[]{:S(2)}) collective-permute-start(bf16[2,4,128,128]{3,2,1,0:T(8,128)(2,1)S(1)} %shard_map.86.refs_2_), channel_id=1, source_target_pairs={{8,16},{16,8},{24,32},{32,24},{40,48},{48,40},{56,64},{64,56},{72,... | collective-permute-start | bytes 786440 | tf_op jit(solution)/shard_map/ppermute | solution.py:34
  45.8 8.5 %collective-permute-start.9 = (bf16[2,4,128,128]{3,2,1,0:T(8,128)(2,1)S(1)}, bf16[2,4,128,128]{3,2,1,0:T(8,128)(2,1)S(1)}, u32[]{:S(2)}, u32[]{:S(2)}) collective-permute-start(bf16[2,4,128,128]{3,2,1,0:T(8,128)(2,1)S(1)} %shard_map.86.refs_2_), channel_id=1, source_target_pairs={{0,8},{8,0},{16,24},{24,16},{32,40},{40,32},{48,56},{56,48},{64,72... | collective-permute-start | bytes 786440 | tf_op jit(solution)/shard_map/ppermute | solution.py:34
  52.7 8.2 %collective-permute-start.11 = (bf16[2,4,128,128]{3,2,1,0:T(8,128)(2,1)S(1)}, bf16[2,4,128,128]{3,2,1,0:T(8,128)(2,1)S(1)}, u32[]{:S(2)}, u32[]{:S(2)}) collective-permute-start(bf16[2,4,128,128]{3,2,1,0:T(8,128)(2,1)S(1)} %collective-permute-done.10.refs_4_), channel_id=1, source_target_pairs={{0,8},{8,0},{16,24},{24,16},{32,40},{40,32},{48,56},{56,48},{64,72... | collective-permute-start | bytes 786440 | tf_op jit(solution)/shard_map/ppermute | solution.py:34
  54.3 12.1 %collective-permute-start.12 = (bf16[2,4,128,128]{3,2,1,0:T(8,128)(2,1)S(1)}, bf16[2,4,128,128]{3,2,1,0:T(8,128)(2,1)S(1)}, u32[]{:S(2)}, u32[]{:S(2)}) collective-permute-start(bf16[2,4,128,128]{3,2,1,0:T(8,128)(2,1)S(1)} %collective-permute-done.9.refs_3_), channel_id=1, source_target_pairs={{8,16},{16,8},{24,32},{32,24},{40,48},{48,40},{56,64},{64,56},{72,... | collective-permute-start | bytes 786440 | tf_op jit(solution)/shard_map/ppermute | solution.py:34
  60.9 11.3 %collective-permute-start.14 = (bf16[2,4,128,128]{3,2,1,0:T(8,128)(2,1)S(1)}, bf16[2,4,128,128]{3,2,1,0:T(8,128)(2,1)S(1)}, u32[]{:S(2)}, u32[]{:S(2)}) collective-permute-start(bf16[2,4,128,128]{3,2,1,0:T(8,128)(2,1)S(1)} %collective-permute-done.11.refs_5_.refs_2_), channel_id=1, source_target_pairs={{8,16},{16,8},{24,32},{32,24},{40,48},{48,40},{56,64},{64,56},{72,... | collective-permute-start | bytes 786440 | tf_op jit(solution)/shard_map/ppermute | solution.py:34
  66.4 7.0 %collective-permute-start.13 = (bf16[2,4,128,128]{3,2,1,0:T(8,128)(2,1)S(1)}, bf16[2,4,128,128]{3,2,1,0:T(8,128)(2,1)S(1)}, u32[]{:S(2)}, u32[]{:S(2)}) collective-permute-start(bf16[2,4,128,128]{3,2,1,0:T(8,128)(2,1)S(1)} %collective-permute-done.12.refs_6_.refs_3_), channel_id=1, source_target_pairs={{0,8},{8,0},{16,24},{24,16},{32,40},{40,32},{48,56},{56,48},{64,72... | collective-permute-start | bytes 786440 | tf_op jit(solution)/shard_map/ppermute | solution.py:34
  72.2 17.1 %collective-permute-start.15 = (bf16[2,4,128,128]{3,2,1,0:T(8,128)(2,1)S(1)}, bf16[2,4,128,128]{3,2,1,0:T(8,128)(2,1)S(1)}, u32[]{:S(2)}, u32[]{:S(2)}) collective-permute-start(bf16[2,4,128,128]{3,2,1,0:T(8,128)(2,1)S(1)} %collective-permute-done.14.refs_8_.refs_5_.refs_3_), channel_id=1, source_target_pairs={{0,8},{8,0},{16,24},{24,16},{32,40},{40,32},{48,56},{56,48},{64,72... | collective-permute-start | bytes 786440 | tf_op jit(solution)/shard_map/ppermute | solution.py:34
  73.4 15.9 %collective-permute-start.16 = (bf16[2,4,128,128]{3,2,1,0:T(8,128)(2,1)S(1)}, bf16[2,4,128,128]{3,2,1,0:T(8,128)(2,1)S(1)}, u32[]{:S(2)}, u32[]{:S(2)}) collective-permute-start(bf16[2,4,128,128]{3,2,1,0:T(8,128)(2,1)S(1)} %collective-permute-done.13.refs_7_.refs_4_.refs_2_), channel_id=1, source_target_pairs={{8,16},{16,8},{24,32},{32,24},{40,48},{48,40},{56,64},{64,56},{72,... | collective-permute-start | bytes 786440 | tf_op jit(solution)/shard_map/ppermute | solution.py:34
  80.8 8.6 %copy-start = (bf16[512,4096]{1,0:T(8,128)(2,1)S(1)}, bf16[512,4096]{1,0:T(8,128)(2,1)}, u32[]{:S(2)}) copy-start(bf16[512,4096]{1,0:T(8,128)(2,1)} %refs_9_.1) | copy-start | bytes 12582916
  91.5 11.4 %collective-permute-start.22 = (bf16[64,4096]{1,0:T(8,128)(2,1)S(1)}, bf16[64,4096]{1,0:T(8,128)(2,1)S(1)}, u32[]{:S(2)}, u32[]{:S(2)}) collective-permute-start(bf16[64,4096]{1,0:T(8,128)(2,1)S(1)} %get-tuple-element.52), channel_id=1, source_target_pairs={{0,1},{1,0},{2,3},{3,2},{4,5},{5,4},{6,7},{7,6},{8,9},{9,8},{10,11... | collective-permute-start | bytes 1572872 | tf_op jit(solution)/shard_map/ppermute | solution.py:23
  94.7 8.7 %collective-permute-start.20 = (bf16[64,4096]{1,0:T(8,128)(2,1)S(1)}, bf16[64,4096]{1,0:T(8,128)(2,1)S(1)}, u32[]{:S(2)}, u32[]{:S(2)}) collective-permute-start(bf16[64,4096]{1,0:T(8,128)(2,1)S(1)} %get-tuple-element.47), channel_id=1, source_target_pairs={{0,1},{1,0},{2,3},{3,2},{4,5},{5,4},{6,7},{7,6},{8,9},{9,8},{10,11... | collective-permute-start | bytes 1572872 | tf_op jit(solution)/shard_map/ppermute | solution.py:23
  97.0 7.1 %collective-permute-start.18 = (bf16[64,4096]{1,0:T(8,128)(2,1)S(1)}, bf16[64,4096]{1,0:T(8,128)(2,1)S(1)}, u32[]{:S(2)}, u32[]{:S(2)}) collective-permute-start(bf16[64,4096]{1,0:T(8,128)(2,1)S(1)} %get-tuple-element.42), channel_id=1, source_target_pairs={{0,1},{1,0},{2,3},{3,2},{4,5},{5,4},{6,7},{7,6},{8,9},{9,8},{10,11... | collective-permute-start | bytes 1572872 | tf_op jit(solution)/shard_map/ppermute | solution.py:23
  102.3 5.9 %collective-permute-start.17 = (bf16[64,4096]{1,0:T(8,128)(2,1)S(1)}, bf16[64,4096]{1,0:T(8,128)(2,1)S(1)}, u32[]{:S(2)}, u32[]{:S(2)}) collective-permute-start(bf16[64,4096]{1,0:T(8,128)(2,1)S(1)} %get-tuple-element.37), channel_id=1, source_target_pairs={{0,1},{1,0},{2,3},{3,2},{4,5},{5,4},{6,7},{7,6},{8,9},{9,8},{10,11... | collective-permute-start | bytes 1572872 | tf_op jit(solution)/shard_map/ppermute | solution.py:23
  103.0 15.2 %collective-permute-start.23 = (bf16[64,4096]{1,0:T(8,128)(2,1)S(1)}, bf16[64,4096]{1,0:T(8,128)(2,1)S(1)}, u32[]{:S(2)}, u32[]{:S(2)}) collective-permute-start(bf16[64,4096]{1,0:T(8,128)(2,1)S(1)} %add.6), channel_id=1, source_target_pairs={{0,6},{1,7},{2,4},{3,5},{4,2},{5,3},{6,0},{7,1},{8,14},{9,15},{10,... | collective-permute-start | bytes 1572872 | tf_op jit(solution)/shard_map/ppermute | solution.py:27
  103.6 14.9 %collective-permute-start.21 = (bf16[64,4096]{1,0:T(8,128)(2,1)S(1)}, bf16[64,4096]{1,0:T(8,128)(2,1)S(1)}, u32[]{:S(2)}, u32[]{:S(2)}) collective-permute-start(bf16[64,4096]{1,0:T(8,128)(2,1)S(1)} %add.5), channel_id=1, source_target_pairs={{0,2},{1,3},{2,0},{3,1},{4,6},{5,7},{6,4},{7,5},{8,10},{9,11},{10,... | collective-permute-start | bytes 1572872 | tf_op jit(solution)/shard_map/ppermute | solution.py:27
  104.1 26.6 %collective-permute-start.19 = (bf16[64,4096]{1,0:T(8,128)(2,1)S(1)}, bf16[64,4096]{1,0:T(8,128)(2,1)S(1)}, u32[]{:S(2)}, u32[]{:S(2)}) collective-permute-start(bf16[64,4096]{1,0:T(8,128)(2,1)S(1)} %add.4), channel_id=1, source_target_pairs={{0,4},{1,5},{2,6},{3,7},{4,0},{5,1},{6,2},{7,3},{8,12},{9,13},{10,... | collective-permute-start | bytes 1572872 | tf_op jit(solution)/shard_map/ppermute | solution.py:27

commit v4 on v3

--- a/solution.py
+++ b/solution.py
@@ -153,6 +153,46 @@
         compiler_params=limit(6),
         name="add",
     )(*parts)
+
+
+def halves_kernel(a, b, low, high):
+    rows = low.shape[0]
+    total = a[...].astype(jnp.float32) + b[...].astype(jnp.float32)
+    low[...] = total[:rows].astype(jnp.bfloat16)
+    high[...] = total[rows:].astype(jnp.bfloat16)
+
+
+def add_to_halves(a, b):
+    shape = jax.ShapeDtypeStruct((a.shape[0] // 2, a.shape[1]), a.dtype)
+    return pl.pallas_call(
+        halves_kernel,
+        out_shape=(shape, shape),
+        in_specs=[vmem()] * 2,
+        out_specs=(vmem(), vmem()),
+        compiler_params=limit(6),
+        name="add_to_halves",
+    )(a, b)
+
+
+def add_half(a, b, half, second):
+    rows = half.shape[0]
+
+    def body(a, b, half, out):
+        total = a[...].astype(jnp.float32) + b[...].astype(jnp.float32)
+        more = half[...].astype(jnp.float32)
+        low, high = total[:rows], total[rows:]
+        low, high = (low, high + more) if second else (low + more, high)
+        out[pl.ds(0, rows), :] = low.astype(jnp.bfloat16)
+        out[pl.ds(rows, rows), :] = high.astype(jnp.bfloat16)
+
+    return pl.pallas_call(
+        body,
+        out_shape=jax.ShapeDtypeStruct(a.shape, a.dtype),
+        in_specs=[vmem()] * 3,
+        out_specs=vmem(),
+        compiler_params=limit(6),
+        name="add_half",
+    )(a, b, half)
 
 
 def keep_sums(out, accs):
@@ -340,18 +380,24 @@
     for k in range(1, REACH + 1):
         even, odd = exchange(odd, 0), exchange(even, 1)
         pieces[k] = even, odd
-    merge = lambda pair: add(pair[0], swap(pair[1]))
-
-    def two_parts(which, cut):
-        parts = {k: pieces[k] for k in range(cut)}, {k: pieces[k] for k in range(cut, REACH + 1)}
-        state = attend(table, q, which, parts[0], None, None)
-        return attend(table, q, which, parts[1], state, out_weight)
-
-    across = across_y(merge(two_parts(0, 4)), 2)
-    from_below = across_y(merge(two_parts(1, 2)), 1)
-    from_above = across_y(merge(two_parts(2, 3)), 3)
+
+    def in_parts(which, cuts):
+        state, start = None, 0
+        for cut in cuts:
+            part = {k: pieces[k] for k in range(start, cut)}
+            wo = out_weight if cut > REACH else None
+            state, start = attend(table, q, which, part, state, wo), cut
+        return state
+
+    keep, give = in_parts(0, (3, 4, 5))
+    low, high = add_to_halves(keep, swap(give))
+    low, high = across_y(low, 1), across_y(high, 3)
+    keep, give = in_parts(1, (2, 4, 5))
+    one = across_y(add_half(keep, swap(give), high, True), 1)
+    keep, give = in_parts(2, (2, 4, 5))
+    other = across_y(add_half(keep, swap(give), low, False), 3)
     keep, give = attend(table, q, 3, pieces, None, out_weight)
-    return add(keep, swap(give), across, from_below, from_above)
+    return add(keep, swap(give), one, other)
 
 
 def solution(mesh):

time: 134 us -> 128 us (0.955)
  the two profiles are of different devices: /device:TPU:6 before, /device:TPU:4 now
where the time goes in v4:
time: 128 us
  waiting for transfers between devices  55 us (43%)
  Pallas kernels  34.5 us (27%)
  starting transfers between devices  32.6 us (25%)
  local copies, waits for them, and re-layouts  5.7 us (4%)
    ppermute x8, waiting for transfers between devices, across_y(): return lax.ppermute(x, 'tp', [(t, t ^ 2 * mask) for t in range(8)])  37.2 us
    pallas_call x10, Pallas kernels, attend(): pl.pallas_call(lambda *refs: attend_kernel(*refs, which=which, steps=step...  25 us
    ppermute x8, starting transfers between devices, exchange(): return lax.ppermute(x, 'ctx', route)  21.7 us
    ppermute x8, waiting for transfers between devices, exchange(): return lax.ppermute(x, 'ctx', route)  17.7 us
    ppermute x8, starting transfers between devices, across_y(): return lax.ppermute(x, 'tp', [(t, t ^ 2 * mask) for t in range(8)])  9.54 us
    unnamed x16, local copies, waits for them, and re-layouts  5.7 us
    pallas_call x3, Pallas kernels, project(): pl.pallas_call(body, out_shape=out_shape, in_specs=[vmem()] * (len(flat)...  4.95 us
  transfers between devices with their start and end apart: 25, of which 13 were waited for; matrix products, arithmetic and copies ran while one was open for 0% of the time, Pallas kernels for 24%

profile of v4, /device:TPU:4, one launch (start us, length us, event | category | flops | bytes accessed | tf_op | source)
XLA Modules:
  0.0 128.0 jit_solution(16300587644183300046)
XLA Ops:
  0.0 1.6 %collective-permute-start = (bf16[512,512]{1,0:T(8,128)(2,1)}, bf16[512,512]{1,0:T(8,128)(2,1)S(1)}, u32[]{:S(2)}, u32[]{:S(2)}) collective-permute-start(bf16[512,512]{1,0:T(8,128)(2,1)} %refs_3_.1), channel_id=1, source_target_pairs={{0,2},{1,3},{2,0},{3,1},{4,6},{5,7},{6,4},{7,5},{8,10},{9,11},{10,... | collective-permute-start | bytes 1572872 | tf_op jit(solution)/shard_map/ppermute | solution.py:27
  1.6 2.2 %collective-permute-start.2 = (bf16[512,512]{1,0:T(8,128)(2,1)}, bf16[512,512]{1,0:T(8,128)(2,1)S(1)}, u32[]{:S(2)}, u32[]{:S(2)}) collective-permute-start(bf16[512,512]{1,0:T(8,128)(2,1)} %refs_3_.1), channel_id=1, source_target_pairs={{0,6},{1,7},{2,4},{3,5},{4,2},{5,3},{6,0},{7,1},{8,14},{9,15},{10,... | collective-permute-start | bytes 1572872 | tf_op jit(solution)/shard_map/ppermute | solution.py:27
  3.8 10.1 %collective-permute-done.x.refs_2_ = bf16[512,512]{1,0:T(8,128)(2,1)S(1)} collective-permute-done((bf16[512,512]{1,0:T(8,128)(2,1)}, bf16[512,512]{1,0:T(8,128)(2,1)S(1)}, u32[]{:S(2)}, u32[]{:S(2)}) %collective-permute-start) | collective-permute-done | bytes 524320 | tf_op jit(solution)/shard_map/ppermute | solution.py:27
  13.9 2.5 %collective-permute-done.2.x.refs_4_ = bf16[512,512]{1,0:T(8,128)(2,1)S(1)} collective-permute-done((bf16[512,512]{1,0:T(8,128)(2,1)}, bf16[512,512]{1,0:T(8,128)(2,1)S(1)}, u32[]{:S(2)}, u32[]{:S(2)}) %collective-permute-start.2) | collective-permute-done | bytes 524320 | tf_op jit(solution)/shard_map/ppermute | solution.py:27
  16.4 2.3 %collective-permute-start.1 = (bf16[256,512]{1,0:T(8,128)(2,1)S(1)}, bf16[256,512]{1,0:T(8,128)(2,1)S(1)}, u32[]{:S(2)}, u32[]{:S(2)}) collective-permute-start(bf16[256,512]{1,0:T(8,128)(2,1)S(1)} %shard_map.82), channel_id=1, source_target_pairs={{0,6},{1,7},{2,4},{3,5},{4,2},{5,3},{6,0},{7,1},{8,14},{9,15},{10,... | collective-permute-start | bytes 786440 | tf_op jit(solution)/shard_map/ppermute | solution.py:27
  18.8 7.6 %collective-permute-done.1.refs_0_ = bf16[256,512]{1,0:T(8,128)(2,1)S(1)} collective-permute-done((bf16[256,512]{1,0:T(8,128)(2,1)S(1)}, bf16[256,512]{1,0:T(8,128)(2,1)S(1)}, u32[]{:S(2)}, u32[]{:S(2)}) %collective-permute-start.1) | collective-permute-done | bytes 262176 | tf_op jit(solution)/shard_map/ppermute | solution.py:27
  26.4 0.8 collective-permute-done.3.refs_1_
  27.2 2.2 %copy-done.1 = bf16[4096,512]{1,0:T(8,128)(2,1)S(1)} copy-done((bf16[4096,512]{1,0:T(8,128)(2,1)S(1)}, bf16[4096,512]{1,0:T(8,128)(2,1)}, u32[]{:S(2)}) %copy-start.1) | copy-done | bytes 4194328
  29.4 1.2 copy-done.2
  30.6 1.2 copy-done.3
  31.9 1.0 copy-done.4
  32.9 0.5 load.1
  33.5 3.4 %shard_map.84 = (f32[512,128]{1,0:T(8,128)S(1)}, f32[512,128]{1,0:T(8,128)S(1)}, f32[512,512]{1,0:T(8,128)S(1)}) custom-call(bf16[512,512]{1,0:T(8,128)(2,1)S(1)} %get-tuple-element.41.refs_0_, bf16[512,512]{1,0:T(8,128)(2,1)S(1)} %collective-permute-done.6.refs_1_, bf16[512,512]{1,0:T(8,128)(2,1)S(1)} %collective-permute-done.x.refs_2_, ...), custom_call_target="tpu_custom_call" | custom-call | flops 2415919104 | bytes 7864320 | tf_op jit(solution)/shard_map/pallas_call | solution.py:89
  36.9 0.8 shard_map.86.refs_2_
  37.7 7.7 %collective-permute-start.10 = (bf16[2,4,128,128]{3,2,1,0:T(8,128)(2,1)S(1)}, bf16[2,4,128,128]{3,2,1,0:T(8,128)(2,1)S(1)}, u32[]{:S(2)}, u32[]{:S(2)}) collective-permute-start(bf16[2,4,128,128]{3,2,1,0:T(8,128)(2,1)S(1)} %shard_map.86.refs_2_), channel_id=1, source_target_pairs={{8,16},{16,8},{24,32},{32,24},{40,48},{48,40},{56,64},{64,56},{72,... | collective-permute-start | bytes 786440 | tf_op jit(solution)/shard_map/ppermute | solution.py:34
  45.5 0.1 collective-permute-start.9
  45.6 6.9 %collective-permute-done.10.refs_4_ = bf16[2,4,128,128]{3,2,1,0:T(8,128)(2,1)S(1)} collective-permute-done((bf16[2,4,128,128]{3,2,1,0:T(8,128)(2,1)S(1)}, bf16[2,4,128,128]{3,2,1,0:T(8,128)(2,1)S(1)}, u32[]{:S(2)}, u32[]{:S(2)}) %collective-permute-start.10) | collective-permute-done | bytes 262176 | tf_op jit(solution)/shard_map/ppermute | solution.py:34
  52.4 1.6 %collective-permute-done.9.refs_3_ = bf16[2,4,128,128]{3,2,1,0:T(8,128)(2,1)S(1)} collective-permute-done((bf16[2,4,128,128]{3,2,1,0:T(8,128)(2,1)S(1)}, bf16[2,4,128,128]{3,2,1,0:T(8,128)(2,1)S(1)}, u32[]{:S(2)}, u32[]{:S(2)}) %collective-permute-start.9) | collective-permute-done | bytes 262176 | tf_op jit(solution)/shard_map/ppermute | solution.py:34
  54.0 4.2 %collective-permute-start.12 = (bf16[2,4,128,128]{3,2,1,0:T(8,128)(2,1)S(1)}, bf16[2,4,128,128]{3,2,1,0:T(8,128)(2,1)S(1)}, u32[]{:S(2)}, u32[]{:S(2)}) collective-permute-start(bf16[2,4,128,128]{3,2,1,0:T(8,128)(2,1)S(1)} %collective-permute-done.9.refs_3_), channel_id=1, source_target_pairs={{8,16},{16,8},{24,32},{32,24},{40,48},{48,40},{56,64},{64,56},{72,... | collective-permute-start | bytes 786440 | tf_op jit(solution)/shard_map/ppermute | solution.py:34
  58.2 2.4 %collective-permute-done.11.refs_5_.refs_2_ = bf16[2,4,128,128]{3,2,1,0:T(8,128)(2,1)S(1)} collective-permute-done((bf16[2,4,128,128]{3,2,1,0:T(8,128)(2,1)S(1)}, bf16[2,4,128,128]{3,2,1,0:T(8,128)(2,1)S(1)}, u32[]{:S(2)}, u32[]{:S(2)}) %collective-permute-start.11) | collective-permute-done | bytes 262176 | tf_op jit(solution)/shard_map/ppermute | solution.py:34
  60.6 5.5 %collective-permute-start.14 = (bf16[2,4,128,128]{3,2,1,0:T(8,128)(2,1)S(1)}, bf16[2,4,128,128]{3,2,1,0:T(8,128)(2,1)S(1)}, u32[]{:S(2)}, u32[]{:S(2)}) collective-permute-start(bf16[2,4,128,128]{3,2,1,0:T(8,128)(2,1)S(1)} %collective-permute-done.11.refs_5_.refs_2_), channel_id=1, source_target_pairs={{8,16},{16,8},{24,32},{32,24},{40,48},{48,40},{56,64},{64,56},{72,... | collective-permute-start | bytes 786440 | tf_op jit(solution)/shard_map/ppermute | solution.py:34
  66.2 5.7 %collective-permute-done.14.refs_8_.refs_5_.refs_3_ = bf16[2,4,128,128]{3,2,1,0:T(8,128)(2,1)S(1)} collective-permute-done((bf16[2,4,128,128]{3,2,1,0:T(8,128)(2,1)S(1)}, bf16[2,4,128,128]{3,2,1,0:T(8,128)(2,1)S(1)}, u32[]{:S(2)}, u32[]{:S(2)}) %collective-permute-start.14) | collective-permute-done | bytes 262176 | tf_op jit(solution)/shard_map/ppermute | solution.py:34
  71.9 1.2 collective-permute-done.13.refs_7_.refs_4_.refs_2_
  73.1 4.2 %collective-permute-start.16 = (bf16[2,4,128,128]{3,2,1,0:T(8,128)(2,1)S(1)}, bf16[2,4,128,128]{3,2,1,0:T(8,128)(2,1)S(1)}, u32[]{:S(2)}, u32[]{:S(2)}) collective-permute-start(bf16[2,4,128,128]{3,2,1,0:T(8,128)(2,1)S(1)} %collective-permute-done.13.refs_7_.refs_4_.refs_2_), channel_id=1, source_target_pairs={{8,16},{16,8},{24,32},{32,24},{40,48},{48,40},{56,64},{64,56},{72,... | collective-permute-start | bytes 786440 | tf_op jit(solution)/shard_map/ppermute | solution.py:34
  77.3 2.4 %list_slots.1.refs_0_ = s32[20,18]{1,0:T(8,128)S(1)} custom-call(s32[4,16]{1,0:T(4,128)S(1)} %copy-done.5, s32[4]{0:T(128)S(1)} %copy-done.6, s32[128]{0:T(128)S(1)} %copy-done.7), custom_call_target="tpu_custom_call" | custom-call | tf_op jit(solution)/shard_map/list_slots/pallas_call | solution.py:269
  79.7 0.7 shard_map.85.refs_1_
  80.4 3.2 %shard_map.91 = (f32[512,128]{1,0:T(8,128)S(1)}, f32[512,128]{1,0:T(8,128)S(1)}, f32[512,128]{1,0:T(8,128)S(1)}) custom-call(s32[20,18]{1,0:T(8,128)S(1)} %list_slots.1.refs_0_, bf16[4,512,128]{2,1,0:T(8,128)(2,1)S(1)} %shard_map.85.refs_1_, bf16[2,4,128,128]{3,2,1,0:T(8,128)(2,1)S(1)} %shard_map.86.refs_2_, ...), custom_call_target="tpu_custom_call" | custom-call | flops 536870912 | bytes 4194304 | tf_op jit(solution)/shard_map/pallas_call | solution.py:340
  83.6 1.8 %shard_map.92 = (f32[512,128]{1,0:T(8,128)S(1)}, f32[512,128]{1,0:T(8,128)S(1)}, f32[512,128]{1,0:T(8,128)S(1)}) custom-call(s32[20,18]{1,0:T(8,128)S(1)} %list_slots.1.refs_0_, bf16[4,512,128]{2,1,0:T(8,128)(2,1)S(1)} %shard_map.85.refs_1_, bf16[2,4,128,128]{3,2,1,0:T(8,128)(2,1)S(1)} %collective-permute-done.13.refs_7_.refs_4_.refs_2_, ...), custom_call_target="tpu_custom_call" | custom-call | flops 536870912 | bytes 4194304 | tf_op jit(solution)/shard_map/pallas_call | solution.py:340
  85.4 2.1 %shard_map.93 = (bf16[64,4096]{1,0:T(8,128)(2,1)S(1)}, bf16[64,4096]{1,0:T(8,128)(2,1)S(1)}) custom-call(s32[20,18]{1,0:T(8,128)S(1)} %list_slots.1.refs_0_, bf16[4,512,128]{2,1,0:T(8,128)(2,1)S(1)} %shard_map.85.refs_1_, bf16[2,4,128,128]{3,2,1,0:T(8,128)(2,1)S(1)} %collective-permute-done.15.refs_9_.refs_2_, ...), custom_call_target="tpu_custom_call" | custom-call | flops 536870912 | bytes 4194304 | tf_op jit(solution)/shard_map/pallas_call | solution.py:340
  87.6 2.2 %shard_map.94 = (f32[512,128]{1,0:T(8,128)S(1)}, f32[512,128]{1,0:T(8,128)S(1)}, f32[512,128]{1,0:T(8,128)S(1)}) custom-call(s32[20,18]{1,0:T(8,128)S(1)} %list_slots.1.refs_0_, bf16[4,512,128]{2,1,0:T(8,128)(2,1)S(1)} %shard_map.85.refs_1_, bf16[2,4,128,128]{3,2,1,0:T(8,128)(2,1)S(1)} %shard_map.86.refs_2_, ...), custom_call_target="tpu_custom_call" | custom-call | flops 536870912 | bytes 4194304 | tf_op jit(solution)/shard_map/pallas_call | solution.py:340
  89.8 1.7 %shard_map.88 = (f32[512,128]{1,0:T(8,128)S(1)}, f32[512,128]{1,0:T(8,128)S(1)}, f32[512,128]{1,0:T(8,128)S(1)}) custom-call(s32[20,18]{1,0:T(8,128)S(1)} %list_slots.1.refs_0_, bf16[4,512,128]{2,1,0:T(8,128)(2,1)S(1)} %shard_map.85.refs_1_, bf16[2,4,128,128]{3,2,1,0:T(8,128)(2,1)S(1)} %shard_map.86.refs_2_, ...), custom_call_target="tpu_custom_call" | custom-call | flops 536870912 | bytes 4194304 | tf_op jit(solution)/shard_map/pallas_call | solution.py:340
  91.5 2.3 %shard_map.95 = (f32[512,128]{1,0:T(8,128)S(1)}, f32[512,128]{1,0:T(8,128)S(1)}, f32[512,128]{1,0:T(8,128)S(1)}) custom-call(s32[20,18]{1,0:T(8,128)S(1)} %list_slots.1.refs_0_, bf16[4,512,128]{2,1,0:T(8,128)(2,1)S(1)} %shard_map.85.refs_1_, bf16[2,4,128,128]{3,2,1,0:T(8,128)(2,1)S(1)} %collective-permute-done.11.refs_5_.refs_2_, ...), custom_call_target="tpu_custom_call" | custom-call | flops 536870912 | bytes 4194304 | tf_op jit(solution)/shard_map/pallas_call | solution.py:340
  93.8 1.3 %shard_map.89 = (f32[512,128]{1,0:T(8,128)S(1)}, f32[512,128]{1,0:T(8,128)S(1)}, f32[512,128]{1,0:T(8,128)S(1)}) custom-call(s32[20,18]{1,0:T(8,128)S(1)} %list_slots.1.refs_0_, bf16[4,512,128]{2,1,0:T(8,128)(2,1)S(1)} %shard_map.85.refs_1_, bf16[2,4,128,128]{3,2,1,0:T(8,128)(2,1)S(1)} %collective-permute-done.11.refs_5_.refs_2_, ...), custom_call_target="tpu_custom_call" | custom-call | flops 536870912 | bytes 4194304 | tf_op jit(solution)/shard_map/pallas_call | solution.py:340
  95.1 3.1 %shard_map.96 = (bf16[64,4096]{1,0:T(8,128)(2,1)S(1)}, bf16[64,4096]{1,0:T(8,128)(2,1)S(1)}) custom-call(s32[20,18]{1,0:T(8,128)S(1)} %list_slots.1.refs_0_, bf16[4,512,128]{2,1,0:T(8,128)(2,1)S(1)} %shard_map.85.refs_1_, bf16[2,4,128,128]{3,2,1,0:T(8,128)(2,1)S(1)} %collective-permute-done.15.refs_9_.refs_2_, ...), custom_call_target="tpu_custom_call" | custom-call | flops 536870912 | bytes 4194304 | tf_op jit(solution)/shard_map/pallas_call | solution.py:340
  98.1 0.6 collective-permute-start.22
  98.7 2.6 %shard_map.90 = (bf16[64,4096]{1,0:T(8,128)(2,1)S(1)}, bf16[64,4096]{1,0:T(8,128)(2,1)S(1)}) custom-call(s32[20,18]{1,0:T(8,128)S(1)} %list_slots.1.refs_0_, bf16[4,512,128]{2,1,0:T(8,128)(2,1)S(1)} %shard_map.85.refs_1_, bf16[2,4,128,128]{3,2,1,0:T(8,128)(2,1)S(1)} %collective-permute-done.15.refs_9_.refs_2_, ...), custom_call_target="tpu_custom_call" | custom-call | flops 536870912 | bytes 4194304 | tf_op jit(solution)/shard_map/pallas_call | solution.py:340
  101.3 0.3 collective-permute-start.18
  101.6 0.1 add_to_halves.1
  101.8 1.4 %collective-permute-start.23 = (bf16[32,4096]{1,0:T(8,128)(2,1)S(1)}, bf16[32,4096]{1,0:T(8,128)(2,1)S(1)}, u32[]{:S(2)}, u32[]{:S(2)}) collective-permute-start(bf16[32,4096]{1,0:T(8,128)(2,1)S(1)} %get-tuple-element.74), channel_id=1, source_target_pairs={{0,2},{1,3},{2,0},{3,1},{4,6},{5,7},{6,4},{7,5},{8,10},{9,11},{10,... | collective-permute-start | bytes 786440 | tf_op jit(solution)/shard_map/ppermute | solution.py:27
  103.1 5.0 %shard_map.87 = (bf16[64,4096]{1,0:T(8,128)(2,1)S(1)}, bf16[64,4096]{1,0:T(8,128)(2,1)S(1)}) custom-call(s32[20,18]{1,0:T(8,128)S(1)} %list_slots.1.refs_0_, bf16[4,512,128]{2,1,0:T(8,128)(2,1)S(1)} %shard_map.85.refs_1_, bf16[2,4,128,128]{3,2,1,0:T(8,128)(2,1)S(1)} %shard_map.86.refs_2_, bf16[2,4,128,128]{3,2,1,0:T(8,128)(2,1)S(1)} %collective-permute-done.9.refs_3_, ...), custom_call_target="tpu_custom_call" | custom-call | flops 536870912 | bytes 4194304 | tf_op jit(solution)/shard_map/pallas_call | solution.py:340
  108.1 0.3 collective-permute-start.17
  108.4 2.2 %collective-permute-done.23.half = bf16[32,4096]{1,0:T(8,128)(2,1)S(1)} collective-permute-done((bf16[32,4096]{1,0:T(8,128)(2,1)S(1)}, bf16[32,4096]{1,0:T(8,128)(2,1)S(1)}, u32[]{:S(2)}, u32[]{:S(2)}) %collective-permute-start.23) | collective-permute-done | bytes 262176 | tf_op jit(solution)/shard_map/ppermute | solution.py:27
  110.6 0.2 add_half.3
  110.7 2.0 %collective-permute-start.24 = (bf16[64,4096]{1,0:T(8,128)(2,1)S(1)}, bf16[64,4096]{1,0:T(8,128)(2,1)S(1)}, u32[]{:S(2)}, u32[]{:S(2)}) collective-permute-start(bf16[64,4096]{1,0:T(8,128)(2,1)S(1)} %add_half.3), channel_id=1, source_target_pairs={{0,6},{1,7},{2,4},{3,5},{4,2},{5,3},{6,0},{7,1},{8,14},{9,15},{10,... | collective-permute-start | bytes 1572872 | tf_op jit(solution)/shard_map/ppermute | solution.py:27
  112.7 0.2 add_half.2
  113.0 12.4 %collective-permute-done.24.refs_3_ = bf16[64,4096]{1,0:T(8,128)(2,1)S(1)} collective-permute-done((bf16[64,4096]{1,0:T(8,128)(2,1)S(1)}, bf16[64,4096]{1,0:T(8,128)(2,1)S(1)}, u32[]{:S(2)}, u32[]{:S(2)}) %collective-permute-start.24) | collective-permute-done | bytes 524320 | tf_op jit(solution)/shard_map/ppermute | solution.py:27
  125.5 1.5 %collective-permute-done.21.refs_2_ = bf16[64,4096]{1,0:T(8,128)(2,1)S(1)} collective-permute-done((bf16[64,4096]{1,0:T(8,128)(2,1)S(1)}, bf16[64,4096]{1,0:T(8,128)(2,1)S(1)}, u32[]{:S(2)}, u32[]{:S(2)}) %collective-permute-start.21) | collective-permute-done | bytes 524320 | tf_op jit(solution)/shard_map/ppermute | solution.py:27
  127.0 1.1 add.1
  (39 shorter events, 0.5 us)
Async XLA Ops:
  0.0 13.9 %collective-permute-start = (bf16[512,512]{1,0:T(8,128)(2,1)}, bf16[512,512]{1,0:T(8,128)(2,1)S(1)}, u32[]{:S(2)}, u32[]{:S(2)}) collective-permute-start(bf16[512,512]{1,0:T(8,128)(2,1)} %refs_3_.1), channel_id=1, source_target_pairs={{0,2},{1,3},{2,0},{3,1},{4,6},{5,7},{6,4},{7,5},{8,10},{9,11},{10,... | collective-permute-start | bytes 1572872 | tf_op jit(solution)/shard_map/ppermute | solution.py:27
  1.6 14.8 %collective-permute-start.2 = (bf16[512,512]{1,0:T(8,128)(2,1)}, bf16[512,512]{1,0:T(8,128)(2,1)S(1)}, u32[]{:S(2)}, u32[]{:S(2)}) collective-permute-start(bf16[512,512]{1,0:T(8,128)(2,1)} %refs_3_.1), channel_id=1, source_target_pairs={{0,6},{1,7},{2,4},{3,5},{4,2},{5,3},{6,0},{7,1},{8,14},{9,15},{10,... | collective-permute-start | bytes 1572872 | tf_op jit(solution)/shard_map/ppermute | solution.py:27
  3.8 29.7 %collective-permute-start.6 = (bf16[512,512]{1,0:T(8,128)(2,1)}, bf16[512,512]{1,0:T(8,128)(2,1)S(1)}, u32[]{:S(2)}, u32[]{:S(2)}) collective-permute-start(bf16[512,512]{1,0:T(8,128)(2,1)} %refs_3_.1), channel_id=1, source_target_pairs={{0,1},{1,0},{2,3},{3,2},{4,5},{5,4},{6,7},{7,6},{8,9},{9,8},{10,11... | collective-permute-start | bytes 1572872 | tf_op jit(solution)/shard_map/ppermute | solution.py:23
  13.9 19.5 %collective-permute-start.7 = (bf16[512,512]{1,0:T(8,128)(2,1)S(1)}, bf16[512,512]{1,0:T(8,128)(2,1)S(1)}, u32[]{:S(2)}, u32[]{:S(2)}) collective-permute-start(bf16[512,512]{1,0:T(8,128)(2,1)S(1)} %collective-permute-done.x.refs_2_), channel_id=1, source_target_pairs={{0,1},{1,0},{2,3},{3,2},{4,5},{5,4},{6,7},{7,6},{8,9},{9,8},{10,11... | collective-permute-start | bytes 1572872 | tf_op jit(solution)/shard_map/ppermute | solution.py:23
  16.4 17.1 %collective-permute-start.8 = (bf16[512,512]{1,0:T(8,128)(2,1)S(1)}, bf16[512,512]{1,0:T(8,128)(2,1)S(1)}, u32[]{:S(2)}, u32[]{:S(2)}) collective-permute-start(bf16[512,512]{1,0:T(8,128)(2,1)S(1)} %collective-permute-done.2.x.refs_4_), channel_id=1, source_target_pairs={{0,1},{1,0},{2,3},{3,2},{4,5},{5,4},{6,7},{7,6},{8,9},{9,8},{10,11... | collective-permute-start | bytes 1572872 | tf_op jit(solution)/shard_map/ppermute | solution.py:23
  16.4 10.0 %collective-permute-start.1 = (bf16[256,512]{1,0:T(8,128)(2,1)S(1)}, bf16[256,512]{1,0:T(8,128)(2,1)S(1)}, u32[]{:S(2)}, u32[]{:S(2)}) collective-permute-start(bf16[256,512]{1,0:T(8,128)(2,1)S(1)} %shard_map.82), channel_id=1, source_target_pairs={{0,6},{1,7},{2,4},{3,5},{4,2},{5,3},{6,0},{7,1},{8,14},{9,15},{10,... | collective-permute-start | bytes 786440 | tf_op jit(solution)/shard_map/ppermute | solution.py:27
  18.7 8.5 %collective-permute-start.3 = (bf16[256,512]{1,0:T(8,128)(2,1)S(1)}, bf16[256,512]{1,0:T(8,128)(2,1)S(1)}, u32[]{:S(2)}, u32[]{:S(2)}) collective-permute-start(bf16[256,512]{1,0:T(8,128)(2,1)S(1)} %shard_map.83), channel_id=1, source_target_pairs={{0,2},{1,3},{2,0},{3,1},{4,6},{5,7},{6,4},{7,5},{8,10},{9,11},{10,... | collective-permute-start | bytes 786440 | tf_op jit(solution)/shard_map/ppermute | solution.py:27
  26.4 10.5 %collective-permute-start.4 = (bf16[256,512]{1,0:T(8,128)(2,1)S(1)}, bf16[256,512]{1,0:T(8,128)(2,1)S(1)}, u32[]{:S(2)}, u32[]{:S(2)}) collective-permute-start(bf16[256,512]{1,0:T(8,128)(2,1)S(1)} %collective-permute-done.1.refs_0_), channel_id=1, source_target_pairs={{0,1},{1,0},{2,3},{3,2},{4,5},{5,4},{6,7},{7,6},{8,9},{9,8},{10,11... | collective-permute-start | bytes 786440 | tf_op jit(solution)/shard_map/ppermute | solution.py:23
  27.2 9.7 %collective-permute-start.5 = (bf16[256,512]{1,0:T(8,128)(2,1)S(1)}, bf16[256,512]{1,0:T(8,128)(2,1)S(1)}, u32[]{:S(2)}, u32[]{:S(2)}) collective-permute-start(bf16[256,512]{1,0:T(8,128)(2,1)S(1)} %collective-permute-done.3.refs_1_), channel_id=1, source_target_pairs={{0,1},{1,0},{2,3},{3,2},{4,5},{5,4},{6,7},{7,6},{8,9},{9,8},{10,11... | collective-permute-start | bytes 786440 | tf_op jit(solution)/shard_map/ppermute | solution.py:23
  27.2 2.2 %copy-start.1 = (bf16[4096,512]{1,0:T(8,128)(2,1)S(1)}, bf16[4096,512]{1,0:T(8,128)(2,1)}, u32[]{:S(2)}) copy-start(bf16[4096,512]{1,0:T(8,128)(2,1)} %refs_2_.1) | copy-start | bytes 12582916
  29.4 1.2 copy-start.2
  30.6 1.2 copy-start.3
  31.9 1.0 copy-start.4
  33.4 43.8 %copy-start.5 = (s32[4,16]{1,0:T(4,128)S(1)}, s32[4,16]{1,0:T(4,128)}, u32[]{:S(2)}) copy-start(s32[4,16]{1,0:T(4,128)} %links.1) | copy-start | bytes 772
  33.5 43.8 %copy-start.6 = (s32[4]{0:T(128)S(1)}, s32[4]{0:T(128)}, u32[]{:S(2)}) copy-start(s32[4]{0:T(128)} %counts.1) | copy-start | bytes 52
  33.5 43.8 %copy-start.7 = (s32[128]{0:T(128)S(1)}, s32[128]{0:T(128)}, u32[]{:S(2)}) copy-start(s32[128]{0:T(128)} %docs.1) | copy-start | bytes 1540
  37.7 14.7 %collective-permute-start.10 = (bf16[2,4,128,128]{3,2,1,0:T(8,128)(2,1)S(1)}, bf16[2,4,128,128]{3,2,1,0:T(8,128)(2,1)S(1)}, u32[]{:S(2)}, u32[]{:S(2)}) collective-permute-start(bf16[2,4,128,128]{3,2,1,0:T(8,128)(2,1)S(1)} %shard_map.86.refs_2_), channel_id=1, source_target_pairs={{8,16},{16,8},{24,32},{32,24},{40,48},{48,40},{56,64},{64,56},{72,... | collective-permute-start | bytes 786440 | tf_op jit(solution)/shard_map/ppermute | solution.py:34
  45.5 8.5 %collective-permute-start.9 = (bf16[2,4,128,128]{3,2,1,0:T(8,128)(2,1)S(1)}, bf16[2,4,128,128]{3,2,1,0:T(8,128)(2,1)S(1)}, u32[]{:S(2)}, u32[]{:S(2)}) collective-permute-start(bf16[2,4,128,128]{3,2,1,0:T(8,128)(2,1)S(1)} %shard_map.86.refs_2_), channel_id=1, source_target_pairs={{0,8},{8,0},{16,24},{24,16},{32,40},{40,32},{48,56},{56,48},{64,72... | collective-permute-start | bytes 786440 | tf_op jit(solution)/shard_map/ppermute | solution.py:34
  52.4 8.1 %collective-permute-start.11 = (bf16[2,4,128,128]{3,2,1,0:T(8,128)(2,1)S(1)}, bf16[2,4,128,128]{3,2,1,0:T(8,128)(2,1)S(1)}, u32[]{:S(2)}, u32[]{:S(2)}) collective-permute-start(bf16[2,4,128,128]{3,2,1,0:T(8,128)(2,1)S(1)} %collective-permute-done.10.refs_4_), channel_id=1, source_target_pairs={{0,8},{8,0},{16,24},{24,16},{32,40},{40,32},{48,56},{56,48},{64,72... | collective-permute-start | bytes 786440 | tf_op jit(solution)/shard_map/ppermute | solution.py:34
  54.0 12.0 %collective-permute-start.12 = (bf16[2,4,128,128]{3,2,1,0:T(8,128)(2,1)S(1)}, bf16[2,4,128,128]{3,2,1,0:T(8,128)(2,1)S(1)}, u32[]{:S(2)}, u32[]{:S(2)}) collective-permute-start(bf16[2,4,128,128]{3,2,1,0:T(8,128)(2,1)S(1)} %collective-permute-done.9.refs_3_), channel_id=1, source_target_pairs={{8,16},{16,8},{24,32},{32,24},{40,48},{48,40},{56,64},{64,56},{72,... | collective-permute-start | bytes 786440 | tf_op jit(solution)/shard_map/ppermute | solution.py:34
  60.6 11.3 %collective-permute-start.14 = (bf16[2,4,128,128]{3,2,1,0:T(8,128)(2,1)S(1)}, bf16[2,4,128,128]{3,2,1,0:T(8,128)(2,1)S(1)}, u32[]{:S(2)}, u32[]{:S(2)}) collective-permute-start(bf16[2,4,128,128]{3,2,1,0:T(8,128)(2,1)S(1)} %collective-permute-done.11.refs_5_.refs_2_), channel_id=1, source_target_pairs={{8,16},{16,8},{24,32},{32,24},{40,48},{48,40},{56,64},{64,56},{72,... | collective-permute-start | bytes 786440 | tf_op jit(solution)/shard_map/ppermute | solution.py:34
  66.1 7.0 %collective-permute-start.13 = (bf16[2,4,128,128]{3,2,1,0:T(8,128)(2,1)S(1)}, bf16[2,4,128,128]{3,2,1,0:T(8,128)(2,1)S(1)}, u32[]{:S(2)}, u32[]{:S(2)}) collective-permute-start(bf16[2,4,128,128]{3,2,1,0:T(8,128)(2,1)S(1)} %collective-permute-done.12.refs_6_.refs_3_), channel_id=1, source_target_pairs={{0,8},{8,0},{16,24},{24,16},{32,40},{40,32},{48,56},{56,48},{64,72... | collective-permute-start | bytes 786440 | tf_op jit(solution)/shard_map/ppermute | solution.py:34
  71.9 13.6 %collective-permute-start.15 = (bf16[2,4,128,128]{3,2,1,0:T(8,128)(2,1)S(1)}, bf16[2,4,128,128]{3,2,1,0:T(8,128)(2,1)S(1)}, u32[]{:S(2)}, u32[]{:S(2)}) collective-permute-start(bf16[2,4,128,128]{3,2,1,0:T(8,128)(2,1)S(1)} %collective-permute-done.14.refs_8_.refs_5_.refs_3_), channel_id=1, source_target_pairs={{0,8},{8,0},{16,24},{24,16},{32,40},{40,32},{48,56},{56,48},{64,72... | collective-permute-start | bytes 786440 | tf_op jit(solution)/shard_map/ppermute | solution.py:34
  73.1 12.4 %collective-permute-start.16 = (bf16[2,4,128,128]{3,2,1,0:T(8,128)(2,1)S(1)}, bf16[2,4,128,128]{3,2,1,0:T(8,128)(2,1)S(1)}, u32[]{:S(2)}, u32[]{:S(2)}) collective-permute-start(bf16[2,4,128,128]{3,2,1,0:T(8,128)(2,1)S(1)} %collective-permute-done.13.refs_7_.refs_4_.refs_2_), channel_id=1, source_target_pairs={{8,16},{16,8},{24,32},{32,24},{40,48},{48,40},{56,64},{64,56},{72,... | collective-permute-start | bytes 786440 | tf_op jit(solution)/shard_map/ppermute | solution.py:34
  79.7 5.7 %copy-start = (bf16[512,4096]{1,0:T(8,128)(2,1)S(1)}, bf16[512,4096]{1,0:T(8,128)(2,1)}, u32[]{:S(2)}) copy-start(bf16[512,4096]{1,0:T(8,128)(2,1)} %refs_7_.5) | copy-start | bytes 12582916
  87.5 14.1 %collective-permute-start.19 = (bf16[64,4096]{1,0:T(8,128)(2,1)S(1)}, bf16[64,4096]{1,0:T(8,128)(2,1)S(1)}, u32[]{:S(2)}, u32[]{:S(2)}) collective-permute-start(bf16[64,4096]{1,0:T(8,128)(2,1)S(1)} %get-tuple-element.64), channel_id=1, source_target_pairs={{0,1},{1,0},{2,3},{3,2},{4,5},{5,4},{6,7},{7,6},{8,9},{9,8},{10,11... | collective-permute-start | bytes 1572872 | tf_op jit(solution)/shard_map/ppermute | solution.py:23
  98.1 10.2 %collective-permute-start.22 = (bf16[64,4096]{1,0:T(8,128)(2,1)S(1)}, bf16[64,4096]{1,0:T(8,128)(2,1)S(1)}, u32[]{:S(2)}, u32[]{:S(2)}) collective-permute-start(bf16[64,4096]{1,0:T(8,128)(2,1)S(1)} %get-tuple-element.73), channel_id=1, source_target_pairs={{0,1},{1,0},{2,3},{3,2},{4,5},{5,4},{6,7},{7,6},{8,9},{9,8},{10,11... | collective-permute-start | bytes 1572872 | tf_op jit(solution)/shard_map/ppermute | solution.py:23
  101.3 11.4 %collective-permute-start.18 = (bf16[64,4096]{1,0:T(8,128)(2,1)S(1)}, bf16[64,4096]{1,0:T(8,128)(2,1)S(1)}, u32[]{:S(2)}, u32[]{:S(2)}) collective-permute-start(bf16[64,4096]{1,0:T(8,128)(2,1)S(1)} %get-tuple-element.56), channel_id=1, source_target_pairs={{0,1},{1,0},{2,3},{3,2},{4,5},{5,4},{6,7},{7,6},{8,9},{9,8},{10,11... | collective-permute-start | bytes 1572872 | tf_op jit(solution)/shard_map/ppermute | solution.py:23
  101.8 8.8 %collective-permute-start.23 = (bf16[32,4096]{1,0:T(8,128)(2,1)S(1)}, bf16[32,4096]{1,0:T(8,128)(2,1)S(1)}, u32[]{:S(2)}, u32[]{:S(2)}) collective-permute-start(bf16[32,4096]{1,0:T(8,128)(2,1)S(1)} %get-tuple-element.74), channel_id=1, source_target_pairs={{0,2},{1,3},{2,0},{3,1},{4,6},{5,7},{6,4},{7,5},{8,10},{9,11},{10,... | collective-permute-start | bytes 786440 | tf_op jit(solution)/shard_map/ppermute | solution.py:27
  103.1 9.6 %collective-permute-start.20 = (bf16[32,4096]{1,0:T(8,128)(2,1)S(1)}, bf16[32,4096]{1,0:T(8,128)(2,1)S(1)}, u32[]{:S(2)}, u32[]{:S(2)}) collective-permute-start(bf16[32,4096]{1,0:T(8,128)(2,1)S(1)} %get-tuple-element.65), channel_id=1, source_target_pairs={{0,6},{1,7},{2,4},{3,5},{4,2},{5,3},{6,0},{7,1},{8,14},{9,15},{10,... | collective-permute-start | bytes 786440 | tf_op jit(solution)/shard_map/ppermute | solution.py:27
  108.1 4.9 %collective-permute-start.17 = (bf16[64,4096]{1,0:T(8,128)(2,1)S(1)}, bf16[64,4096]{1,0:T(8,128)(2,1)S(1)}, u32[]{:S(2)}, u32[]{:S(2)}) collective-permute-start(bf16[64,4096]{1,0:T(8,128)(2,1)S(1)} %get-tuple-element.48), channel_id=1, source_target_pairs={{0,1},{1,0},{2,3},{3,2},{4,5},{5,4},{6,7},{7,6},{8,9},{9,8},{10,11... | collective-permute-start | bytes 1572872 | tf_op jit(solution)/shard_map/ppermute | solution.py:23
  110.7 14.8 %collective-permute-start.24 = (bf16[64,4096]{1,0:T(8,128)(2,1)S(1)}, bf16[64,4096]{1,0:T(8,128)(2,1)S(1)}, u32[]{:S(2)}, u32[]{:S(2)}) collective-permute-start(bf16[64,4096]{1,0:T(8,128)(2,1)S(1)} %add_half.3), channel_id=1, source_target_pairs={{0,6},{1,7},{2,4},{3,5},{4,2},{5,3},{6,0},{7,1},{8,14},{9,15},{10,... | collective-permute-start | bytes 1572872 | tf_op jit(solution)/shard_map/ppermute | solution.py:27
  112.9 14.1 %collective-permute-start.21 = (bf16[64,4096]{1,0:T(8,128)(2,1)S(1)}, bf16[64,4096]{1,0:T(8,128)(2,1)S(1)}, u32[]{:S(2)}, u32[]{:S(2)}) collective-permute-start(bf16[64,4096]{1,0:T(8,128)(2,1)S(1)} %add_half.2), channel_id=1, source_target_pairs={{0,2},{1,3},{2,0},{3,1},{4,6},{5,7},{6,4},{7,5},{8,10},{9,11},{10,... | collective-permute-start | bytes 1572872 | tf_op jit(solution)/shard_map/ppermute | solution.py:27
